TPU v7x, 32 devices: a whole 2x2x4 slice. The times are simulated.
32 devices in a mesh: section: 2 (over y), dp: 16 (over z, x, core).
Axes of the slice: x: 2, y: 2, z: 4, core: 2. Of those that a mesh axis runs over, the one named last changes fastest.
Arguments:
- inputs: bfloat16 [16384, 768], P('dp'), may hold values from -6 to 6
- cotangent: bfloat16 [16384, 768], P('dp'), may hold values from -6 to 6
- segments: int32 [16384], P('dp'), may hold values from 0 to 511, as said below
- valid_flags: int32 [16384], P('dp'), may hold values from 0 to 1, as said below
- first_gain: bfloat16 [2, 768], P('section'), may hold values from 0.5 to 1.5
- first_shift: bfloat16 [2, 768], P('section'), may hold values from -1.75 to 1.75
- project_weight: bfloat16 [2, 768, 2304], P('section'), may hold values from -0.21875 to 0.21875
- query_bias: bfloat16 [2, 768], P('section'), may hold values from -1.75 to 1.75
- value_bias: bfloat16 [2, 768], P('section'), may hold values from -1.75 to 1.75
- out_weight: bfloat16 [2, 768, 768], P('section'), may hold values from -0.875 to 0.875
- out_bias: bfloat16 [2, 768], P('section'), may hold values from -1.75 to 1.75
- second_gain: bfloat16 [2, 768], P('section'), may hold values from 0.5 to 1.5
- second_shift: bfloat16 [2, 768], P('section'), may hold values from -1.75 to 1.75
- up_weight: bfloat16 [2, 768, 3072], P('section'), may hold values from -0.21875 to 0.21875
- up_bias: bfloat16 [2, 3072], P('section'), may hold values from -1.75 to 1.75
- down_weight: bfloat16 [2, 3072, 768], P('section'), may hold values from -0.109375 to 0.109375
- down_bias: bfloat16 [2, 768], P('section'), may hold values from -1.75 to 1.75
Outputs:
- layer_out: bfloat16 [2, 16384, 768], P('section', 'dp')
- input_grad: float32 [2, 16384, 768], P('section', 'dp')
- first_gain_grad: float32 [2, 768], P('section', 'dp')
- first_shift_grad: float32 [2, 768], P('section', 'dp')
- project_weight_grad: float32 [2, 768, 2304], P('section', None, 'dp')
- query_bias_grad: float32 [2, 768], P('section', 'dp')
- value_bias_grad: float32 [2, 768], P('section', 'dp')
- out_weight_grad: float32 [2, 768, 768], P('section', None, 'dp')
- out_bias_grad: float32 [2, 768], P('section', 'dp')
- second_gain_grad: float32 [2, 768], P('section', 'dp')
- second_shift_grad: float32 [2, 768], P('section', 'dp')
- up_weight_grad: float32 [2, 768, 3072], P('section', None, 'dp')
- up_bias_grad: float32 [2, 3072], P('section', 'dp')
- down_weight_grad: float32 [2, 3072, 768], P('section', None, 'dp')
- down_bias_grad: float32 [2, 768], P('section', 'dp')
Inputs may be any that keep to these rules, and one draw needn't show every extreme that they name: `segments`: within each pack of 512 consecutive rows, segment numbers start at 0 and never fall, each number covering one run of rows; rows with flag 0 come after all rows with flag 1 in their pack and carry the segment number 512 - 1, which no row with flag 1 carries. `valid_flags`: each pack of 512 rows begins with a row of flag 1 and ends with a row of flag 0.
All inputs are finite; a program needn't handle non-finite values.
Results may differ from a plain program's by a relative error of at most 0.015.
Values may be sent and summed in bfloat16 or wider, within the bound.
A program may use at most 256 MiB of HBM per device.

v0:
```python
from functools import partial

import jax
import jax.numpy as jnp
from jax import lax
from jax.sharding import PartitionSpec as P

HEADS = 12
HEAD_DIM = 64
SEQ = 512
MICRO = 2


EPSILON = 1e-06
SCORE_SCALE = 0.125


def from_behind(value, axis, by):
    devices = lax.axis_size(axis)
    pairs = [(i, i + by) for i in range(devices) if 0 <= i + by < devices]
    return lax.ppermute(value, axis, pairs)


def norm_rows(values):
    average = jnp.mean(values, axis=-1, keepdims=True)
    centred = values - average
    inv_scale = lax.rsqrt(jnp.mean(centred * centred, axis=-1, keepdims=True) + EPSILON)
    return (centred * inv_scale, inv_scale)


def norm_back(normed_grad, whitened, inv_scale, gain_vec):
    scaled = normed_grad * gain_vec.astype(jnp.float32)
    return inv_scale * (
        scaled
        - jnp.mean(scaled, axis=-1, keepdims=True)
        - whitened * jnp.mean(scaled * whitened, axis=-1, keepdims=True)
    )


def contract_rows(left, right):
    return lax.dot_general(
        left, right, (((0,), (0,)), ((), ())), preferred_element_type=jnp.float32
    )


def times_transpose(left, right):
    return lax.dot_general(
        left, right, (((1,), (1,)), ((), ())), preferred_element_type=jnp.float32
    )


def pair_mask(segment, validity, block_rows):
    length = segment.shape[0]
    row_place = lax.broadcasted_iota(jnp.int32, (block_rows, length), 0)
    col_place = lax.broadcasted_iota(jnp.int32, (block_rows, length), 1)
    return (segment[:, None] == segment[None, :]) & (validity[None, :] == 1) | (
        row_place == col_place
    )


def attend_pack(query_rows, key_rows, value_rows, segment, validity):
    length = query_rows.shape[0]
    block_rows = min(512, length)
    key_heads = key_rows.reshape(length, HEADS, HEAD_DIM)
    value_heads = value_rows.reshape(length, HEADS, HEAD_DIM)
    query_block = query_rows.reshape(block_rows, HEADS, HEAD_DIM)
    scores = (
        jnp.einsum("qhd,khd->hqk", query_block, key_heads, preferred_element_type=jnp.float32)
        * SCORE_SCALE
    )
    scores = jnp.where(pair_mask(segment, validity, block_rows)[None], scores, -1e30)
    row_max = jnp.max(scores, axis=-1, keepdims=True)
    exponent = jnp.exp(scores - row_max)
    row_sum = jnp.sum(exponent, axis=-1, keepdims=True)
    attention_low = (exponent / row_sum).astype(jnp.bfloat16)
    combined = jnp.einsum(
        "hqk,khd->qhd", attention_low, value_heads, preferred_element_type=jnp.float32
    )
    out_parts = [combined.reshape(block_rows, HEADS * HEAD_DIM).astype(jnp.bfloat16)]
    log_parts = [(row_max + jnp.log(row_sum))[:, :, 0]]
    return (jnp.concatenate(out_parts, axis=0), jnp.concatenate(log_parts, axis=1))


def attend_back(query_rows, key_rows, value_rows, log_sums, attended_low, segment, validity):
    length = query_rows.shape[0]
    block_rows = min(512, length)
    key_heads = key_rows.reshape(length, HEADS, HEAD_DIM)
    value_heads = value_rows.reshape(length, HEADS, HEAD_DIM)
    query_block = query_rows.reshape(block_rows, HEADS, HEAD_DIM)
    upstream = attended_low.reshape(block_rows, HEADS, HEAD_DIM)
    scores = (
        jnp.einsum("qhd,khd->hqk", query_block, key_heads, preferred_element_type=jnp.float32)
        * SCORE_SCALE
    )
    scores = jnp.where(pair_mask(segment, validity, block_rows)[None], scores, -1e30)
    attention = jnp.exp(scores - log_sums[:, 0:block_rows, None])
    attention_low = attention.astype(jnp.bfloat16)
    value_grad = jnp.einsum(
        "hqk,qhd->khd", attention_low, upstream, preferred_element_type=jnp.float32
    )
    attention_grad = jnp.einsum(
        "qhd,khd->hqk", upstream, value_heads, preferred_element_type=jnp.float32
    )
    inner = jnp.sum(attention * attention_grad, axis=-1, keepdims=True)
    score_low = (attention * (attention_grad - inner)).astype(jnp.bfloat16)
    query_grad = (
        jnp.einsum("hqk,khd->qhd", score_low, key_heads, preferred_element_type=jnp.float32)
        * SCORE_SCALE
    )
    query_parts = [query_grad.reshape(block_rows, HEADS * HEAD_DIM).astype(jnp.bfloat16)]
    key_grad = (
        jnp.einsum("hqk,qhd->khd", score_low, query_block, preferred_element_type=jnp.float32)
        * SCORE_SCALE
    )
    return (
        jnp.concatenate(query_parts, axis=0),
        key_grad.reshape(length, HEADS * HEAD_DIM).astype(jnp.bfloat16),
        value_grad.reshape(length, HEADS * HEAD_DIM).astype(jnp.bfloat16),
    )


def stash_zeros(micro_count, micro_rows, width, hidden_width):
    plain = jnp.zeros((micro_count, micro_rows, width), jnp.bfloat16)
    log_zero = jnp.zeros((micro_count, micro_rows // SEQ, HEADS, SEQ), jnp.float32)
    middle_zero = jnp.zeros((micro_count, micro_rows, width), jnp.float32)
    zeros_all = (plain, plain, plain, plain, plain, log_zero, plain, middle_zero, plain)
    zeros_all = zeros_all + (jnp.zeros((micro_count, micro_rows, hidden_width), jnp.float32),)
    return zeros_all


def layer_forward(weights, layer_in, segment, validity):
    (
        first_gain,
        first_shift,
        project_weight,
        query_bias,
        value_bias,
        out_weight,
        out_bias,
        second_gain,
        second_shift,
        up_weight,
        up_bias,
        down_weight,
        down_bias,
    ) = weights
    width = layer_in.shape[1]
    widened = layer_in.astype(jnp.float32)
    whitened, inv_scale = norm_rows(widened)
    normed = (whitened * first_gain + first_shift).astype(jnp.bfloat16)
    combined = jnp.dot(normed, project_weight, preferred_element_type=jnp.float32)
    query_rows = (combined[:, :width] + query_bias).astype(jnp.bfloat16)
    key_rows = combined[:, width : 2 * width].astype(jnp.bfloat16)
    value_rows = (combined[:, 2 * width :] + value_bias).astype(jnp.bfloat16)
    attended_piece, log_piece = attend_pack(query_rows, key_rows, value_rows, segment, validity)
    attended_parts = [attended_piece]
    log_parts = [log_piece]
    attended = jnp.concatenate(attended_parts, axis=0)
    log_sums = jnp.stack(log_parts)
    middle = widened + (
        jnp.dot(attended, out_weight, preferred_element_type=jnp.float32) + out_bias
    )
    second_white, second_scale = norm_rows(middle)
    second_normed = (second_white * second_gain + second_shift).astype(jnp.bfloat16)
    upper = jnp.dot(second_normed, up_weight, preferred_element_type=jnp.float32) + up_bias
    hidden = jax.nn.gelu(upper, approximate=False).astype(jnp.bfloat16)
    layer_result = middle + (
        jnp.dot(hidden, down_weight, preferred_element_type=jnp.float32) + down_bias
    )
    stash = (
        layer_in,
        normed,
        query_rows,
        key_rows,
        value_rows,
        log_sums,
        attended,
        middle,
        second_normed,
    )
    stash = stash + (upper,)
    return (layer_result, stash)


def layer_backward(weights, stash, gradient, segment, validity):
    (
        first_gain,
        first_shift,
        project_weight,
        query_bias,
        value_bias,
        out_weight,
        out_bias,
        second_gain,
        second_shift,
        up_weight,
        up_bias,
        down_weight,
        down_bias,
    ) = weights
    (
        layer_in,
        normed,
        query_rows,
        key_rows,
        value_rows,
        log_sums,
        attended,
        middle,
        second_normed,
    ) = stash[:9]
    upper = stash[9]
    hidden = jax.nn.gelu(upper, approximate=False).astype(jnp.bfloat16)
    output_low = gradient.astype(jnp.bfloat16)
    hidden_low = times_transpose(output_low, down_weight).astype(jnp.bfloat16)
    unused, gelu_back = jax.vjp(partial(jax.nn.gelu, approximate=False), upper)
    upper_low = gelu_back(hidden_low.astype(jnp.float32))[0].astype(jnp.bfloat16)
    second_grad = times_transpose(upper_low, up_weight)
    second_white, second_scale = norm_rows(middle)
    middle_grad = gradient + norm_back(second_grad, second_white, second_scale, second_gain)
    branch_low = middle_grad.astype(jnp.bfloat16)
    attended_low = times_transpose(branch_low, out_weight).astype(jnp.bfloat16)
    query_grad, key_grad, value_grad = attend_back(
        query_rows, key_rows, value_rows, log_sums[0], attended_low, segment, validity
    )
    query_parts = [query_grad]
    key_parts = [key_grad]
    value_parts = [value_grad]
    mixed_low = jnp.concatenate(
        [
            jnp.concatenate(query_parts, axis=0),
            jnp.concatenate(key_parts, axis=0),
            jnp.concatenate(value_parts, axis=0),
        ],
        axis=1,
    )
    first_grad = times_transpose(mixed_low, project_weight)
    whitened, inv_scale = norm_rows(layer_in.astype(jnp.float32))
    input_grad = middle_grad + norm_back(first_grad, whitened, inv_scale, first_gain)
    norm_terms = (
        jnp.sum(first_grad * whitened, axis=0),
        jnp.sum(first_grad, axis=0),
        jnp.sum(second_grad * second_white, axis=0),
        jnp.sum(second_grad, axis=0),
    )
    parts = (output_low, branch_low, upper_low, mixed_low, hidden, normed, attended, second_normed)
    return (input_grad, parts, norm_terms)


def weight_terms(parts):
    output_low, branch_low, upper_low, mixed_low, hidden, normed, attended, second_normed = parts
    width = output_low.shape[1]
    return (
        contract_rows(normed, mixed_low),
        jnp.sum(mixed_low[:, :width], axis=0, dtype=jnp.float32),
        jnp.sum(mixed_low[:, 2 * width :], axis=0, dtype=jnp.float32),
        contract_rows(attended, branch_low),
        jnp.sum(branch_low, axis=0, dtype=jnp.float32),
        contract_rows(second_normed, upper_low),
        jnp.sum(upper_low, axis=0, dtype=jnp.float32),
        contract_rows(hidden, output_low),
        jnp.sum(output_low, axis=0, dtype=jnp.float32),
    )


def on_device(
    inputs,
    cotangent,
    segments,
    valid_flags,
    first_gain,
    first_shift,
    project_weight,
    query_bias,
    value_bias,
    out_weight,
    out_bias,
    second_gain,
    second_shift,
    up_weight,
    up_bias,
    down_weight,
    down_bias,
):
    section_index = lax.axis_index("section")
    section_count = lax.axis_size("section")
    weights = tuple(
        (
            member[0]
            for member in (
                first_gain,
                first_shift,
                project_weight,
                query_bias,
                value_bias,
                out_weight,
                out_bias,
                second_gain,
                second_shift,
                up_weight,
                up_bias,
                down_weight,
                down_bias,
            )
        )
    )
    width = inputs.shape[1]
    hidden_width = up_weight.shape[2]
    micro_rows = inputs.shape[0] // MICRO
    buffers = stash_zeros(MICRO, micro_rows, width, hidden_width)
    layer_outs = jnp.zeros((MICRO, micro_rows, width), jnp.bfloat16)
    arrived = jnp.zeros((micro_rows, width), jnp.bfloat16)
    tick_total = MICRO + section_count - 1
    for tick_index in range(tick_total):
        micro_index = tick_index - section_index
        active = (micro_index >= 0) & (micro_index < MICRO)
        mb_slot = jnp.clip(micro_index, 0, MICRO - 1)
        row_start = mb_slot * micro_rows

        def run_tick(carried):
            buffers_in, outs_in, arrived_in = carried
            fresh = lax.dynamic_slice_in_dim(inputs, row_start, micro_rows, 0)
            layer_in = jnp.where(section_index == 0, fresh, arrived_in)
            segment = lax.dynamic_slice_in_dim(segments, row_start, micro_rows, 0)
            validity = lax.dynamic_slice_in_dim(valid_flags, row_start, micro_rows, 0)
            layer_result, stash = layer_forward(weights, layer_in, segment, validity)
            stash = stash[: len(buffers_in)]
            buffers_out = tuple(
                (
                    lax.dynamic_update_index_in_dim(buffer, member, mb_slot, 0)
                    for buffer, member in zip(buffers_in, stash)
                )
            )
            outs_out = lax.dynamic_update_index_in_dim(
                outs_in, layer_result.astype(jnp.bfloat16), mb_slot, 0
            )
            return (buffers_out, outs_out)

        def skip_tick(carried):
            return (carried[0], carried[1])

        buffers, layer_outs = lax.cond(active, run_tick, skip_tick, (buffers, layer_outs, arrived))
        if tick_index + 1 < tick_total:
            outgoing = lax.dynamic_index_in_dim(layer_outs, mb_slot, 0, keepdims=False)
            arrived = from_behind(outgoing, "section", 1)
    input_grads = jnp.zeros((MICRO, micro_rows, width), jnp.float32)
    weight_parts = (
        jnp.zeros((width, 3 * width), jnp.float32),
        jnp.zeros((width,), jnp.float32),
        jnp.zeros((width,), jnp.float32),
        jnp.zeros((width, width), jnp.float32),
        jnp.zeros((width,), jnp.float32),
        jnp.zeros((width, hidden_width), jnp.float32),
        jnp.zeros((hidden_width,), jnp.float32),
        jnp.zeros((hidden_width, width), jnp.float32),
        jnp.zeros((width,), jnp.float32),
    )
    norm_sums = tuple((jnp.zeros((width,), jnp.float32) for unused in range(4)))
    coming = jnp.zeros((micro_rows, width), jnp.bfloat16)
    for tick_index in range(tick_total):
        back_order = tick_index - (section_count - 1 - section_index)
        active = (back_order >= 0) & (back_order < MICRO)
        mb_slot = jnp.clip(MICRO - 1 - back_order, 0, MICRO - 1)
        row_start = mb_slot * micro_rows

        def back_tick(carried):
            grads_in, parts_in, sums_in, coming_in = carried
            last_rows = lax.dynamic_slice_in_dim(cotangent, row_start, micro_rows, 0)
            gradient = jnp.where(section_index == section_count - 1, last_rows, coming_in).astype(
                jnp.float32
            )
            segment = lax.dynamic_slice_in_dim(segments, row_start, micro_rows, 0)
            validity = lax.dynamic_slice_in_dim(valid_flags, row_start, micro_rows, 0)
            stash = tuple(
                (lax.dynamic_index_in_dim(buffer, mb_slot, 0, keepdims=False) for buffer in buffers)
            )
            input_grad, parts, norm_terms = layer_backward(
                weights, stash, gradient, segment, validity
            )
            grads_out = lax.dynamic_update_index_in_dim(grads_in, input_grad, mb_slot, 0)
            parts_out = tuple(
                (running + addend for running, addend in zip(parts_in, weight_terms(parts)))
            )
            sums_out = tuple((running + addend for running, addend in zip(sums_in, norm_terms)))
            return (grads_out, parts_out, sums_out)

        def rest_tick(carried):
            return (carried[0], carried[1], carried[2])

        input_grads, weight_parts, norm_sums = lax.cond(
            active, back_tick, rest_tick, (input_grads, weight_parts, norm_sums, coming)
        )
        if tick_index + 1 < tick_total:
            outgoing = lax.dynamic_index_in_dim(input_grads, mb_slot, 0, keepdims=False).astype(
                jnp.bfloat16
            )
            coming = from_behind(outgoing, "section", -1)
    all_rows = MICRO * micro_rows
    (
        project_term,
        query_bias_term,
        value_bias_term,
        out_weight_term,
        out_bias_term,
        up_weight_term,
        up_bias_term,
        down_weight_term,
        down_bias_term,
    ) = tuple((member[None] for member in weight_parts))
    first_gain_term = norm_sums[0][None]
    first_shift_term = norm_sums[1][None]
    second_gain_term = norm_sums[2][None]
    second_shift_term = norm_sums[3][None]
    summed = (
        lax.psum_scatter(first_gain_term, "dp", scatter_dimension=1, tiled=True),
        lax.psum_scatter(first_shift_term, "dp", scatter_dimension=1, tiled=True),
        lax.psum_scatter(project_term, "dp", scatter_dimension=2, tiled=True),
        lax.psum_scatter(query_bias_term, "dp", scatter_dimension=1, tiled=True),
        lax.psum_scatter(value_bias_term, "dp", scatter_dimension=1, tiled=True),
        lax.psum_scatter(out_weight_term, "dp", scatter_dimension=2, tiled=True),
        lax.psum_scatter(out_bias_term, "dp", scatter_dimension=1, tiled=True),
        lax.psum_scatter(second_gain_term, "dp", scatter_dimension=1, tiled=True),
        lax.psum_scatter(second_shift_term, "dp", scatter_dimension=1, tiled=True),
        lax.psum_scatter(up_weight_term, "dp", scatter_dimension=2, tiled=True),
        lax.psum_scatter(up_bias_term, "dp", scatter_dimension=1, tiled=True),
        lax.psum_scatter(down_weight_term, "dp", scatter_dimension=2, tiled=True),
        lax.psum_scatter(down_bias_term, "dp", scatter_dimension=1, tiled=True),
    )
    return (
        layer_outs.reshape(1, all_rows, width),
        input_grads.reshape(1, all_rows, width),
        summed[0],
        summed[1],
        summed[2],
        summed[3],
        summed[4],
        summed[5],
        summed[6],
        summed[7],
        summed[8],
        summed[9],
        summed[10],
        summed[11],
        summed[12],
    )


def solution(mesh):
    in_specs = (
        P("dp", None),
        P("dp", None),
        P("dp"),
        P("dp"),
        P("section", None),
        P("section", None),
        P("section", None, None),
        P("section", None),
        P("section", None),
        P("section", None, None),
        P("section", None),
        P("section", None),
        P("section", None),
        P("section", None, None),
        P("section", None),
        P("section", None, None),
        P("section", None),
    )
    out_specs = (
        P("section", "dp", None),
        P("section", "dp", None),
        P("section", "dp"),
        P("section", "dp"),
        P("section", None, "dp"),
        P("section", "dp"),
        P("section", "dp"),
        P("section", None, "dp"),
        P("section", "dp"),
        P("section", "dp"),
        P("section", "dp"),
        P("section", None, "dp"),
        P("section", "dp"),
        P("section", None, "dp"),
        P("section", "dp"),
    )
    return jax.shard_map(
        on_device, mesh=mesh, in_specs=in_specs, out_specs=out_specs, check_vma=False
    )
```

profile of v0, /device:TPU:0, one launch (start us, length us, event | category | flops | bytes accessed | tf_op | source)
XLA Modules:
  0.0 1628.0 jit_solution(6835325227012525188)
XLA Ops:
  13.6 80.5 %conditional.6 = (bf16[2,512,768]{2,1,0:T(8,128)(2,1)}, bf16[2,512,768]{2,1,0:T(8,128)(2,1)}, bf16[2,512,768]{2,1,0:T(8,128)(2,1)}, bf16[2,512,768]{2,1,0:T(8,12...) conditional(s32[]{:T(128)} %convert_element_type.512, () %tuple.55, ...), branch_computations={%region_0.1_spmd, %region_1.8_spmd} | conditional | flops 8216515584 | bytes 217369152 | solution.py:342
  77.0 16.9 %fusion.29 = bf16[2,512,768]{2,1,0:T(8,128)(2,1)} fusion(bf16[2,512,768]{2,1,0:T(8,128)(2,1)} %broadcast.977.clone.7, s32[]{:T(128)S(6)} %select_n.150, f32[512,768]{1,0:T(8,128)S(1)} %copy-done.7, bf16[3072,768]{1,0:T(8,128)(2,1)S(1)} %bitcast.698, f32[512,3072]{1,0:T(8,128)S(1)} %get-tuple-element.1333, f32[3072]{0:T(1024)S(1)} %convert_element_type.376, ...), kind=kOutput, calls=%fused_computation.47 | convolution fusion | flops 2520907776 | bytes 13384708 | tf_op jit(solution)/shard_map/cond/branch_1_fun/dot_general | solution.py:168
  98.3 17.1 %collective-permute-done = bf16[512,768]{1,0:T(8,128)(2,1)} collective-permute-done((bf16[512,768]{1,0:T(8,128)(2,1)}, bf16[512,768]{1,0:T(8,128)(2,1)}, u32[]{:S(2)}, u32[]{:S(2)}) %collective-permute-start) | collective-permute-done | bytes 786464 | tf_op jit(solution)/shard_map/ppermute | solution.py:21
  115.5 67.8 %conditional.7 = ((bf16[2,512,768]{2,1,0:T(8,128)(2,1)}, bf16[2,512,768]{2,1,0:T(8,128)(2,1)}, bf16[2,512,768]{2,1,0:T(8,128)(2,1)}, bf16[2,512,768]{2,1,0:T(8,1...) conditional(s32[]{:T(128)} %convert_element_type.511, ...), branch_computations={%region_8.9_spmd, %region_9.16_spmd} | conditional | flops 8214549504 | bytes 150139328 | solution.py:342
  166.5 16.7 %fusion.97 = bf16[2,512,768]{2,1,0:T(8,128)(2,1)} fusion(bf16[2,512,768]{2,1,0:T(8,128)(2,1)} %get-tuple-element.540, s32[]{:T(128)S(6)} %select_n.155, f32[512,768]{1,0:T(8,128)S(1)} %copy-done.5, bf16[3072,768]{1,0:T(8,128)(2,1)S(1)} %bitcast.700, f32[512,3072]{1,0:T(8,128)S(1)} %get-tuple-element.1345, f32[3072]{0:T(1024)S(1)} %copy-done.64, ...), kind=kOutput, calls=%fused_computation.145 | convolution fusion | flops 2520907776 | bytes 13384708 | tf_op jit(solution)/shard_map/cond/branch_1_fun/dot_general | solution.py:168
  191.0 16.2 collective-permute-done.1
  213.5 24.5 %conditional.9 = (f32[2,512,768]{2,1,0:T(8,128)}, f32[768,2304]{1,0:T(8,128)}, f32[768]{0:T(1024)}, f32[768]{0:T(1024)S(1)}, f32[768,768]{1,0:T(8,128)}, /*index...) conditional(s32[]{:T(128)} %convert_element_type.515, () %tuple.60, ...), branch_computations={%region_24.25_spmd, %region_25.44_spmd} | conditional | flops 16727656448 | bytes 404855680 | solution.py:390
  241.7 177.3 %collective-permute-done.2 = bf16[512,768]{1,0:T(8,128)(2,1)} collective-permute-done((bf16[512,768]{1,0:T(8,128)(2,1)}, bf16[512,768]{1,0:T(8,128)(2,1)}, u32[]{:S(2)}, u32[]{:S(2)}) %collective-permute-start.2) | collective-permute-done | bytes 786464 | tf_op jit(solution)/shard_map/ppermute | solution.py:21
  419.0 135.7 %conditional.10 = ((f32[2,512,768]{2,1,0:T(8,128)}, f32[768,2304]{1,0:T(8,128)}, f32[768]{0:T(1024)}, f32[768]{0:T(1024)S(1)}, f32[768,768]{1,0:T(8,128)}, /*ind...) conditional(s32[]{:T(128)} %convert_element_type.514, ...), branch_computations={%region_44.45_spmd, %region_45.64_spmd} | conditional | flops 16734354432 | bytes 424664000 | solution.py:390
  444.2 14.1 fusion.284
  458.4 12.1 convolution_add_fusion.1
  511.4 13.6 multiply_reduce_fusion.9
  558.4 18.7 %collective-permute-done.3 = bf16[512,768]{1,0:T(8,128)(2,1)} collective-permute-done((bf16[512,768]{1,0:T(8,128)(2,1)}, bf16[512,768]{1,0:T(8,128)(2,1)}, u32[]{:S(2)}, u32[]{:S(2)}) %collective-permute-start.3) | collective-permute-done | bytes 786464 | tf_op jit(solution)/shard_map/ppermute | solution.py:21
  577.2 125.5 %conditional.11 = (f32[768,2304]{1,0:T(8,128)}, f32[768]{0:T(1024)}, f32[768]{0:T(1024)S(1)}, f32[768,768]{1,0:T(8,128)}, f32[768]{0:T(1024)S(1)}, /*index=5*/f3...) conditional(s32[]{:T(128)} %convert_element_type.513, ...), branch_computations={%region_64.65_spmd, %region_65.84_spmd} | conditional | flops 16734353408 | bytes 418356032 | solution.py:390
  602.4 14.1 fusion.349
  616.6 12.1 convolution_add_fusion.5
  662.8 11.0 multiply_reduce_fusion.15
  724.5 9.6 copy.162
  734.2 9.6 copy.163
  743.9 14.8 reduce-scatter.40.cloned.1.call-done
  760.0 57.2 %reduce-scatter.42.cloned.1.call-done = f32[48,1]{1,0:T(8,128)} async-done(((f32[768,1]{1,0:T(8,128)}), f32[48,1]{1,0:T(8,128)}) %reduce-scatter.42.cloned.1.call-update) | async-done | bytes 208
  818.5 56.9 %reduce-scatter.44.cloned.1.call-done = f32[48,1]{1,0:T(8,128)} async-done(((f32[768,1]{1,0:T(8,128)}), f32[48,1]{1,0:T(8,128)}) %reduce-scatter.44.cloned.1.call-update) | async-done | bytes 208
  876.7 57.1 %reduce-scatter.46.cloned.1.call-done = f32[48,1]{1,0:T(8,128)} async-done(((f32[768,1]{1,0:T(8,128)}), f32[48,1]{1,0:T(8,128)}) %reduce-scatter.46.cloned.1.call-update) | async-done | bytes 208
  935.1 56.7 %reduce-scatter.48.cloned.1.call-done = f32[48,1]{1,0:T(8,128)} async-done(((f32[768,1]{1,0:T(8,128)}), f32[48,1]{1,0:T(8,128)}) %reduce-scatter.48.cloned.1.call-update) | async-done | bytes 208
  993.1 57.1 %reduce-scatter.50.cloned.1.call-done = f32[48,1]{1,0:T(8,128)} async-done(((f32[768,1]{1,0:T(8,128)}), f32[48,1]{1,0:T(8,128)}) %reduce-scatter.50.cloned.1.call-update) | async-done | bytes 208
  1051.5 56.8 %reduce-scatter.52.cloned.1.call-done = f32[48,1]{1,0:T(8,128)} async-done(((f32[768,1]{1,0:T(8,128)}), f32[48,1]{1,0:T(8,128)}) %reduce-scatter.52.cloned.1.call-update) | async-done | bytes 208
  1109.6 57.2 %reduce-scatter.56.cloned.1.call-done = f32[48,1]{1,0:T(8,128)} async-done(((f32[768,1]{1,0:T(8,128)}), f32[48,1]{1,0:T(8,128)}) %reduce-scatter.56.cloned.1.call-update) | async-done | bytes 208
  1168.2 60.9 %reduce-scatter.54.cloned.1.call-done = f32[192,1]{1,0:T(8,128)} async-done(((f32[3072,1]{1,0:T(8,128)}), f32[192,1]{1,0:T(8,128)}) %reduce-scatter.54.cloned.1.call-update) | async-done | bytes 784
  1230.6 65.1 %reduce-scatter.34.cloned.1.call-done = f32[1,768,48]{1,2,0:T(8,128)} async-done(((f32[1,768,768]{1,2,0:T(8,128)}), f32[1,768,48]{1,2,0:T(8,128)}) %reduce-scatter.34.cloned.1.call-update) | async-done | bytes 147472 | tf_op jit(solution)/shard_map/reduce_scatter | solution.py:420
  1295.7 93.7 %reduce-scatter.32.cloned.1.call-done = f32[1,768,144]{1,2,0:T(8,128)} async-done(((f32[1,768,2304]{1,2,0:T(8,128)}), f32[1,768,144]{1,2,0:T(8,128)}) %reduce-scatter.32.cloned.1.call-update) | async-done | bytes 442384 | tf_op jit(solution)/shard_map/reduce_scatter | solution.py:417
  1389.3 116.0 %reduce-scatter.36.cloned.1.call-done = f32[1,768,192]{1,2,0:T(8,128)} async-done(((f32[1,768,3072]{1,2,0:T(8,128)}), f32[1,768,192]{1,2,0:T(8,128)}) %reduce-scatter.36.cloned.1.call-update) | async-done | bytes 589840 | tf_op jit(solution)/shard_map/reduce_scatter | solution.py:424
  1505.3 115.8 %reduce-scatter.38.cloned.1.call-done = f32[1,3072,48]{1,2,0:T(8,128)} async-done(((f32[1,3072,768]{1,2,0:T(8,128)}), f32[1,3072,48]{1,2,0:T(8,128)}) %reduce-scatter.38.cloned.1.call-update) | async-done | bytes 589840 | tf_op jit(solution)/shard_map/reduce_scatter | solution.py:426
  (390 shorter events, 378.9 us)
Async XLA Ops:
  7.2 751.5 %reduce-scatter.40.cloned.1.call-start = ((), (), s32[]{:S(2)}) async-start(), calls=%async_computation.17 | async-start | bytes 417792
  14.0 11.8 copy-start.71
  51.4 17.1 %copy-start.3 = (f32[2,512,768]{2,1,0:T(8,128)}, f32[2,512,768]{2,1,0:T(8,128)S(1)}, u32[]{:S(2)}) copy-start(f32[2,512,768]{2,1,0:T(8,128)S(1)} %get-tuple-element.1422) | copy-start | bytes 9437188 | tf_op jit(solution)/shard_map/cond
  62.3 14.6 slice-start.9
  77.0 16.9 %copy-start.4 = (f32[2,512,768]{2,1,0:T(8,128)S(1)}, f32[2,512,768]{2,1,0:T(8,128)}, u32[]{:S(2)}) copy-start(f32[2,512,768]{2,1,0:T(8,128)} %copy-done.3) | copy-start | bytes 9437188 | tf_op jit(solution)/shard_map/cond
  77.0 16.9 %copy-start.50 = (f32[2,1,12,512]{3,2,1,0:T(8,128)S(1)}, f32[2,1,12,512]{3,2,1,0:T(8,128)}, u32[]{:S(2)}) copy-start(f32[2,1,12,512]{3,2,1,0:T(8,128)} %copy-done.49) | copy-start | bytes 147460 | tf_op jit(solution)/shard_map/cond
  96.2 19.3 %collective-permute-start = (bf16[512,768]{1,0:T(8,128)(2,1)}, bf16[512,768]{1,0:T(8,128)(2,1)}, u32[]{:S(2)}, u32[]{:S(2)}) collective-permute-start(bf16[512,768]{1,0:T(8,128)(2,1)} %dynamic-slice_bitcast_fusion.4), channel_id=1, source_target_pairs={{0,16},{1,17},{2,18},{3,19},{4,20},{5,21},{6,22},{7,23},{8,24},{9,... | collective-permute-start | bytes 2359304 | tf_op jit(solution)/shard_map/ppermute | solution.py:21
  154.9 11.6 slice-start.11
  185.3 21.9 %collective-permute-start.1 = (bf16[512,768]{1,0:T(8,128)(2,1)}, bf16[512,768]{1,0:T(8,128)(2,1)}, u32[]{:S(2)}, u32[]{:S(2)}) collective-permute-start(bf16[512,768]{1,0:T(8,128)(2,1)} %dynamic-slice_bitcast_fusion.3), channel_id=1, source_target_pairs={{0,16},{1,17},{2,18},{3,19},{4,20},{5,21},{6,22},{7,23},{8,24},{9,... | collective-permute-start | bytes 2359304 | tf_op jit(solution)/shard_map/ppermute | solution.py:21
  240.4 178.6 %collective-permute-start.2 = (bf16[512,768]{1,0:T(8,128)(2,1)}, bf16[512,768]{1,0:T(8,128)(2,1)}, u32[]{:S(2)}, u32[]{:S(2)}) collective-permute-start(bf16[512,768]{1,0:T(8,128)(2,1)} %fusion.406), channel_id=1, source_target_pairs={{16,0},{17,1},{18,2},{19,3},{20,4},{21,5},{22,6},{23,7},{24,8},{25... | collective-permute-start | bytes 2359304 | tf_op jit(solution)/shard_map/ppermute | solution.py:21
  444.2 14.2 copy-start.32
  511.4 13.6 slice-start
  511.4 13.6 slice-start.1
  511.4 13.6 slice-start.2
  557.1 20.0 %collective-permute-start.3 = (bf16[512,768]{1,0:T(8,128)(2,1)}, bf16[512,768]{1,0:T(8,128)(2,1)}, u32[]{:S(2)}, u32[]{:S(2)}) collective-permute-start(bf16[512,768]{1,0:T(8,128)(2,1)} %fusion.407), channel_id=1, source_target_pairs={{16,0},{17,1},{18,2},{19,3},{20,4},{21,5},{22,6},{23,7},{24,8},{25... | collective-permute-start | bytes 2359304 | tf_op jit(solution)/shard_map/ppermute | solution.py:21
  583.8 14.0 copy-start.53
  602.4 14.2 copy-start.33
  662.8 11.0 slice-start.3
  662.8 11.0 slice-start.4
  662.8 12.6 slice-start.5
  703.7 113.6 %reduce-scatter.42.cloned.1.call-start = ((), (), s32[]{:S(2)}) async-start(), calls=%async_computation.18 | async-start | bytes 417792
  704.6 170.7 %reduce-scatter.44.cloned.1.call-start = ((), (), s32[]{:S(2)}) async-start(), calls=%async_computation.19 | async-start | bytes 417792
  706.3 227.5 %reduce-scatter.46.cloned.1.call-start = ((), (), s32[]{:S(2)}) async-start(), calls=%async_computation.20 | async-start | bytes 417792
  707.3 284.5 %reduce-scatter.48.cloned.1.call-start = ((), (), s32[]{:S(2)}) async-start(), calls=%async_computation.21 | async-start | bytes 417792
  708.3 341.8 %reduce-scatter.50.cloned.1.call-start = ((), (), s32[]{:S(2)}) async-start(), calls=%async_computation.22 | async-start | bytes 417792
  709.3 399.0 %reduce-scatter.52.cloned.1.call-start = ((), (), s32[]{:S(2)}) async-start(), calls=%async_computation.23 | async-start | bytes 417792
  710.3 456.5 %reduce-scatter.56.cloned.1.call-start = ((), (), s32[]{:S(2)}) async-start(), calls=%async_computation.25 | async-start | bytes 417792
  711.3 517.7 %reduce-scatter.54.cloned.1.call-start = ((), (), s32[]{:S(2)}) async-start(), calls=%async_computation.24 | async-start | bytes 1671168
  713.1 582.6 %reduce-scatter.34.cloned.1.call-start = ((), (), s32[]{:S(2)}) async-start(), calls=%async_computation.14 | async-start | bytes 2506752 | tf_op jit(solution)/shard_map/reduce_scatter | solution.py:420
  716.3 673.1 %reduce-scatter.32.cloned.1.call-start = ((), (), s32[]{:S(2)}) async-start(), calls=%async_computation.13 | async-start | bytes 7520256 | tf_op jit(solution)/shard_map/reduce_scatter | solution.py:417
  724.4 780.9 %reduce-scatter.36.cloned.1.call-start = ((), (), s32[]{:S(2)}) async-start(), calls=%async_computation.15 | async-start | bytes 10027008 | tf_op jit(solution)/shard_map/reduce_scatter | solution.py:424
  734.1 887.0 %reduce-scatter.38.cloned.1.call-start = ((), (), s32[]{:S(2)}) async-start(), calls=%async_computation.16 | async-start | bytes 10027008 | tf_op jit(solution)/shard_map/reduce_scatter | solution.py:426
  (47 other events, 299.4 us)
Sparse Core Ops, SparseCore 0:
  703.8 54.8 reduce-scatter.39
  762.5 54.6 reduce-scatter.41
  820.7 54.6 reduce-scatter.43
  879.1 54.6 reduce-scatter.45
  937.1 54.6 reduce-scatter.47
  995.6 54.5 reduce-scatter.49
  1053.7 54.5 reduce-scatter.51
  1112.2 54.5 reduce-scatter.55
  1170.5 58.4 reduce-scatter.53
  1233.7 61.9 reduce-scatter.33
  1300.3 89.0 reduce-scatter.31
  1394.4 110.8 reduce-scatter.35
  1510.0 111.1 reduce-scatter.37
where the time goes:
time: 1630 us
  waiting for transfers between devices  1090 us (67%)
  matrix products  226 us (14%)
  local copies, waits for them, and re-layouts  151 us (9%)
  other arithmetic  114 us (7%)
  loops' own time  16.5 us (1%)
    unnamed x22, waiting for transfers between devices  475 us
    ppermute x4, waiting for transfers between devices, from_behind(): return lax.ppermute(value, axis, pairs)  229 us
    reduce_scatter x1, waiting for transfers between devices, on_device(): lax.psum_scatter(up_weight_term, 'dp', scatter_dimension=2, tiled=True)  116 us
    reduce_scatter x1, waiting for transfers between devices, on_device(): lax.psum_scatter(down_weight_term, 'dp', scatter_dimension=2, tiled=True)  116 us
    reduce_scatter x1, waiting for transfers between devices, on_device(): lax.psum_scatter(project_term, 'dp', scatter_dimension=2, tiled=True)  93.7 us
    dot_general x8, matrix products, contract_rows(): lax.dot_general(left, right, (((0,), (0,)), ((), ())), preferred_element_...  66.1 us
    reduce_scatter x1, waiting for transfers between devices, on_device(): lax.psum_scatter(out_weight_term, 'dp', scatter_dimension=2, tiled=True)  65.1 us
    dot_general x8, matrix products, times_transpose(): lax.dot_general(left, right, (((1,), (1,)), ((), ())), preferred_element_...  36.7 us
  transfers between devices with their start and end apart: 17, of which 17 were waited for; matrix products, arithmetic and copies ran while one was open for 3% of the time, Pallas kernels for 0%

commit v1 on v0

--- a/solution.py
+++ b/solution.py
@@ -251,14 +251,14 @@
     output_low, branch_low, upper_low, mixed_low, hidden, normed, attended, second_normed = parts
     width = output_low.shape[1]
     return (
-        contract_rows(normed, mixed_low),
+        contract_rows(mixed_low, normed),
         jnp.sum(mixed_low[:, :width], axis=0, dtype=jnp.float32),
         jnp.sum(mixed_low[:, 2 * width :], axis=0, dtype=jnp.float32),
-        contract_rows(attended, branch_low),
+        contract_rows(branch_low, attended),
         jnp.sum(branch_low, axis=0, dtype=jnp.float32),
-        contract_rows(second_normed, upper_low),
+        contract_rows(upper_low, second_normed),
         jnp.sum(upper_low, axis=0, dtype=jnp.float32),
-        contract_rows(hidden, output_low),
+        contract_rows(output_low, hidden),
         jnp.sum(output_low, axis=0, dtype=jnp.float32),
     )
 
@@ -345,14 +345,14 @@
             arrived = from_behind(outgoing, "section", 1)
     input_grads = jnp.zeros((MICRO, micro_rows, width), jnp.float32)
     weight_parts = (
-        jnp.zeros((width, 3 * width), jnp.float32),
+        jnp.zeros((3 * width, width), jnp.float32),
         jnp.zeros((width,), jnp.float32),
         jnp.zeros((width,), jnp.float32),
         jnp.zeros((width, width), jnp.float32),
         jnp.zeros((width,), jnp.float32),
+        jnp.zeros((hidden_width, width), jnp.float32),
+        jnp.zeros((hidden_width,), jnp.float32),
         jnp.zeros((width, hidden_width), jnp.float32),
-        jnp.zeros((hidden_width,), jnp.float32),
-        jnp.zeros((hidden_width, width), jnp.float32),
         jnp.zeros((width,), jnp.float32),
     )
     norm_sums = tuple((jnp.zeros((width,), jnp.float32) for unused in range(4)))
@@ -406,42 +406,50 @@
         up_bias_term,
         down_weight_term,
         down_bias_term,
-    ) = tuple((member[None] for member in weight_parts))
-    first_gain_term = norm_sums[0][None]
-    first_shift_term = norm_sums[1][None]
-    second_gain_term = norm_sums[2][None]
-    second_shift_term = norm_sums[3][None]
-    summed = (
-        lax.psum_scatter(first_gain_term, "dp", scatter_dimension=1, tiled=True),
-        lax.psum_scatter(first_shift_term, "dp", scatter_dimension=1, tiled=True),
-        lax.psum_scatter(project_term, "dp", scatter_dimension=2, tiled=True),
-        lax.psum_scatter(query_bias_term, "dp", scatter_dimension=1, tiled=True),
-        lax.psum_scatter(value_bias_term, "dp", scatter_dimension=1, tiled=True),
-        lax.psum_scatter(out_weight_term, "dp", scatter_dimension=2, tiled=True),
-        lax.psum_scatter(out_bias_term, "dp", scatter_dimension=1, tiled=True),
-        lax.psum_scatter(second_gain_term, "dp", scatter_dimension=1, tiled=True),
-        lax.psum_scatter(second_shift_term, "dp", scatter_dimension=1, tiled=True),
-        lax.psum_scatter(up_weight_term, "dp", scatter_dimension=2, tiled=True),
-        lax.psum_scatter(up_bias_term, "dp", scatter_dimension=1, tiled=True),
-        lax.psum_scatter(down_weight_term, "dp", scatter_dimension=2, tiled=True),
-        lax.psum_scatter(down_bias_term, "dp", scatter_dimension=1, tiled=True),
-    )
+    ) = weight_parts
+    shards = lax.axis_size("dp")
+    vectors = (
+        norm_sums[0],
+        norm_sums[1],
+        query_bias_term,
+        value_bias_term,
+        out_bias_term,
+        norm_sums[2],
+        norm_sums[3],
+        up_bias_term,
+        down_bias_term,
+    )
+    sizes = [vector.shape[0] // shards for vector in vectors]
+    packed = jnp.concatenate([vector.reshape(shards, -1) for vector in vectors], axis=1)
+    packed = lax.psum_scatter(packed, "dp", scatter_dimension=0, tiled=True)[0]
+    small = []
+    start = 0
+    for size in sizes:
+        small.append(packed[start : start + size][None])
+        start += size
+
+    def reduce_rows(term):
+        piece = lax.psum_scatter(
+            term.astype(jnp.bfloat16), "dp", scatter_dimension=0, tiled=True
+        )
+        return piece.astype(jnp.float32).T[None]
+
     return (
         layer_outs.reshape(1, all_rows, width),
         input_grads.reshape(1, all_rows, width),
-        summed[0],
-        summed[1],
-        summed[2],
-        summed[3],
-        summed[4],
-        summed[5],
-        summed[6],
-        summed[7],
-        summed[8],
-        summed[9],
-        summed[10],
-        summed[11],
-        summed[12],
+        small[0],
+        small[1],
+        reduce_rows(project_term),
+        small[2],
+        small[3],
+        reduce_rows(out_weight_term),
+        small[4],
+        small[5],
+        small[6],
+        reduce_rows(up_weight_term),
+        small[7],
+        reduce_rows(down_weight_term),
+        small[8],
     )
 
 

time: 1630 us -> 995 us (0.61)
  waiting for transfers between devices: 1090 us -> 425 us
  blocking collectives: 0 us -> 57.9 us
  local copies, waits for them, and re-layouts: 151 us -> 104 us
  other arithmetic: 114 us -> 142 us
    unnamed x22 -> x4, waiting for transfers between devices: 475 us -> 0.07 us
    reduce_scatter x4, waiting for transfers between devices: 391 us -> 200 us  [reduce_rows(): lax.psum_scatter(term.astype(jnp.bfloat16), 'dp', scatter_dimension=0, ti...]
    unnamed x0 -> x1, blocking collectives: none -> 57.9 us
    cond x128 -> x134, local copies, waits for them, and re-layouts: 33.3 us -> 2.9 us  [the longest x4 30.5 us: on_device(): lax.cond(active, back_tick, rest_tick, (input_grads, weight_parts, norm_s...]
    unnamed x18 -> x3, local copies, waits for them, and re-layouts: 21.9 us -> 0.59 us
    convert_element_type x0 -> x4, other arithmetic: none -> 21.1 us  [reduce_rows(): term.astype(jnp.bfloat16)]
  transfers between devices with their start and end apart: 17 -> 8, of which waited for: 17 -> 7; matrix products, arithmetic and copies ran while one was open for 3% -> 3% of each run, Pallas kernels for 0% -> 0%
where the time goes in v1:
time: 995 us; the launch traced here: 990 us
  waiting for transfers between devices  425 us (43%)
  matrix products  219 us (22%)
  other arithmetic  142 us (14%)
  local copies, waits for them, and re-layouts  104 us (10%)
  blocking collectives  57.9 us (6%)
  loops' own time  16.7 us (2%)
  between operations  14.2 us (1%)
  starting transfers between devices  10.7 us (1%)
    ppermute x4, waiting for transfers between devices, from_behind(): return lax.ppermute(value, axis, pairs)  226 us
    reduce_scatter x4, waiting for transfers between devices, reduce_rows(): lax.psum_scatter(term.astype(jnp.bfloat16), 'dp', scatter_dimension=0, ti...  200 us
    dot_general x8, matrix products, contract_rows(): lax.dot_general(left, right, (((0,), (0,)), ((), ())), preferred_element_...  61.8 us
    unnamed x1, blocking collectives  57.9 us
    another operation x27, local copies, waits for them, and re-layouts  36.7 us
    dot_general x8, matrix products, times_transpose(): lax.dot_general(left, right, (((1,), (1,)), ((), ())), preferred_element_...  34.4 us
    dot_general x2, matrix products, layer_forward(): jnp.dot(hidden, down_weight, preferred_element_type=jnp.float32) + down_bias  34.1 us
    another operation x2, other arithmetic, layer_backward(): unused, gelu_back = jax.vjp(partial(jax.nn.gelu, approximate=False), upper)  28.4 us
  transfers between devices with their start and end apart: 8, of which 7 were waited for; matrix products, arithmetic and copies ran while one was open for 3% of the time, Pallas kernels for 0%

profile of v1, /device:TPU:0, one launch (start us, length us, event | category | flops | bytes accessed | tf_op | source)
XLA Modules:
  0.0 990.1 jit_solution(13542160511310261175)
XLA Ops:
  13.6 80.5 %conditional.6 = (bf16[2,512,768]{2,1,0:T(8,128)(2,1)}, bf16[2,512,768]{2,1,0:T(8,128)(2,1)}, bf16[2,512,768]{2,1,0:T(8,128)(2,1)}, bf16[2,512,768]{2,1,0:T(8,12...) conditional(s32[]{:T(128)} %convert_element_type.528, () %tuple.76, ...), branch_computations={%region_0.1_spmd, %region_1.8_spmd} | conditional | flops 8216515584 | bytes 217369152 | solution.py:342
  68.2 7.2 bitcast_dynamic-update-slice_fusion
  76.7 17.3 %fusion.29 = bf16[2,512,768]{2,1,0:T(8,128)(2,1)} fusion(bf16[2,512,768]{2,1,0:T(8,128)(2,1)} %broadcast.977.clone.7, s32[]{:T(128)S(6)} %select_n.150, f32[512,768]{1,0:T(8,128)S(1)} %copy-done.7, bf16[3072,768]{1,0:T(8,128)(2,1)S(1)} %bitcast.671, f32[512,3072]{1,0:T(8,128)S(1)} %get-tuple-element.1380, f32[3072]{0:T(1024)S(1)} %convert_element_type.388, ...), kind=kOutput, calls=%fused_computation.47 | convolution fusion | flops 2520907776 | bytes 13384708 | tf_op jit(solution)/shard_map/cond/branch_1_fun/dot_general | solution.py:168
  98.4 17.1 %collective-permute-done = bf16[512,768]{1,0:T(8,128)(2,1)} collective-permute-done((bf16[512,768]{1,0:T(8,128)(2,1)}, bf16[512,768]{1,0:T(8,128)(2,1)}, u32[]{:S(2)}, u32[]{:S(2)}) %collective-permute-start) | collective-permute-done | bytes 786464 | tf_op jit(solution)/shard_map/ppermute | solution.py:21
  115.5 67.6 %conditional.7 = ((bf16[2,512,768]{2,1,0:T(8,128)(2,1)}, bf16[2,512,768]{2,1,0:T(8,128)(2,1)}, bf16[2,512,768]{2,1,0:T(8,128)(2,1)}, bf16[2,512,768]{2,1,0:T(8,1...) conditional(s32[]{:T(128)} %convert_element_type.527, ...), branch_computations={%region_8.9_spmd, %region_9.16_spmd} | conditional | flops 8214549504 | bytes 150139328 | solution.py:342
  159.1 7.3 bitcast_dynamic-update-slice_fusion.9
  166.4 16.7 %fusion.97 = bf16[2,512,768]{2,1,0:T(8,128)(2,1)} fusion(bf16[2,512,768]{2,1,0:T(8,128)(2,1)} %get-tuple-element.563, s32[]{:T(128)S(6)} %select_n.155, f32[512,768]{1,0:T(8,128)S(1)} %copy-done.5, bf16[3072,768]{1,0:T(8,128)(2,1)S(1)} %bitcast.673, f32[512,3072]{1,0:T(8,128)S(1)} %get-tuple-element.1392, f32[3072]{0:T(1024)S(1)} %copy-done.64, ...), kind=kOutput, calls=%fused_computation.145 | convolution fusion | flops 2520907776 | bytes 13384708 | tf_op jit(solution)/shard_map/cond/branch_1_fun/dot_general | solution.py:168
  191.0 16.2 %collective-permute-done.1 = bf16[512,768]{1,0:T(8,128)(2,1)} collective-permute-done((bf16[512,768]{1,0:T(8,128)(2,1)}, bf16[512,768]{1,0:T(8,128)(2,1)}, u32[]{:S(2)}, u32[]{:S(2)}) %collective-permute-start.1) | collective-permute-done | bytes 786464 | tf_op jit(solution)/shard_map/ppermute | solution.py:21
  207.2 7.4 conditional.8
  214.6 23.7 %conditional.9 = (f32[2,512,768]{2,1,0:T(8,128)}, f32[2304,768]{1,0:T(8,128)}, f32[768]{0:T(1024)}, f32[768]{0:T(1024)S(1)}, f32[768,768]{1,0:T(8,128)}, /*index...) conditional(s32[]{:T(128)} %convert_element_type.531, () %tuple.81, ...), branch_computations={%region_24.25_spmd, %region_25.44_spmd} | conditional | flops 16727656448 | bytes 419011520 | solution.py:390
  242.0 173.8 %collective-permute-done.2 = bf16[512,768]{1,0:T(8,128)(2,1)} collective-permute-done((bf16[512,768]{1,0:T(8,128)(2,1)}, bf16[512,768]{1,0:T(8,128)(2,1)}, u32[]{:S(2)}, u32[]{:S(2)}) %collective-permute-start.2) | collective-permute-done | bytes 786464 | tf_op jit(solution)/shard_map/ppermute | solution.py:21
  415.7 132.4 %conditional.10 = ((f32[2,512,768]{2,1,0:T(8,128)}, f32[2304,768]{1,0:T(8,128)}, f32[768]{0:T(1024)}, f32[768]{0:T(1024)S(1)}, f32[768,768]{1,0:T(8,128)}, /*ind...) conditional(s32[]{:T(128)} %convert_element_type.530, ...), branch_computations={%region_44.45_spmd, %region_45.64_spmd} | conditional | flops 16734354432 | bytes 438819840 | solution.py:390
  441.0 14.2 %fusion.284 = f32[512,3072]{1,0:T(8,128)S(1)} fusion(f32[2,512,3072]{2,1,0:T(8,128)} %get-tuple-element.636, s32[]{:T(128)S(6)} %select_n.170), kind=kLoop, calls=%fused_computation.423 | loop fusion | flops 97517568 | bytes 12582916 | tf_op jit(solution)/shard_map/cond/branch_1_fun/jvp()/erfc | solution.py:216
  455.2 10.0 %convolution_add_fusion.1 = f32[768,3072]{1,0:T(8,128)} fusion(f32[768,3072]{1,0:T(8,128)} %get-tuple-element.660, bf16[512,768]{1,0:T(8,128)(2,1)S(1)} %copy-done.32, f32[512,3072]{1,0:T(8,128)S(1)} %fusion.284, f32[2,512,3072]{2,1,0:T(8,128)} %get-tuple-element.636, s32[]{:T(128)S(6)} %select_n.170), kind=kOutput, calls=%fused_computation.448 | convolution fusion | flops 2422996992 | bytes 32243716 | tf_op jit(solution)/shard_map/cond/branch_1_fun/dot_general | solution.py:41
  465.2 6.6 convert_reduce_fusion.9
  471.9 7.8 convolution_add_fusion.2
  505.0 13.6 %multiply_reduce_fusion.9 = (f32[12,512]{1,0:T(8,128)S(1)}, f32[12,512,512]{1,2,0:T(8,128)}) fusion(f32[12,512,512]{1,2,0:T(8,128)} %copy-done, f32[12,512]{1,0:T(8,128)S(1)} %dynamic-slice_bitcast_fusion.1, pred[512,512]{0,1:T(8,128)(4,1)S(1)} %fusion.322, bf16[512,12,64]{0,2,1:T(8,128)(2,1)} %bitcast.620, bf16[512,12,64]{0,2,1:T(8,128)(2,1)} %bitcast.632), kind=kOutput, calls=%fused_computation.410 | convolution fusion | flops 418375680 | bytes 27049984 | tf_op jit(solution)/shard_map/cond/branch_1_fun/qhd,khd->hqk/dot_general | solution.py:101
  518.6 7.2 multiply_convert_fusion.3
  532.3 9.0 convolution_add_fusion
  551.8 18.7 %collective-permute-done.3 = bf16[512,768]{1,0:T(8,128)(2,1)} collective-permute-done((bf16[512,768]{1,0:T(8,128)(2,1)}, bf16[512,768]{1,0:T(8,128)(2,1)}, u32[]{:S(2)}, u32[]{:S(2)}) %collective-permute-start.3) | collective-permute-done | bytes 786464 | tf_op jit(solution)/shard_map/ppermute | solution.py:21
  570.6 122.5 %conditional.11 = (f32[2304,768]{1,0:T(8,128)}, f32[768,768]{1,0:T(8,128)}, f32[3072,768]{1,0:T(8,128)}, f32[768,3072]{1,0:T(8,128)}, f32[1,1024,768]{2,1,0:T(8,...) conditional(s32[]{:T(128)} %convert_element_type.529, ...), branch_computations={%region_64.65_spmd, %region_65.84_spmd} | conditional | flops 16734354432 | bytes 435657600 | solution.py:390
  596.0 14.2 %fusion.349 = f32[512,3072]{1,0:T(8,128)S(1)} fusion(f32[2,512,3072]{2,1,0:T(8,128)} %get-tuple-element.677, s32[]{:T(128)S(6)} %min.15), kind=kLoop, calls=%fused_computation.535 | loop fusion | flops 97517568 | bytes 12582916 | tf_op jit(solution)/shard_map/cond/branch_1_fun/jvp()/erfc | solution.py:216
  610.3 10.0 %convolution_add_fusion.5 = f32[768,3072]{1,0:T(8,128)} fusion(f32[768,3072]{1,0:T(8,128)} %get-tuple-element.688, bf16[512,768]{1,0:T(8,128)(2,1)S(1)} %copy-done.33, f32[512,3072]{1,0:T(8,128)S(1)} %fusion.349, f32[2,512,3072]{2,1,0:T(8,128)} %get-tuple-element.677, s32[]{:T(128)S(6)} %min.15), kind=kOutput, calls=%fused_computation.560 | convolution fusion | flops 2422996992 | bytes 32243716 | tf_op jit(solution)/shard_map/cond/branch_1_fun/dot_general | solution.py:41
  626.9 7.8 convolution_add_fusion.6
  653.3 11.0 %multiply_reduce_fusion.15 = (f32[12,512]{1,0:T(8,128)S(1)}, f32[12,512,512]{1,2,0:T(8,128)}) fusion(f32[12,512,512]{1,2,0:T(8,128)} %copy-done.1, f32[12,512]{1,0:T(8,128)S(1)} %dynamic-slice_bitcast_fusion.2, pred[512,512]{0,1:T(8,128)(4,1)S(1)} %fusion.387, bf16[512,12,64]{0,2,1:T(8,128)(2,1)S(1)} %bitcast.623, bf16[512,12,64]{0,2,1:T(8,128)(2,1)S(1)} %bitcast.633), kind=kOutput, calls=%fused_computation.522 | convolution fusion | flops 418375680 | bytes 27049984 | tf_op jit(solution)/shard_map/cond/branch_1_fun/qhd,khd->hqk/dot_general | solution.py:101
  665.9 7.2 multiply_convert_fusion.6
  677.7 8.3 convolution_add_fusion.4
  701.1 6.7 convert_element_type.539
  716.5 57.9 %all-reduce = f32[16,576]{1,0:T(8,128)S(1)} all-reduce(f32[16,576]{1,0:T(8,128)S(1)} %concatenate.12), channel_id=2, replica_groups=mesh['section'=2,'dp'=16] {'dp'}, use_global_device_ids=true, to_apply=%region_84.85.clone | all-reduce | flops 9216 | bytes 73728
  778.4 45.9 %reduce-scatter.5.cloned.1.call-done = bf16[144,768]{1,0:T(8,128)(2,1)} async-done(((bf16[2304,768]{1,0:T(8,128)(2,1)}), bf16[144,768]{1,0:T(8,128)(2,1)}) %reduce-scatter.5.cloned.1.call-update) | async-done | bytes 221200 | tf_op jit(solution)/shard_map/reduce_scatter | solution.py:432
  826.0 76.6 %reduce-scatter.11.cloned.1.call-done = bf16[48,3072]{1,0:T(8,128)(2,1)} async-done(((bf16[768,3072]{1,0:T(8,128)(2,1)}), bf16[48,3072]{1,0:T(8,128)(2,1)}) %reduce-scatter.11.cloned.1.call-update) | async-done | bytes 294928 | tf_op jit(solution)/shard_map/reduce_scatter | solution.py:432
  904.5 77.0 %reduce-scatter.9.cloned.1.call-done = bf16[192,768]{1,0:T(8,128)(2,1)} async-done(((bf16[3072,768]{1,0:T(8,128)(2,1)}), bf16[192,768]{1,0:T(8,128)(2,1)}) %reduce-scatter.9.cloned.1.call-update) | async-done | bytes 294928 | tf_op jit(solution)/shard_map/reduce_scatter | solution.py:432
  (377 shorter events, 293.9 us)
Async XLA Ops:
  7.2 769.7 %reduce-scatter.7.cloned.1.call-start = ((), (), s32[]{:S(2)}) async-start(), calls=%async_computation.5 | async-start | bytes 1253376 | tf_op jit(solution)/shard_map/reduce_scatter | solution.py:432
  13.9 10.7 %copy-start.10 = (bf16[1024,768]{1,0:T(8,128)(2,1)S(1)}, bf16[1024,768]{1,0:T(8,128)(2,1)}, u32[]{:S(2)}) copy-start(bf16[1024,768]{1,0:T(8,128)(2,1)} %get-tuple-element.517) | copy-start | bytes 4718596 | tf_op jit(solution)/shard_map/cond
  14.0 11.8 %copy-start.71 = (bf16[768,2304]{1,0:T(8,128)(2,1)S(1)}, bf16[768,2304]{1,0:T(8,128)(2,1)}, u32[]{:S(2)}) copy-start(bf16[768,2304]{1,0:T(8,128)(2,1)} %get-tuple-element.522) | copy-start | bytes 10616836 | tf_op jit(solution)/shard_map/cond
  51.1 17.1 %copy-start.3 = (f32[2,512,768]{2,1,0:T(8,128)}, f32[2,512,768]{2,1,0:T(8,128)S(1)}, u32[]{:S(2)}) copy-start(f32[2,512,768]{2,1,0:T(8,128)S(1)} %get-tuple-element.1477) | copy-start | bytes 9437188 | tf_op jit(solution)/shard_map/cond
  62.0 14.6 %slice-start.11 = ((s8[4718592]{0:T(1024)(128)(4,1)}), s8[4194304]{0:T(1024)(128)(4,1)S(1)}, s32[]{:S(2)}) async-start(s8[4718592]{0:T(1024)(128)(4,1)} %bitcast.670), calls=%async_computation.19 | async-start | bytes 8388608 | tf_op jit(solution)/shard_map/cond
  76.7 17.3 %copy-start.4 = (f32[2,512,768]{2,1,0:T(8,128)S(1)}, f32[2,512,768]{2,1,0:T(8,128)}, u32[]{:S(2)}) copy-start(f32[2,512,768]{2,1,0:T(8,128)} %copy-done.3) | copy-start | bytes 9437188 | tf_op jit(solution)/shard_map/cond
  76.7 17.3 %copy-start.50 = (f32[2,1,12,512]{3,2,1,0:T(8,128)S(1)}, f32[2,1,12,512]{3,2,1,0:T(8,128)}, u32[]{:S(2)}) copy-start(f32[2,1,12,512]{3,2,1,0:T(8,128)} %copy-done.49) | copy-start | bytes 147460 | tf_op jit(solution)/shard_map/cond
  96.2 19.3 %collective-permute-start = (bf16[512,768]{1,0:T(8,128)(2,1)}, bf16[512,768]{1,0:T(8,128)(2,1)}, u32[]{:S(2)}, u32[]{:S(2)}) collective-permute-start(bf16[512,768]{1,0:T(8,128)(2,1)} %dynamic-slice_bitcast_fusion.4), channel_id=1, source_target_pairs={{0,16},{1,17},{2,18},{3,19},{4,20},{5,21},{6,22},{7,23},{8,24},{9,... | collective-permute-start | bytes 2359304 | tf_op jit(solution)/shard_map/ppermute | solution.py:21
  149.6 9.5 copy-start.64
  155.0 11.4 %slice-start.13 = ((s8[4718592]{0:T(1024)(128)(4,1)}), s8[4194304]{0:T(1024)(128)(4,1)S(1)}, s32[]{:S(2)}) async-start(s8[4718592]{0:T(1024)(128)(4,1)} %bitcast.672), calls=%async_computation.21 | async-start | bytes 8388608 | tf_op jit(solution)/shard_map/cond
  185.2 22.0 %collective-permute-start.1 = (bf16[512,768]{1,0:T(8,128)(2,1)}, bf16[512,768]{1,0:T(8,128)(2,1)}, u32[]{:S(2)}, u32[]{:S(2)}) collective-permute-start(bf16[512,768]{1,0:T(8,128)(2,1)} %dynamic-slice_bitcast_fusion.3), channel_id=1, source_target_pairs={{0,16},{1,17},{2,18},{3,19},{4,20},{5,21},{6,22},{7,23},{8,24},{9,... | collective-permute-start | bytes 2359304 | tf_op jit(solution)/shard_map/ppermute | solution.py:21
  240.7 175.0 %collective-permute-start.2 = (bf16[512,768]{1,0:T(8,128)(2,1)}, bf16[512,768]{1,0:T(8,128)(2,1)}, u32[]{:S(2)}, u32[]{:S(2)}) collective-permute-start(bf16[512,768]{1,0:T(8,128)(2,1)} %fusion.406), channel_id=1, source_target_pairs={{16,0},{17,1},{18,2},{19,3},{20,4},{21,5},{22,6},{23,7},{24,8},{25... | collective-permute-start | bytes 2359304 | tf_op jit(solution)/shard_map/ppermute | solution.py:21
  441.0 14.2 %copy-start.32 = (bf16[512,768]{1,0:T(8,128)(2,1)S(1)}, bf16[512,768]{1,0:T(8,128)(2,1)}, u32[]{:S(2)}) copy-start(bf16[512,768]{1,0:T(8,128)(2,1)} %get-tuple-element.1368) | copy-start | bytes 2359300 | tf_op jit(solution)/shard_map/cond
  441.0 24.3 %slice-start.17 = ((s8[4718592]{0:T(1024)(128)(4,1)}), s8[4194304]{0:T(1024)(128)(4,1)S(1)}, s32[]{:S(2)}) async-start(s8[4718592]{0:T(1024)(128)(4,1)} %bitcast.676), calls=%async_computation.25 | async-start | bytes 8388608 | tf_op jit(solution)/shard_map/cond
  455.2 10.0 %slice-start.18 = ((s8[4718592]{0:T(1024)(128)(4,1)}), s8[524288]{0:T(1024)(128)(4,1)S(1)}, s32[]{:S(2)}) async-start(s8[4718592]{0:T(1024)(128)(4,1)} %bitcast.676), calls=%async_computation.26 | async-start | bytes 1048576 | tf_op jit(solution)/shard_map/cond
  505.0 13.6 %slice-start = ((s8[12582912]{0:T(1024)(128)(4,1)}), s8[4194304]{0:T(1024)(128)(4,1)S(1)}, s32[]{:S(2)}) async-start(s8[12582912]{0:T(1024)(128)(4,1)} %bitcast.592), calls=%async_computation.8 | async-start | bytes 8388608 | tf_op jit(solution)/shard_map/cond
  505.0 13.6 %slice-start.1 = ((s8[12582912]{0:T(1024)(128)(4,1)}), s8[4194304]{0:T(1024)(128)(4,1)S(1)}, s32[]{:S(2)}) async-start(s8[12582912]{0:T(1024)(128)(4,1)} %bitcast.592), calls=%async_computation.9 | async-start | bytes 8388608 | tf_op jit(solution)/shard_map/cond
  505.0 13.6 %slice-start.2 = ((s8[12582912]{0:T(1024)(128)(4,1)}), s8[4194304]{0:T(1024)(128)(4,1)S(1)}, s32[]{:S(2)}) async-start(s8[12582912]{0:T(1024)(128)(4,1)} %bitcast.592), calls=%async_computation.10 | async-start | bytes 8388608 | tf_op jit(solution)/shard_map/cond
  532.3 9.0 copy-start.59
  532.3 9.0 copy-start.65
  532.3 9.0 copy-start.72
  550.5 20.0 %collective-permute-start.3 = (bf16[512,768]{1,0:T(8,128)(2,1)}, bf16[512,768]{1,0:T(8,128)(2,1)}, u32[]{:S(2)}, u32[]{:S(2)}) collective-permute-start(bf16[512,768]{1,0:T(8,128)(2,1)} %fusion.407), channel_id=1, source_target_pairs={{16,0},{17,1},{18,2},{19,3},{20,4},{21,5},{22,6},{23,7},{24,8},{25... | collective-permute-start | bytes 2359304 | tf_op jit(solution)/shard_map/ppermute | solution.py:21
  577.2 14.2 %copy-start.53 = (f32[512]{0:T(512)}, f32[512]{0:T(512)S(1)}, u32[]{:S(2)}) copy-start(f32[512]{0:T(512)S(1)} %broadcast_multiply_fusion.20) | copy-start | bytes 6148 | tf_op jit(solution)/shard_map/cond
  596.0 14.2 %copy-start.33 = (bf16[512,768]{1,0:T(8,128)(2,1)S(1)}, bf16[512,768]{1,0:T(8,128)(2,1)}, u32[]{:S(2)}) copy-start(bf16[512,768]{1,0:T(8,128)(2,1)} %get-tuple-element.1372) | copy-start | bytes 2359300 | tf_op jit(solution)/shard_map/cond
  596.0 24.3 %slice-start.19 = ((s8[4718592]{0:T(1024)(128)(4,1)}), s8[4194304]{0:T(1024)(128)(4,1)S(1)}, s32[]{:S(2)}) async-start(s8[4718592]{0:T(1024)(128)(4,1)} %bitcast.678), calls=%async_computation.27 | async-start | bytes 8388608 | tf_op jit(solution)/shard_map/cond
  610.3 10.0 %slice-start.20 = ((s8[4718592]{0:T(1024)(128)(4,1)}), s8[524288]{0:T(1024)(128)(4,1)S(1)}, s32[]{:S(2)}) async-start(s8[4718592]{0:T(1024)(128)(4,1)} %bitcast.678), calls=%async_computation.28 | async-start | bytes 1048576 | tf_op jit(solution)/shard_map/cond
  653.3 11.0 %slice-start.3 = ((s8[12582912]{0:T(1024)(128)(4,1)}), s8[4194304]{0:T(1024)(128)(4,1)S(1)}, s32[]{:S(2)}) async-start(s8[12582912]{0:T(1024)(128)(4,1)} %bitcast.594), calls=%async_computation.11 | async-start | bytes 8388608 | tf_op jit(solution)/shard_map/cond
  653.3 11.0 %slice-start.4 = ((s8[12582912]{0:T(1024)(128)(4,1)}), s8[4194304]{0:T(1024)(128)(4,1)S(1)}, s32[]{:S(2)}) async-start(s8[12582912]{0:T(1024)(128)(4,1)} %bitcast.594), calls=%async_computation.12 | async-start | bytes 8388608 | tf_op jit(solution)/shard_map/cond
  653.3 12.6 %slice-start.5 = ((s8[12582912]{0:T(1024)(128)(4,1)}), s8[4194304]{0:T(1024)(128)(4,1)S(1)}, s32[]{:S(2)}) async-start(s8[12582912]{0:T(1024)(128)(4,1)} %bitcast.594), calls=%async_computation.13 | async-start | bytes 8388608 | tf_op jit(solution)/shard_map/cond
  695.9 128.4 %reduce-scatter.5.cloned.1.call-start = ((), (), s32[]{:S(2)}) async-start(), calls=%async_computation.4 | async-start | bytes 3760128 | tf_op jit(solution)/shard_map/reduce_scatter | solution.py:432
  701.1 201.6 %reduce-scatter.11.cloned.1.call-start = ((), (), s32[]{:S(2)}) async-start(), calls=%async_computation.7 | async-start | bytes 5013504 | tf_op jit(solution)/shard_map/reduce_scatter | solution.py:432
  707.8 273.7 %reduce-scatter.9.cloned.1.call-start = ((), (), s32[]{:S(2)}) async-start(), calls=%async_computation.6 | async-start | bytes 5013504 | tf_op jit(solution)/shard_map/reduce_scatter | solution.py:432
  (44 other events, 266.0 us)
Sparse Core Ops, SparseCore 0:
  696.0 57.1 reduce-scatter.6
  757.1 67.1 reduce-scatter.4
  828.1 74.4 reduce-scatter.10
  906.9 74.6 reduce-scatter.8

commit v2 on v1

v2 whole, which is shorter than its diff:
```python
import jax
import jax.numpy as jnp
from jax import lax
from jax.experimental import pallas as pl
from jax.experimental.pallas import tpu as pltpu
from jax.sharding import PartitionSpec as P

HEADS = 12
HEAD_DIM = 64
SEQ = 512
PAIR = 2 * HEAD_DIM
PAIRS = HEADS // 2
TILE = 256
ROWS = 128
EPSILON = 1e-06
SCORE_SCALE = 0.125
FAR = -1e30
F32 = jnp.float32
LOW = jnp.bfloat16
MESH = pl.DeviceIdType.MESH


def times(left, right):
    return lax.dot_general(left, right, (((1,), (0,)), ((), ())), preferred_element_type=F32)


def times_t(left, right):
    return lax.dot_general(left, right, (((1,), (1,)), ((), ())), preferred_element_type=F32)


def loop(count, body):
    def step(index, carry):
        body(index)
        return carry

    lax.fori_loop(0, count, step, 0)


def part(index, size):
    return pl.ds(pl.multiple_of(index * size, size), size)


def norm_rows(values):
    average = jnp.mean(values, axis=-1, keepdims=True)
    centred = values - average
    inv_scale = lax.rsqrt(jnp.mean(centred * centred, axis=-1, keepdims=True) + EPSILON)
    return centred * inv_scale, inv_scale


def norm_back(normed_grad, whitened, inv_scale, gain):
    scaled = normed_grad * gain
    return inv_scale * (
        scaled
        - jnp.mean(scaled, axis=-1, keepdims=True)
        - whitened * jnp.mean(scaled * whitened, axis=-1, keepdims=True)
    )


def fold_rows(values):
    rows, width = values.shape
    return jnp.sum(values.reshape(rows // 8, 8, width), axis=0)


def fill_bias(code_row, bias):
    across = jnp.transpose(jnp.broadcast_to(code_row, (128, SEQ)))
    for block in range(SEQ // 128):
        lanes = slice(block * 128, (block + 1) * 128)
        bias[:, lanes] = jnp.where(across == code_row[:, lanes], 0.0, FAR)


def gelu_both(upper):
    cumulative = 0.5 * (1.0 + lax.erf(upper * (0.5**0.5)))
    density = jnp.exp(-0.5 * (upper * upper)) * 0.3989422804014327
    return upper * cumulative, cumulative + upper * density


def relay_kernel(
    x_hbm,
    cot_hbm,
    code_ref,
    first_gain,
    first_shift,
    project_hbm,
    query_bias,
    value_bias,
    out_hbm,
    out_bias,
    second_gain,
    second_shift,
    up_hbm,
    up_bias,
    down_hbm,
    down_bias,
    result_hbm,
    input_grad_hbm,
    sums_ref,
    up_sums_ref,
    normed_hbm,
    attended_hbm,
    second_hbm,
    hidden_hbm,
    mixed_hbm,
    branch_hbm,
    upper_hbm,
    output_hbm,
    project,
    out_weight,
    up_weight,
    down_weight,
    x_in,
    g_in,
    normed,
    mixed,
    attended,
    middle,
    second_normed,
    hidden,
    slope,
    result,
    branch,
    attended_low,
    wide,
    input_grad,
    grad_low,
    bias,
    lse_cols,
    lse_rows,
    delta_rows,
    sums,
    up_sums,
    weight_sem,
    x_sem,
    g_sem,
    send_sem,
    out_sem,
):
    section = lax.axis_index("section")
    width = x_in.shape[2]
    hidden_width = hidden.shape[2]
    packs = x_in.shape[0]
    last = lax.axis_size("section") - 1
    partner = {"section": 1 - section}

    def rows_of(ref, pack):
        return ref.at[pl.ds(pl.multiple_of(pack * SEQ, SEQ), SEQ)]

    weights = (
        pltpu.make_async_copy(project_hbm.at[0], project, weight_sem.at[0]),
        pltpu.make_async_copy(out_hbm.at[0], out_weight, weight_sem.at[1]),
        pltpu.make_async_copy(up_hbm.at[0], up_weight, weight_sem.at[2]),
        pltpu.make_async_copy(down_hbm.at[0], down_weight, weight_sem.at[3]),
    )

    @pl.when(section == 0)
    def _():
        for pack in range(packs):
            pltpu.make_async_copy(rows_of(x_hbm, pack), x_in.at[pack], x_sem.at[pack]).start()

    for copy in weights:
        copy.start()

    @pl.when(section == last)
    def _():
        for pack in range(packs):
            pltpu.make_async_copy(rows_of(cot_hbm, pack), g_in.at[pack], g_sem.at[pack]).start()

    barrier = pltpu.get_barrier_semaphore()
    pl.semaphore_signal(barrier, inc=1, device_id=partner, device_id_type=MESH)
    pl.semaphore_wait(barrier, 1)

    sums[...] = jnp.zeros_like(sums)
    up_sums[...] = jnp.zeros_like(up_sums)

    def hop_forward(pack):
        return pltpu.make_async_remote_copy(
            src_ref=result.at[pack],
            dst_ref=x_in.at[pack],
            send_sem=send_sem.at[0, pack],
            recv_sem=x_sem.at[pack],
            device_id=partner,
            device_id_type=MESH,
        )

    def hop_backward(pack):
        return pltpu.make_async_remote_copy(
            src_ref=grad_low.at[pack],
            dst_ref=g_in.at[pack],
            send_sem=send_sem.at[1, pack],
            recv_sem=g_sem.at[pack],
            device_id=partner,
            device_id_type=MESH,
        )

    kept = (
        (result, result_hbm),
        (normed, normed_hbm),
        (attended, attended_hbm),
        (second_normed, second_hbm),
        (hidden, hidden_hbm),
        (mixed, mixed_hbm),
        (branch, branch_hbm),
        (slope, upper_hbm),
        (g_in, output_hbm),
        (input_grad, input_grad_hbm),
    )

    def store(index, pack):
        source, target = kept[index]
        return pltpu.make_async_copy(source.at[pack], rows_of(target, pack), out_sem.at[index, pack])

    lane = lax.broadcasted_iota(jnp.int32, (SEQ, PAIR), 1)

    def forward(pack):
        first = pack == 0

        @pl.when(section == 0)
        def _():
            pltpu.make_async_copy(rows_of(x_hbm, pack), x_in.at[pack], x_sem.at[pack]).wait()

        @pl.when(section == last)
        def _():
            hop_forward(pack).wait_recv()

        gain = first_gain[...].astype(F32)
        shift = first_shift[...].astype(F32)

        def norm_step(block):
            rows = part(block, ROWS)
            white, _ = norm_rows(x_in[pack, rows].astype(F32))
            normed[pack, rows] = (white * gain + shift).astype(LOW)

        loop(SEQ // ROWS, norm_step)
        fill_bias(code_ref[pack], bias)

        @pl.when(first)
        def _():
            weights[0].wait()

        for third, offset_ref in enumerate((query_bias, None, value_bias)):

            def project_step(tile, third=third, offset_ref=offset_ref):
                here = part(tile, TILE)
                there = pl.ds(pl.multiple_of(third * width + tile * TILE, TILE), TILE)
                value = times(normed[pack], project[:, there])
                if offset_ref is not None:
                    value = value + offset_ref[:, here].astype(F32)
                mixed[pack, :, there] = value.astype(LOW)

            loop(width // TILE, project_step)

        def attend_step(pair):
            here = part(pair, PAIR)
            query = mixed[pack, :, here]
            key = mixed[pack, :, pl.ds(pl.multiple_of(width + pair * PAIR, PAIR), PAIR)]
            value = mixed[pack, :, pl.ds(pl.multiple_of(2 * width + pair * PAIR, PAIR), PAIR)]
            for block in range(SEQ // TILE):
                rows = slice(block * TILE, (block + 1) * TILE)
                outs = []
                for side in range(2):
                    own = (lane[rows] < HEAD_DIM) == (side == 0)
                    one = jnp.where(own, query[rows] * SCORE_SCALE, 0.0).astype(LOW)
                    scores = times_t(one, key) + bias[rows]
                    row_max = jnp.max(scores, axis=-1, keepdims=True)
                    exponent = jnp.exp(scores - row_max)
                    row_sum = jnp.sum(exponent, axis=-1, keepdims=True)
                    outs.append(times(exponent.astype(LOW), value) * (1.0 / row_sum))
                    log_sum = row_max + jnp.log(row_sum)
                    lse_cols[rows] = jnp.where(lane[rows] == 2 * pair + side, log_sum, lse_cols[rows])
                attended[pack, rows, here] = jnp.where(lane[rows] < HEAD_DIM, outs[0], outs[1]).astype(LOW)

        loop(PAIRS, attend_step)
        lse_rows[pack] = jnp.transpose(lse_cols[...])[: lse_rows.shape[1]]

        @pl.when(first)
        def _():
            weights[1].wait()

        def out_step(tile):
            here = part(tile, TILE)
            middle[pack, :, here] = x_in[pack, :, here].astype(F32) + (
                times(attended[pack], out_weight[:, here]) + out_bias[:, here].astype(F32)
            )

        loop(width // TILE, out_step)
        gain2 = second_gain[...].astype(F32)
        shift2 = second_shift[...].astype(F32)

        def second_step(block):
            rows = part(block, ROWS)
            white, _ = norm_rows(middle[pack, rows])
            second_normed[pack, rows] = (white * gain2 + shift2).astype(LOW)

        loop(SEQ // ROWS, second_step)

        @pl.when(first)
        def _():
            weights[2].wait()

        def up_step(tile):
            here = part(tile, TILE)
            upper = times(second_normed[pack], up_weight[:, here]) + up_bias[:, here].astype(F32)
            act, act_slope = gelu_both(upper)
            hidden[pack, :, here] = act.astype(LOW)
            slope[pack, :, here] = act_slope.astype(LOW)

        loop(hidden_width // TILE, up_step)

        @pl.when(first)
        def _():
            weights[3].wait()

        def down_step(tile):
            here = part(tile, TILE)
            value = middle[pack, :, here] + (
                times(hidden[pack], down_weight[:, here]) + down_bias[:, here].astype(F32)
            )
            result[pack, :, here] = value.astype(LOW)

        loop(width // TILE, down_step)

        @pl.when(section == 0)
        def _():
            hop_forward(pack).start()

        for index in range(5):
            store(index, pack).start()

    def backward(order):
        pack = packs - 1 - order

        @pl.when(section == last)
        def _():
            pltpu.make_async_copy(rows_of(cot_hbm, pack), g_in.at[pack], g_sem.at[pack]).wait()

        @pl.when(section == 0)
        def _():
            hop_backward(pack).wait_recv()

        store(8, pack).start()
        fill_bias(code_ref[pack], bias)

        def fold_g(block):
            sums[7] += fold_rows(g_in[pack, part(block, ROWS)].astype(F32))

        loop(SEQ // ROWS, fold_g)

        def hidden_step(tile):
            here = part(tile, TILE)
            value = times_t(g_in[pack], down_weight[here]).astype(LOW).astype(F32)
            low = (value * slope[pack, :, here].astype(F32)).astype(LOW)
            slope[pack, :, here] = low
            up_sums[:, here] += fold_rows(low.astype(F32))

        loop(hidden_width // TILE, hidden_step)
        store(7, pack).start()

        def second_step(tile):
            here = part(tile, TILE)
            wide[:, here] = times_t(slope[pack], up_weight[here])

        loop(width // TILE, second_step)
        gain2 = second_gain[...].astype(F32)

        def second_back(block):
            rows = part(block, ROWS)
            grad = wide[rows]
            white, scale = norm_rows(middle[pack, rows])
            total = g_in[pack, rows].astype(F32) + norm_back(grad, white, scale, gain2)
            sums[5] += fold_rows(grad * white)
            sums[6] += fold_rows(grad)
            middle[pack, rows] = total
            low = total.astype(LOW)
            branch[pack, rows] = low
            sums[4] += fold_rows(low.astype(F32))

        loop(SEQ // ROWS, second_back)
        store(6, pack).start()

        def attended_step(tile):
            here = part(tile, TILE)
            attended_low[:, here] = times_t(branch[pack], out_weight[here]).astype(LOW)

        loop(width // TILE, attended_step)

        head_of = lax.broadcasted_iota(jnp.int32, (delta_rows.shape[0], width), 1) // HEAD_DIM
        pick = jnp.where(head_of == lax.broadcasted_iota(jnp.int32, head_of.shape, 0), 1.0, 0.0).astype(LOW)
        product = attended_low[...].astype(F32) * attended[pack].astype(F32)
        coarse = product.astype(LOW)
        fine = (product - coarse.astype(F32)).astype(LOW)
        delta_rows[...] = times_t(pick, coarse) + times_t(pick, fine)

        def attend_back(pair):
            here = part(pair, PAIR)
            key_part = pl.ds(pl.multiple_of(width + pair * PAIR, PAIR), PAIR)
            value_part = pl.ds(pl.multiple_of(2 * width + pair * PAIR, PAIR), PAIR)
            query = mixed[pack, :, here]
            key = mixed[pack, :, key_part]
            value = mixed[pack, :, value_part]
            upstream = attended_low[:, here]
            key_across = jnp.transpose(key)
            query_across = []
            key_grad = [0.0, 0.0]
            value_grad = [0.0, 0.0]
            for side in range(2):
                own = (lane < HEAD_DIM) == (side == 0)
                one_query = jnp.where(own, query * SCORE_SCALE, 0.0).astype(LOW)
                one_up = jnp.where(own, upstream, 0.0).astype(LOW)
                log_row = lse_rows[pack, pl.ds(2 * pair + side, 1)]
                delta_row = delta_rows[pl.ds(2 * pair + side, 1)]
                heads = slice(side * HEAD_DIM, (side + 1) * HEAD_DIM)
                across = 0.0
                for block in range(SEQ // TILE):
                    rows = slice(block * TILE, (block + 1) * TILE)
                    soft = jnp.exp(times_t(key[rows], one_query) + bias[rows] - log_row)
                    soft_grad = times_t(value[rows], one_up)
                    score_low = (soft * (soft_grad - delta_row)).astype(LOW)
                    value_grad[block] += times(soft.astype(LOW), one_up)
                    key_grad[block] += times(score_low, one_query)
                    across += times(key_across[heads, rows], score_low)
                query_across.append(across)
            query_grad = (jnp.transpose(jnp.concatenate(query_across, axis=0)) * SCORE_SCALE).astype(LOW)
            mixed[pack, :, here] = query_grad
            sums[2, :, here] += fold_rows(query_grad.astype(F32))
            for block in range(SEQ // TILE):
                rows = slice(block * TILE, (block + 1) * TILE)
                mixed[pack, rows, key_part] = key_grad[block].astype(LOW)
                low = value_grad[block].astype(LOW)
                mixed[pack, rows, value_part] = low
                sums[3, :, here] += fold_rows(low.astype(F32))

        loop(PAIRS, attend_back)
        store(5, pack).start()

        def first_step(tile):
            here = part(tile, TILE)
            wide[:, here] = times_t(mixed[pack], project[here])

        loop(width // TILE, first_step)
        gain = first_gain[...].astype(F32)

        def first_back(block):
            rows = part(block, ROWS)
            grad = wide[rows]
            white, scale = norm_rows(x_in[pack, rows].astype(F32))
            total = middle[pack, rows] + norm_back(grad, white, scale, gain)
            sums[0] += fold_rows(grad * white)
            sums[1] += fold_rows(grad)
            input_grad[pack, rows] = total
            grad_low[pack, rows] = total.astype(LOW)

        loop(SEQ // ROWS, first_back)

        @pl.when(section == last)
        def _():
            hop_backward(pack).start()

        store(9, pack).start()

    loop(packs, forward)
    loop(packs, backward)

    for index in range(sums.shape[0]):
        sums_ref[index : index + 1] = jnp.sum(sums[index], axis=0, keepdims=True)
    up_sums_ref[...] = jnp.sum(up_sums[...], axis=0, keepdims=True)

    for pack in range(packs):
        for index in range(len(kept)):
            store(index, pack).wait()

    @pl.when(section == 0)
    def _():
        for pack in range(packs):
            hop_forward(pack).wait_send()

    @pl.when(section == last)
    def _():
        for pack in range(packs):
            hop_backward(pack).wait_send()


def relay(arrays):
    inputs, cotangent, segments, valid_flags = arrays[:4]
    rows, width = inputs.shape
    hidden_width = arrays[13].shape[2]
    packs = rows // SEQ
    places = lax.broadcasted_iota(jnp.int32, (rows,), 0) + SEQ
    code = jnp.where(valid_flags == 1, segments, places).astype(F32).reshape(packs, 1, SEQ)
    anywhere = pl.BlockSpec(memory_space=pl.ANY)
    vmem = pl.BlockSpec(memory_space=pltpu.VMEM)

    def low(columns):
        return jax.ShapeDtypeStruct((rows, columns), LOW)

    outs = (
        low(width),
        jax.ShapeDtypeStruct((rows, width), F32),
        jax.ShapeDtypeStruct((8, width), F32),
        jax.ShapeDtypeStruct((1, hidden_width), F32),
        low(width),
        low(width),
        low(width),
        low(hidden_width),
        low(3 * width),
        low(width),
        low(hidden_width),
        low(width),
    )

    def held(columns, kind=LOW):
        return pltpu.VMEM((packs, SEQ, columns), kind)

    scratch = [
        pltpu.VMEM((width, 3 * width), LOW),
        pltpu.VMEM((width, width), LOW),
        pltpu.VMEM((width, hidden_width), LOW),
        pltpu.VMEM((hidden_width, width), LOW),
        held(width),
        held(width),
        held(width),
        held(3 * width),
        held(width),
        held(width, F32),
        held(width),
        held(hidden_width),
        held(hidden_width),
        held(width),
        held(width),
        pltpu.VMEM((SEQ, width), LOW),
        pltpu.VMEM((SEQ, width), F32),
        held(width, F32),
        held(width),
        pltpu.VMEM((SEQ, SEQ), F32),
        pltpu.VMEM((SEQ, 128), F32),
        pltpu.VMEM((packs, 16, SEQ), F32),
        pltpu.VMEM((16, SEQ), F32),
        pltpu.VMEM((8, 8, width), F32),
        pltpu.VMEM((8, hidden_width), F32),
        pltpu.SemaphoreType.DMA((4,)),
        pltpu.SemaphoreType.DMA((packs,)),
        pltpu.SemaphoreType.DMA((packs,)),
        pltpu.SemaphoreType.DMA((2, packs)),
        pltpu.SemaphoreType.DMA((10, packs)),
    ]
    return pl.pallas_call(
        relay_kernel,
        out_shape=outs,
        in_specs=[
            anywhere, anywhere, vmem,
            vmem, vmem, anywhere, vmem, vmem, anywhere, vmem,
            vmem, vmem, anywhere, vmem, anywhere, vmem,
        ],
        out_specs=[anywhere, anywhere, vmem, vmem] + [anywhere] * 8,
        scratch_shapes=scratch,
        name="relay",
        compiler_params=pltpu.CompilerParams(
            collective_id=0, has_side_effects=True, vmem_limit_bytes=66 * 2**20 - 2**21
        ),
    )(inputs, cotangent, code, *arrays[4:])


def contract_rows(left, right):
    return lax.dot_general(left, right, (((0,), (0,)), ((), ())), preferred_element_type=F32)


def on_device(*arrays):
    shards = lax.axis_size("dp")
    (
        result, input_grad, sums, up_sums,
        normed, attended, second_normed, hidden, mixed, branch, upper_low, output_low,
    ) = relay(arrays)

    def reduce_rows(left, right):
        term = contract_rows(left, right).astype(LOW)
        piece = lax.psum_scatter(term, "dp", scatter_dimension=0, tiled=True)
        return piece.astype(F32).T[None]

    packed = jnp.concatenate([sums.reshape(-1, shards, sums.shape[1] // shards).transpose(1, 0, 2).reshape(shards, -1), up_sums.reshape(shards, -1)], axis=1)
    packed = lax.psum_scatter(packed, "dp", scatter_dimension=0, tiled=True)
    size = sums.shape[1] // shards
    small = [packed[:, index * size : (index + 1) * size] for index in range(8)]
    up_small = packed[:, 8 * size :]
    return (
        result[None],
        input_grad[None],
        small[0],
        small[1],
        reduce_rows(mixed, normed),
        small[2],
        small[3],
        reduce_rows(branch, attended),
        small[4],
        small[5],
        small[6],
        reduce_rows(upper_low, second_normed),
        up_small,
        reduce_rows(output_low, hidden),
        small[7],
    )


def solution(mesh):
    stack1 = P("section", None)
    stack2 = P("section", None, None)
    in_specs = (
        P("dp", None), P("dp", None), P("dp"), P("dp"),
        stack1, stack1, stack2, stack1, stack1, stack2, stack1,
        stack1, stack1, stack2, stack1, stack2, stack1,
    )
    row = P("section", "dp")
    matrix = P("section", None, "dp")
    rows = P("section", "dp", None)
    out_specs = (
        rows, rows, row, row, matrix, row, row, matrix, row, row, row, matrix, row, matrix, row,
    )
    return jax.shard_map(
        on_device, mesh=mesh, in_specs=in_specs, out_specs=out_specs, check_vma=False
    )
```

time: 995 us -> 508 us (0.51)
  waiting for transfers between devices: 425 us -> 186 us
  Pallas kernels: 0 us -> 195 us
  matrix products: 219 us -> 31.8 us
  other arithmetic: 142 us -> 8.89 us
  local copies, waits for them, and re-layouts: 104 us -> 10.9 us
  loops' own time: 16.7 us -> 0 us
  starting transfers between devices: 10.7 us -> 0.34 us
    ppermute x4 -> x0, waiting for transfers between devices: 226 us -> none  [from_behind(): return lax.ppermute(value, axis, pairs)]
    pallas_call x0 -> x1, Pallas kernels: none -> 195 us  [relay(): pl.pallas_call(relay_kernel, out_shape=outs, in_specs=[anywhere, anywhere...]
    dot_general x30 -> x0, matrix products: 157 us -> none  [the longest x8 34.4 us: times_transpose(): lax.dot_general(left, right, (((1,), (1,)), ((), ())), preferred_element_...]
    convert_element_type x28 -> x1, other arithmetic: 39.2 us -> 1.3 us  [relay(): jnp.where(valid_flags == 1, segments, places).astype(F32)]
    another operation x27 -> x0, local copies, waits for them, and re-layouts: 36.7 us -> none
    reduce_sum x20 -> x0, other arithmetic: 30.7 us -> none  [the longest x6 10 us: norm_rows(): average = jnp.mean(values, axis=-1, keepdims=True)]
    dot_general x8 -> x4, matrix products: 61.8 us -> 31.8 us  [contract_rows(): lax.dot_general(left, right, (((0,), (0,)), ((), ())), preferred_element_...]
    another operation x2 -> x0, other arithmetic: 28.4 us -> none  [layer_backward(): unused, gelu_back = jax.vjp(partial(jax.nn.gelu, approximate=False), upper)]
  transfers between devices with their start and end apart: 8 -> 4, of which waited for: 7 -> 3; matrix products, arithmetic and copies ran while one was open for 3% -> 7% of each run, Pallas kernels for 0% -> 0%
where the time goes in v2:
time: 508 us; the launch traced here: 507 us
  Pallas kernels  195 us (38%)
  waiting for transfers between devices  186 us (37%)
  blocking collectives  60.7 us (12%)
  matrix products  31.8 us (6%)
  between operations  13.9 us (3%)
  local copies, waits for them, and re-layouts  10.9 us (2%)
  other arithmetic  8.89 us (2%)
    pallas_call x1, Pallas kernels, relay(): pl.pallas_call(relay_kernel, out_shape=outs, in_specs=[anywhere, anywhere...  195 us
    reduce_scatter x4, waiting for transfers between devices, reduce_rows(): piece = lax.psum_scatter(term, 'dp', scatter_dimension=0, tiled=True)  186 us
    unnamed x1, blocking collectives  60.7 us
    dot_general x4, matrix products, contract_rows(): lax.dot_general(left, right, (((0,), (0,)), ((), ())), preferred_element_...  31.8 us
  transfers between devices with their start and end apart: 4, of which 3 were waited for; matrix products, arithmetic and copies ran while one was open for 7% of the time, Pallas kernels for 0%

profile of v2, /device:TPU:0, one launch (start us, length us, event | category | flops | bytes accessed | tf_op | source)
XLA Modules:
  0.0 507.2 jit_solution(7291782913157601204)
XLA Ops:
  7.2 0.0 reduce-scatter.7.cloned.1.call-start
  7.2 1.3 select_convert_fusion
  8.5 194.6 %relay.1 = (bf16[1024,768]{1,0:T(8,128)(2,1)}, f32[1024,768]{1,0:T(8,128)}, f32[8,768]{1,0:T(8,128)}, f32[1,3072]{1,0:T(1,128)}, bf16[1024,768]{1,0:T(8,128)(2,1...) custom-call(bf16[1024,768]{1,0:T(8,128)(2,1)} %x_hbm.1, ...), custom_call_target="tpu_custom_call" | custom-call | tf_op jit(solution)/shard_map/relay/pallas_call | solution.py:544
  203.1 4.5 convolution_convert_fusion.3
  207.6 0.0 reduce-scatter.7.cloned.1.call-update
  207.6 0.0 reduce-scatter.5.cloned.1.call-start
  207.6 7.8 %convolution_convert_fusion.2 = bf16[2304,768]{1,0:T(8,128)(2,1)} fusion(bf16[1024,2304]{1,0:T(8,128)(2,1)} %get-tuple-element.31, bf16[1024,768]{1,0:T(8,128)(2,1)S(1)} %copy-done.5), kind=kOutput, calls=%fused_computation.2 | convolution fusion | flops 3625648128 | bytes 9830400 | tf_op jit(solution)/shard_map/dot_general | solution.py:562
  215.5 0.2 reduce-scatter.9.cloned.1.call-start
  215.7 1.2 copy-done.4
  216.9 9.9 %convolution_convert_fusion.1 = bf16[3072,768]{1,0:T(8,128)(2,1)} fusion(bf16[1024,3072]{1,0:T(8,128)(2,1)} %get-tuple-element.35, bf16[1024,768]{1,0:T(8,128)(2,1)S(1)} %copy-done.4), kind=kOutput, calls=%fused_computation.1 | convolution fusion | flops 4834197504 | bytes 12582912 | tf_op jit(solution)/shard_map/dot_general | solution.py:562
  226.8 0.0 reduce-scatter.11.cloned.1.call-start
  226.9 1.3 copy-done.3
  228.2 9.6 %convolution_convert_fusion = bf16[768,3072]{1,0:T(8,128)(2,1)} fusion(bf16[1024,768]{1,0:T(8,128)(2,1)S(1)} %copy-done.3, bf16[1024,3072]{1,0:T(8,128)(2,1)} %get-tuple-element.38), kind=kOutput, calls=%fused_computation | convolution fusion | flops 4834197504 | bytes 12582912 | tf_op jit(solution)/shard_map/dot_general | solution.py:562
  237.8 0.5 broadcast.3
  238.3 0.2 copy-done.2
  238.5 0.7 reduce.3
  239.2 0.1 reshape.45
  239.3 0.1 reshape.43
  239.4 0.1 reshape.44
  239.5 0.6 dynamic-slice
  240.1 60.7 %all-reduce = f32[16,576]{1,0:T(8,128)S(1)} all-reduce(f32[16,576]{1,0:T(8,128)S(1)} %pad_maximum_fusion), channel_id=2, replica_groups=mesh['section'=2,'dp'=16] {'dp'}, use_global_device_ids=true, to_apply=%region_0.1.clone | all-reduce | flops 9216 | bytes 73728
  300.8 1.3 dynamic-slice.9
  302.1 1.3 fusion
  303.4 1.6 convert_bitcast_fusion.3
  304.9 32.4 %reduce-scatter.5.cloned.1.call-done = bf16[144,768]{1,0:T(8,128)(2,1)} async-done(((bf16[2304,768]{1,0:T(8,128)(2,1)}), bf16[144,768]{1,0:T(8,128)(2,1)}) %reduce-scatter.5.cloned.1.call-update) | async-done | bytes 221200 | tf_op jit(solution)/shard_map/reduce_scatter | solution.py:574
  337.3 1.7 convert_bitcast_fusion.2
  339.0 76.6 %reduce-scatter.9.cloned.1.call-done = bf16[192,768]{1,0:T(8,128)(2,1)} async-done(((bf16[3072,768]{1,0:T(8,128)(2,1)}), bf16[192,768]{1,0:T(8,128)(2,1)}) %reduce-scatter.9.cloned.1.call-update) | async-done | bytes 294928 | tf_op jit(solution)/shard_map/reduce_scatter | solution.py:574
  415.7 1.8 convert_bitcast_fusion.1
  417.5 77.0 %reduce-scatter.11.cloned.1.call-done = bf16[48,3072]{1,0:T(8,128)(2,1)} async-done(((bf16[768,3072]{1,0:T(8,128)(2,1)}), bf16[48,3072]{1,0:T(8,128)(2,1)}) %reduce-scatter.11.cloned.1.call-update) | async-done | bytes 294928 | tf_op jit(solution)/shard_map/reduce_scatter | solution.py:574
  494.5 1.8 convert_bitcast_fusion
  496.3 2.7 copy.36
  499.0 1.7 copy.37
  (17 shorter events, 0.1 us)
Async XLA Ops:
  7.2 296.2 %reduce-scatter.7.cloned.1.call-start = ((), (), s32[]{:S(2)}) async-start(), calls=%async_computation.5 | async-start | bytes 1253376 | tf_op jit(solution)/shard_map/reduce_scatter | solution.py:574
  203.1 4.5 copy-start.5
  207.6 129.7 %reduce-scatter.5.cloned.1.call-start = ((), (), s32[]{:S(2)}) async-start(), calls=%async_computation.4 | async-start | bytes 3760128 | tf_op jit(solution)/shard_map/reduce_scatter | solution.py:574
  215.4 1.4 copy-start.4
  215.5 200.2 %reduce-scatter.9.cloned.1.call-start = ((), (), s32[]{:S(2)}) async-start(), calls=%async_computation.6 | async-start | bytes 5013504 | tf_op jit(solution)/shard_map/reduce_scatter | solution.py:574
  226.8 1.4 copy-start.3
  226.8 267.7 %reduce-scatter.11.cloned.1.call-start = ((), (), s32[]{:S(2)}) async-start(), calls=%async_computation.7 | async-start | bytes 5013504 | tf_op jit(solution)/shard_map/reduce_scatter | solution.py:574
  237.8 0.7 copy-start.2
  237.8 1.5 copy-start.1
  237.8 1.7 copy-start.6
  339.0 159.9 %copy-start = (f32[1024,768]{1,0:T(8,128)S(1)}, f32[1024,768]{1,0:T(8,128)}, u32[]{:S(2)}) copy-start(f32[1024,768]{1,0:T(8,128)} %get-tuple-element.28) | copy-start | bytes 9437188
Sparse Core Ops, SparseCore 0:
  207.7 58.5 reduce-scatter.6
  270.2 67.0 reduce-scatter.4
  341.2 74.4 reduce-scatter.8
  419.9 74.5 reduce-scatter.10

commit v3 on v2

--- a/solution.py
+++ b/solution.py
@@ -93,8 +93,7 @@
     down_bias,
     result_hbm,
     input_grad_hbm,
-    sums_ref,
-    up_sums_ref,
+    vector_ref,
     normed_hbm,
     attended_hbm,
     second_hbm,
@@ -125,7 +124,8 @@
     bias,
     lse_cols,
     lse_rows,
-    delta_rows,
+    soft_all,
+    weighted_all,
     sums,
     up_sums,
     weight_sem,
@@ -382,13 +382,6 @@
 
         loop(width // TILE, attended_step)
 
-        head_of = lax.broadcasted_iota(jnp.int32, (delta_rows.shape[0], width), 1) // HEAD_DIM
-        pick = jnp.where(head_of == lax.broadcasted_iota(jnp.int32, head_of.shape, 0), 1.0, 0.0).astype(LOW)
-        product = attended_low[...].astype(F32) * attended[pack].astype(F32)
-        coarse = product.astype(LOW)
-        fine = (product - coarse.astype(F32)).astype(LOW)
-        delta_rows[...] = times_t(pick, coarse) + times_t(pick, fine)
-
         def attend_back(pair):
             here = part(pair, PAIR)
             key_part = pl.ds(pl.multiple_of(width + pair * PAIR, PAIR), PAIR)
@@ -406,15 +399,20 @@
                 one_query = jnp.where(own, query * SCORE_SCALE, 0.0).astype(LOW)
                 one_up = jnp.where(own, upstream, 0.0).astype(LOW)
                 log_row = lse_rows[pack, pl.ds(2 * pair + side, 1)]
-                delta_row = delta_rows[pl.ds(2 * pair + side, 1)]
                 heads = slice(side * HEAD_DIM, (side + 1) * HEAD_DIM)
+                inner = 0.0
+                for block in range(SEQ // TILE):
+                    rows = slice(block * TILE, (block + 1) * TILE)
+                    soft = jnp.exp(times_t(key[rows], one_query) + bias[rows] - log_row)
+                    weighted = soft * times_t(value[rows], one_up)
+                    value_grad[block] += times(soft.astype(LOW), one_up)
+                    inner += jnp.sum(fold_rows(weighted), axis=0, keepdims=True)
+                    soft_all[rows] = soft
+                    weighted_all[rows] = weighted
                 across = 0.0
                 for block in range(SEQ // TILE):
                     rows = slice(block * TILE, (block + 1) * TILE)
-                    soft = jnp.exp(times_t(key[rows], one_query) + bias[rows] - log_row)
-                    soft_grad = times_t(value[rows], one_up)
-                    score_low = (soft * (soft_grad - delta_row)).astype(LOW)
-                    value_grad[block] += times(soft.astype(LOW), one_up)
+                    score_low = (weighted_all[rows] - soft_all[rows] * inner).astype(LOW)
                     key_grad[block] += times(score_low, one_query)
                     across += times(key_across[heads, rows], score_low)
                 query_across.append(across)
@@ -459,9 +457,12 @@
     loop(packs, forward)
     loop(packs, backward)
 
-    for index in range(sums.shape[0]):
-        sums_ref[index : index + 1] = jnp.sum(sums[index], axis=0, keepdims=True)
-    up_sums_ref[...] = jnp.sum(up_sums[...], axis=0, keepdims=True)
+    count = sums.shape[0]
+    for index in range(count):
+        vector_ref[index : index + 1] = jnp.sum(sums[index], axis=0, keepdims=True)
+    for index in range(hidden_width // width):
+        lanes = slice(index * width, (index + 1) * width)
+        vector_ref[count + index : count + index + 1] = jnp.sum(up_sums[:, lanes], axis=0, keepdims=True)
 
     for pack in range(packs):
         for index in range(len(kept)):
@@ -494,8 +495,7 @@
     outs = (
         low(width),
         jax.ShapeDtypeStruct((rows, width), F32),
-        jax.ShapeDtypeStruct((8, width), F32),
-        jax.ShapeDtypeStruct((1, hidden_width), F32),
+        jax.ShapeDtypeStruct((8 + hidden_width // width, width), F32),
         low(width),
         low(width),
         low(width),
@@ -532,7 +532,8 @@
         pltpu.VMEM((SEQ, SEQ), F32),
         pltpu.VMEM((SEQ, 128), F32),
         pltpu.VMEM((packs, 16, SEQ), F32),
-        pltpu.VMEM((16, SEQ), F32),
+        pltpu.VMEM((SEQ, SEQ), F32),
+        pltpu.VMEM((SEQ, SEQ), F32),
         pltpu.VMEM((8, 8, width), F32),
         pltpu.VMEM((8, hidden_width), F32),
         pltpu.SemaphoreType.DMA((4,)),
@@ -549,7 +550,7 @@
             vmem, vmem, anywhere, vmem, vmem, anywhere, vmem,
             vmem, vmem, anywhere, vmem, anywhere, vmem,
         ],
-        out_specs=[anywhere, anywhere, vmem, vmem] + [anywhere] * 8,
+        out_specs=[anywhere, anywhere, vmem] + [anywhere] * 8,
         scratch_shapes=scratch,
         name="relay",
         compiler_params=pltpu.CompilerParams(
@@ -558,43 +559,355 @@
     )(inputs, cotangent, code, *arrays[4:])
 
 
+def reduce_kernel(
+    vector_ref,
+    branch_hbm,
+    output_hbm,
+    upper_hbm,
+    mixed_hbm,
+    attended_hbm,
+    hidden_hbm,
+    second_hbm,
+    normed_hbm,
+    total_ref,
+    whole_ref,
+    rights,
+    loaded,
+    lefts,
+    send_core,
+    take_core,
+    send_x,
+    take_x,
+    send_z,
+    take_z,
+    own,
+    vectors,
+    take_vector,
+    right_sem,
+    load_sem,
+    core_sems,
+    x_sems,
+    z_sems,
+    vector_sems,
+):
+    units, unit, width = total_ref.shape
+    rows = rights.shape[1]
+    shards = lax.axis_size("dp")
+    levels = shards // 4
+    ups = upper_hbm.shape[1] // width
+    me = lax.axis_index("dp")
+    core, x, z = me % 2, (me // 2) % 2, me // 4
+    sibling = {"dp": me + 1 - 2 * core}
+    across = {"dp": me + 2 - 4 * x}
+
+    def level_peer(step):
+        return {"dp": ((z + step) % levels) * 4 + x * 2 + core}
+
+    first_up = 1 + ups
+    first_mixed = first_up + ups
+
+    sources = (
+        [attended_hbm]
+        + [hidden_hbm.at[:, pl.ds(block * width, width)] for block in range(ups)]
+        + [second_hbm, normed_hbm]
+    )
+
+    def right_copy(index):
+        return pltpu.make_async_copy(sources[index], rights.at[index], right_sem.at[index])
+
+    chunks = [(branch_hbm, 0), (output_hbm, 0)]
+    chunks += [(upper_hbm, block) for block in range(ups)]
+    chunks += [(mixed_hbm, block) for block in range(3)]
+
+    def left_copy(index):
+        source, block = chunks[index]
+        return pltpu.make_async_copy(
+            source.at[:, pl.ds(block * width, width)], loaded.at[index % 2], load_sem.at[index % 2]
+        )
+
+    left_copy(0).start()
+    right_copy(0).start()
+    left_copy(1).start()
+    for index in range(1, len(sources)):
+        right_copy(index).start()
+
+    barrier = pltpu.get_barrier_semaphore()
+    peers = [sibling, across] + [level_peer(step) for step in range(1, levels)]
+    for peer in peers:
+        pl.semaphore_signal(barrier, inc=1, device_id=peer, device_id_type=MESH)
+    pl.semaphore_wait(barrier, len(peers))
+
+    def send(source, target, sems, index, peer):
+        return pltpu.make_async_remote_copy(
+            src_ref=source,
+            dst_ref=target,
+            send_sem=sems.at[(0,) + index],
+            recv_sem=sems.at[(1,) + index],
+            device_id=peer,
+            device_id_type=MESH,
+        )
+
+    def to_core(j):
+        return send(send_core.at[j], take_core.at[j], core_sems, (j,), sibling)
+
+    def to_x(j):
+        return send(send_x.at[j], take_x.at[j], x_sems, (j,), across)
+
+    def to_z(j, step):
+        return send(send_z.at[j, step - 1], take_z.at[j, step - 1], z_sems, (j, step - 1), level_peer(step))
+
+    def vector_hop(index):
+        peer = (sibling, across)[index] if index < 2 else level_peer(index - 1)
+        return send(vectors.at[min(index, 2)], take_vector.at[index], vector_sems, (index,), peer)
+
+    vectors[0] = vector_ref[...]
+    vector_hop(0).start()
+
+    def turn(index, group, first_left):
+        left_copy(index).wait()
+        block = chunks[index][1]
+        source = loaded.at[index % 2]
+        pieces = unit // 16
+
+        def step(lane_block):
+            turned = jnp.transpose(source[:, part(lane_block, 128)])
+            for piece in range(8):
+                place = block * (width // 16) + lane_block * 8 + piece
+                shard, inner = lax.div(place, group), lax.rem(place, group)
+                order = (
+                    2 * levels * (1 - lax.rem(shard + core, 2))
+                    + levels * (1 - lax.rem(lax.div(shard, 2) + x, 2))
+                    + lax.div(shard, 4)
+                )
+                row = pl.multiple_of(order * unit + lax.rem(inner, pieces) * 16, 16)
+                lefts[first_left + lax.div(inner, pieces), pl.ds(row, 16)] = turned[piece * 16 : (piece + 1) * 16]
+
+        loop(width // 128, step)
+        if index + 2 < len(chunks):
+            left_copy(index + 2).start()
+
+    half = 2 * levels * unit
+    quarter = levels * unit
+
+    def left_of(j):
+        return jnp.maximum(jnp.minimum(j, 1), j + 1 - ups)
+
+    def right_of(j):
+        return jnp.minimum(j, first_up) + jnp.where(j >= first_mixed, 1, 0)
+
+    def product(j, start, count, tile):
+        return times(lefts[left_of(j), start : start + count], rights[right_of(j), :, part(tile, TILE)])
+
+    def stage_core(j):
+        def step(tile):
+            send_core[j, :, part(tile, TILE)] = product(j, 0, half, tile).astype(LOW)
+
+        loop(width // TILE, step)
+        to_core(j).start()
+
+    def stage_x(j):
+        to_core(j).wait_recv()
+
+        def step(tile):
+            here = part(tile, TILE)
+            value = product(j, half, quarter, tile) + take_core[j, :quarter, here].astype(F32)
+            send_x[j, :, here] = value.astype(LOW)
+
+        loop(width // TILE, step)
+        to_x(j).start()
+
+    def stage_z(j):
+        to_x(j).wait_recv()
+
+        def step(tile):
+            here = part(tile, TILE)
+            value = (
+                product(j, half + quarter, quarter, tile)
+                + take_core[j, quarter:, here].astype(F32)
+                + take_x[j, :, here].astype(F32)
+            )
+            own[:, :, here] = value.reshape(levels, unit, TILE)
+
+        loop(width // TILE, step)
+        for hop in range(1, levels):
+            send_z[j, hop - 1] = own[(z + hop) % levels].astype(LOW)
+            to_z(j, hop).start()
+        total_ref[j] = own[z]
+
+    def finish(j):
+        value = total_ref[j]
+        for hop in range(1, levels):
+            to_z(j, hop).wait_recv()
+            value = value + take_z[j, hop - 1].astype(F32)
+        total_ref[j] = value
+
+    def first_phase(start, stop):
+        def step(index):
+            j = index + start
+            stage_core(j)
+
+            @pl.when(j > 0)
+            def _():
+                stage_x(j - 1)
+
+        loop(stop - start, step)
+
+    turn(0, unit // 16, 0)
+    right_copy(0).wait()
+    first_phase(0, 1)
+    turn(1, unit // 16, 1)
+    for index in range(1, 1 + ups):
+        right_copy(index).wait()
+    first_phase(1, first_up)
+    vector_hop(0).wait_recv()
+    vectors[1] = vectors[0] + take_vector[0]
+    vector_hop(1).start()
+    for block in range(ups):
+        turn(2 + block, ups * unit // 16, 2)
+    right_copy(1 + ups).wait()
+    first_phase(first_up, first_mixed)
+    for block in range(3):
+        turn(2 + ups + block, 3 * unit // 16, 2 + ups)
+    right_copy(2 + ups).wait()
+    first_phase(first_mixed, units)
+    stage_x(units - 1)
+    vector_hop(1).wait_recv()
+    vectors[2] = vectors[1] + take_vector[1]
+    for hop in range(1, levels):
+        vector_hop(hop + 1).start()
+
+    def second_phase(j):
+        stage_z(j)
+
+        @pl.when(j > 0)
+        def _():
+            finish(j - 1)
+
+    loop(units, second_phase)
+    finish(units - 1)
+    whole = vectors[2]
+    for hop in range(1, levels):
+        vector_hop(hop + 1).wait_recv()
+        whole = whole + take_vector[hop + 1]
+    whole_ref[...] = whole
+
+    def drain(j):
+        to_core(j).wait_send()
+        to_x(j).wait_send()
+        for hop in range(1, levels):
+            to_z(j, hop).wait_send()
+
+    loop(units, drain)
+    for hop in range(levels + 1):
+        vector_hop(hop).wait_send()
+
+
+def reduce_parts(vector, lefts, rights):
+    shards = lax.axis_size("dp")
+    branch, output_low, upper_low, mixed = lefts
+    attended, hidden, second_normed, normed = rights
+    rows, width = branch.shape
+    ups = hidden.shape[1] // width
+    unit, levels = width // shards, shards // 4
+    units = 1 + 2 * ups + 3
+    anywhere = pl.BlockSpec(memory_space=pl.ANY)
+    vmem = pl.BlockSpec(memory_space=pltpu.VMEM)
+    total, whole = pl.pallas_call(
+        reduce_kernel,
+        out_shape=(
+            jax.ShapeDtypeStruct((units, unit, width), F32),
+            jax.ShapeDtypeStruct(vector.shape, F32),
+        ),
+        in_specs=[vmem] + [anywhere] * 8,
+        out_specs=[vmem, vmem],
+        scratch_shapes=[
+            pltpu.VMEM((3 + ups, rows, width), LOW),
+            pltpu.VMEM((2, rows, width), LOW),
+            pltpu.VMEM((5 + ups, width, rows), LOW),
+            pltpu.VMEM((units, 2 * levels * unit, width), LOW),
+            pltpu.VMEM((units, 2 * levels * unit, width), LOW),
+            pltpu.VMEM((units, levels * unit, width), LOW),
+            pltpu.VMEM((units, levels * unit, width), LOW),
+            pltpu.VMEM((units, levels - 1, unit, width), LOW),
+            pltpu.VMEM((units, levels - 1, unit, width), LOW),
+            pltpu.VMEM((levels, unit, width), F32),
+            pltpu.VMEM((3,) + vector.shape, F32),
+            pltpu.VMEM((levels + 1,) + vector.shape, F32),
+            pltpu.SemaphoreType.DMA((3 + ups,)),
+            pltpu.SemaphoreType.DMA((2,)),
+            pltpu.SemaphoreType.DMA((2, units)),
+            pltpu.SemaphoreType.DMA((2, units)),
+            pltpu.SemaphoreType.DMA((2, units, levels - 1)),
+            pltpu.SemaphoreType.DMA((2, levels + 1)),
+        ],
+        name="reduce",
+        compiler_params=pltpu.CompilerParams(
+            collective_id=1, has_side_effects=True, vmem_limit_bytes=67043328
+        ),
+    )(vector, branch, output_low, upper_low, mixed, attended, hidden, second_normed, normed)
+    first_up, first_mixed = 1 + ups, 1 + 2 * ups
+    return (
+        whole,
+        total[first_mixed:].reshape(3 * unit, width).T,
+        total[0].T,
+        total[first_up:first_mixed].reshape(ups * unit, width).T,
+        total[1:first_up].transpose(0, 2, 1).reshape(ups * width, unit),
+    )
+
+
 def contract_rows(left, right):
     return lax.dot_general(left, right, (((0,), (0,)), ((), ())), preferred_element_type=F32)
 
 
+def scatter_parts(vector, lefts, rights):
+    def reduce_rows(left, right):
+        piece = lax.psum_scatter(contract_rows(left, right), "dp", scatter_dimension=0, tiled=True)
+        return piece.T
+
+    branch, output_low, upper_low, mixed = lefts
+    attended, hidden, second_normed, normed = rights
+    return (
+        lax.psum(vector, "dp"),
+        reduce_rows(mixed, normed),
+        reduce_rows(branch, attended),
+        reduce_rows(upper_low, second_normed),
+        reduce_rows(output_low, hidden),
+    )
+
+
 def on_device(*arrays):
     shards = lax.axis_size("dp")
+    me = lax.axis_index("dp")
     (
-        result, input_grad, sums, up_sums,
+        result, input_grad, vector,
         normed, attended, second_normed, hidden, mixed, branch, upper_low, output_low,
     ) = relay(arrays)
-
-    def reduce_rows(left, right):
-        term = contract_rows(left, right).astype(LOW)
-        piece = lax.psum_scatter(term, "dp", scatter_dimension=0, tiled=True)
-        return piece.astype(F32).T[None]
-
-    packed = jnp.concatenate([sums.reshape(-1, shards, sums.shape[1] // shards).transpose(1, 0, 2).reshape(shards, -1), up_sums.reshape(shards, -1)], axis=1)
-    packed = lax.psum_scatter(packed, "dp", scatter_dimension=0, tiled=True)
-    size = sums.shape[1] // shards
-    small = [packed[:, index * size : (index + 1) * size] for index in range(8)]
-    up_small = packed[:, 8 * size :]
+    lefts = (branch, output_low, upper_low, mixed)
+    rights = (attended, hidden, second_normed, normed)
+    width = branch.shape[1]
+    aligned = shards % 4 == 0 and width % (16 * shards) == 0
+    combine = reduce_parts if aligned else scatter_parts
+    whole, project_grad, out_grad, up_grad, down_grad = combine(vector, lefts, rights)
+    size = width // shards
+    small = lax.dynamic_slice_in_dim(whole[:8], me * size, size, 1)
+    up_size = hidden.shape[1] // shards
+    up_small = lax.dynamic_slice_in_dim(whole[8:].reshape(1, -1), me * up_size, up_size, 1)
     return (
         result[None],
         input_grad[None],
-        small[0],
-        small[1],
-        reduce_rows(mixed, normed),
-        small[2],
-        small[3],
-        reduce_rows(branch, attended),
-        small[4],
-        small[5],
-        small[6],
-        reduce_rows(upper_low, second_normed),
+        small[0:1],
+        small[1:2],
+        project_grad[None],
+        small[2:3],
+        small[3:4],
+        out_grad[None],
+        small[4:5],
+        small[5:6],
+        small[6:7],
+        up_grad[None],
         up_small,
-        reduce_rows(output_low, hidden),
-        small[7],
+        down_grad[None],
+        small[7:8],
     )
 
 

time: 508 us -> 337 us (0.66)
  waiting for transfers between devices: 186 us -> 0 us
  Pallas kernels: 195 us -> 322 us
  blocking collectives: 60.7 us -> 0 us
  matrix products: 31.8 us -> 0 us
  between operations: 13.9 us -> 0.68 us
  other arithmetic: 8.89 us -> 1.3 us
    reduce_scatter x4 -> x0, waiting for transfers between devices: 186 us -> none  [reduce_rows(): piece = lax.psum_scatter(term, 'dp', scatter_dimension=0, tiled=True)]
    pallas_call x0 -> x1, Pallas kernels: none -> 124 us  [reduce_parts(): pl.pallas_call(reduce_kernel, out_shape=(jax.ShapeDtypeStruct((units, uni...]
    unnamed x1 -> x0, blocking collectives: 60.7 us -> none
    dot_general x4 -> x0, matrix products: 31.8 us -> none  [contract_rows(): lax.dot_general(left, right, (((0,), (0,)), ((), ())), preferred_element_...]
    broadcast_in_dim x4 -> x0, other arithmetic: 6.91 us -> none  [reduce_rows(): return piece.astype(F32).T[None]]
  transfers between devices with their start and end apart: 4 -> 0, of which waited for: 3 -> 0; matrix products, arithmetic and copies ran while one was open for 7% -> 0% of each run, Pallas kernels for 0% -> 0%
where the time goes in v3:
time: 337 us
  Pallas kernels  322 us (96%)
  local copies, waits for them, and re-layouts  12.8 us (4%)
    pallas_call x1, Pallas kernels, relay(): pl.pallas_call(relay_kernel, out_shape=outs, in_specs=[anywhere, anywhere...  197 us
    pallas_call x1, Pallas kernels, reduce_parts(): pl.pallas_call(reduce_kernel, out_shape=(jax.ShapeDtypeStruct((units, uni...  124 us

profile of v3, /device:TPU:0, one launch (start us, length us, event | category | flops | bytes accessed | tf_op | source)
XLA Modules:
  0.0 336.5 jit_solution(790628926175416499)
XLA Ops:
  0.6 1.3 select_convert_fusion
  1.9 197.4 %relay.1 = (bf16[1024,768]{1,0:T(8,128)(2,1)}, f32[1024,768]{1,0:T(8,128)}, f32[12,768]{1,0:T(8,128)}, bf16[1024,768]{1,0:T(8,128)(2,1)}, bf16[1024,768]{1,0:T(8...) custom-call(bf16[1024,768]{1,0:T(8,128)(2,1)} %x_hbm.1, ...), custom_call_target="tpu_custom_call" | custom-call | tf_op jit(solution)/shard_map/relay/pallas_call | solution.py:545
  199.4 124.4 %reduce.1 = (f32[12,48,768]{2,1,0:T(8,128)}, f32[12,768]{1,0:T(8,128)}) custom-call(f32[12,768]{1,0:T(8,128)} %get-tuple-element.30.vector_ref, bf16[1024,768]{1,0:T(8,128)(2,1)} %get-tuple-element.31.branch_hbm, bf16[1024,768]{1,0:T(8,128)(2,1)} %get-tuple-element.32.output_hbm, bf16[1024,3072]{1,0:T(8,128)(2,1)} %get-tuple-element.33.upper_hbm, ...), custom_call_target="tpu_custom_call" | custom-call | tf_op jit(solution)/shard_map/reduce/pallas_call | solution.py:815
  323.7 2.1 slice_bitcast_fusion
  325.9 0.0 copy-start.1
  325.9 0.4 copy.32
  326.3 1.1 broadcast_in_dim_reshape.3
  327.4 1.8 slice.45
  329.2 0.0 copy-start
  329.2 1.7 slice_bitcast_fusion.1
  330.9 0.0 copy-done.1
  330.9 0.1 constant_dynamic-slice_fusion.1
  331.0 0.5 fusion
  331.6 0.6 constant_dynamic-slice_fusion
  332.2 2.7 copy.36
  334.8 0.0 copy-done
  334.9 1.7 copy.37
  (3 shorter events, 0.0 us)
Async XLA Ops:
  325.9 5.0 %copy-start.1 = (f32[12,768]{1,0:T(8,128)S(1)}, f32[12,768]{1,0:T(8,128)}, u32[]{:S(2)}) copy-start(f32[12,768]{1,0:T(8,128)} %get-tuple-element.39) | copy-start | bytes 110596
  329.2 5.7 %copy-start = (f32[1024,768]{1,0:T(8,128)S(1)}, f32[1024,768]{1,0:T(8,128)}, u32[]{:S(2)}) copy-start(f32[1024,768]{1,0:T(8,128)} %get-tuple-element.29) | copy-start | bytes 9437188

commit v4 on v3

--- a/solution.py
+++ b/solution.py
@@ -741,50 +741,63 @@
             value = value + take_z[j, hop - 1].astype(F32)
         total_ref[j] = value
 
-    def first_phase(start, stop):
-        def step(index):
-            j = index + start
+    def feed(j):
+        @pl.when(j == 0)
+        def _():
+            turn(0, unit // 16, 0)
+            right_copy(0).wait()
+
+        @pl.when(j == 1)
+        def _():
+            turn(1, unit // 16, 1)
+            for index in range(1, 1 + ups):
+                right_copy(index).wait()
+
+        @pl.when(j == first_up)
+        def _():
+            for block in range(ups):
+                turn(2 + block, ups * unit // 16, 2)
+            right_copy(1 + ups).wait()
+
+        @pl.when(j == first_mixed)
+        def _():
+            for block in range(3):
+                turn(2 + ups + block, 3 * unit // 16, 2 + ups)
+            right_copy(2 + ups).wait()
+
+    def advance(j):
+        feed(j)
+
+        @pl.when((j >= 1) & (j < units + 1))
+        def _():
+            stage_x(j - 1)
+
+        @pl.when(j < units)
+        def _():
             stage_core(j)
 
-            @pl.when(j > 0)
-            def _():
-                stage_x(j - 1)
-
-        loop(stop - start, step)
-
-    turn(0, unit // 16, 0)
-    right_copy(0).wait()
-    first_phase(0, 1)
-    turn(1, unit // 16, 1)
-    for index in range(1, 1 + ups):
-        right_copy(index).wait()
-    first_phase(1, first_up)
-    vector_hop(0).wait_recv()
-    vectors[1] = vectors[0] + take_vector[0]
-    vector_hop(1).start()
-    for block in range(ups):
-        turn(2 + block, ups * unit // 16, 2)
-    right_copy(1 + ups).wait()
-    first_phase(first_up, first_mixed)
-    for block in range(3):
-        turn(2 + ups + block, 3 * unit // 16, 2 + ups)
-    right_copy(2 + ups).wait()
-    first_phase(first_mixed, units)
-    stage_x(units - 1)
-    vector_hop(1).wait_recv()
-    vectors[2] = vectors[1] + take_vector[1]
-    for hop in range(1, levels):
-        vector_hop(hop + 1).start()
-
-    def second_phase(j):
-        stage_z(j)
-
-        @pl.when(j > 0)
-        def _():
-            finish(j - 1)
-
-    loop(units, second_phase)
-    finish(units - 1)
+        @pl.when((j >= 3) & (j < units + 3))
+        def _():
+            stage_z(j - 3)
+
+        @pl.when(j >= 5)
+        def _():
+            finish(j - 5)
+
+        @pl.when(j == 2)
+        def _():
+            vector_hop(0).wait_recv()
+            vectors[1] = vectors[0] + take_vector[0]
+            vector_hop(1).start()
+
+        @pl.when(j == 4)
+        def _():
+            vector_hop(1).wait_recv()
+            vectors[2] = vectors[1] + take_vector[1]
+            for hop in range(1, levels):
+                vector_hop(hop + 1).start()
+
+    loop(units + 5, advance)
     whole = vectors[2]
     for hop in range(1, levels):
         vector_hop(hop + 1).wait_recv()

time: 337 us -> 317 us (0.941)
  Pallas kernels: 322 us -> 302 us
    pallas_call x1, Pallas kernels: 124 us -> 104 us  [reduce_parts(): pl.pallas_call(reduce_kernel, out_shape=(jax.ShapeDtypeStruct((units, uni...]
where the time goes in v4:
time: 317 us; the launch traced here: 316 us
  Pallas kernels  302 us (95%)
  local copies, waits for them, and re-layouts  12.8 us (4%)
    pallas_call x1, Pallas kernels, relay(): pl.pallas_call(relay_kernel, out_shape=outs, in_specs=[anywhere, anywhere...  197 us
    pallas_call x1, Pallas kernels, reduce_parts(): pl.pallas_call(reduce_kernel, out_shape=(jax.ShapeDtypeStruct((units, uni...  104 us

profile of v4, /device:TPU:0, one launch (start us, length us, event | category | flops | bytes accessed | tf_op | source)
XLA Modules:
  0.0 316.3 jit_solution(2162308467943160716)
XLA Ops:
  0.6 1.3 select_convert_fusion
  1.9 197.4 %relay.1 = (bf16[1024,768]{1,0:T(8,128)(2,1)}, f32[1024,768]{1,0:T(8,128)}, f32[12,768]{1,0:T(8,128)}, bf16[1024,768]{1,0:T(8,128)(2,1)}, bf16[1024,768]{1,0:T(8...) custom-call(bf16[1024,768]{1,0:T(8,128)(2,1)} %x_hbm.1, ...), custom_call_target="tpu_custom_call" | custom-call | tf_op jit(solution)/shard_map/relay/pallas_call | solution.py:545
  199.4 104.2 %reduce.1 = (f32[12,48,768]{2,1,0:T(8,128)}, f32[12,768]{1,0:T(8,128)}) custom-call(f32[12,768]{1,0:T(8,128)} %get-tuple-element.30.vector_ref, bf16[1024,768]{1,0:T(8,128)(2,1)} %get-tuple-element.31.branch_hbm, bf16[1024,768]{1,0:T(8,128)(2,1)} %get-tuple-element.32.output_hbm, bf16[1024,3072]{1,0:T(8,128)(2,1)} %get-tuple-element.33.upper_hbm, ...), custom_call_target="tpu_custom_call" | custom-call | tf_op jit(solution)/shard_map/reduce/pallas_call | solution.py:828
  303.6 2.1 slice_bitcast_fusion
  305.7 0.0 copy-start.1
  305.7 0.4 copy.32
  306.1 1.1 broadcast_in_dim_reshape.3
  307.2 1.8 slice.45
  309.0 0.0 copy-start
  309.0 1.7 slice_bitcast_fusion.1
  310.7 0.0 copy-done.1
  310.7 0.1 constant_dynamic-slice_fusion.1
  310.8 0.5 fusion
  311.4 0.6 constant_dynamic-slice_fusion
  312.0 2.7 copy.36
  314.7 0.0 copy-done
  314.7 1.7 copy.37
  (3 shorter events, 0.0 us)
Async XLA Ops:
  305.7 5.0 %copy-start.1 = (f32[12,768]{1,0:T(8,128)S(1)}, f32[12,768]{1,0:T(8,128)}, u32[]{:S(2)}) copy-start(f32[12,768]{1,0:T(8,128)} %get-tuple-element.39) | copy-start | bytes 110596
  309.0 5.7 %copy-start = (f32[1024,768]{1,0:T(8,128)S(1)}, f32[1024,768]{1,0:T(8,128)}, u32[]{:S(2)}) copy-start(f32[1024,768]{1,0:T(8,128)} %get-tuple-element.29) | copy-start | bytes 9437188

commit v5 on v4

--- a/solution.py
+++ b/solution.py
@@ -11,6 +11,7 @@
 PAIR = 2 * HEAD_DIM
 PAIRS = HEADS // 2
 TILE = 256
+WIDE = 1024
 ROWS = 128
 EPSILON = 1e-06
 SCORE_SCALE = 0.125
@@ -122,10 +123,10 @@
     input_grad,
     grad_low,
     bias,
-    lse_cols,
-    lse_rows,
-    soft_all,
-    weighted_all,
+    log_sums,
+    score_buf,
+    soft_low,
+    score_low,
     sums,
     up_sums,
     weight_sem,
@@ -210,6 +211,10 @@
 
     lane = lax.broadcasted_iota(jnp.int32, (SEQ, PAIR), 1)
 
+    def heads_of(pack, pair):
+        start = pl.multiple_of(pair * PAIR, PAIR)
+        return [mixed[pack, :, pl.ds(third * width + start, PAIR)] for third in range(3)]
+
     def forward(pack):
         first = pack == 0
 
@@ -237,51 +242,50 @@
             weights[0].wait()
 
         for third, offset_ref in enumerate((query_bias, None, value_bias)):
-
-            def project_step(tile, third=third, offset_ref=offset_ref):
-                here = part(tile, TILE)
-                there = pl.ds(pl.multiple_of(third * width + tile * TILE, TILE), TILE)
-                value = times(normed[pack], project[:, there])
-                if offset_ref is not None:
-                    value = value + offset_ref[:, here].astype(F32)
-                mixed[pack, :, there] = value.astype(LOW)
-
-            loop(width // TILE, project_step)
-
-        def attend_step(pair):
-            here = part(pair, PAIR)
-            query = mixed[pack, :, here]
-            key = mixed[pack, :, pl.ds(pl.multiple_of(width + pair * PAIR, PAIR), PAIR)]
-            value = mixed[pack, :, pl.ds(pl.multiple_of(2 * width + pair * PAIR, PAIR), PAIR)]
-            for block in range(SEQ // TILE):
-                rows = slice(block * TILE, (block + 1) * TILE)
-                outs = []
-                for side in range(2):
-                    own = (lane[rows] < HEAD_DIM) == (side == 0)
-                    one = jnp.where(own, query[rows] * SCORE_SCALE, 0.0).astype(LOW)
-                    scores = times_t(one, key) + bias[rows]
-                    row_max = jnp.max(scores, axis=-1, keepdims=True)
-                    exponent = jnp.exp(scores - row_max)
-                    row_sum = jnp.sum(exponent, axis=-1, keepdims=True)
-                    outs.append(times(exponent.astype(LOW), value) * (1.0 / row_sum))
-                    log_sum = row_max + jnp.log(row_sum)
-                    lse_cols[rows] = jnp.where(lane[rows] == 2 * pair + side, log_sum, lse_cols[rows])
-                attended[pack, rows, here] = jnp.where(lane[rows] < HEAD_DIM, outs[0], outs[1]).astype(LOW)
-
-        loop(PAIRS, attend_step)
-        lse_rows[pack] = jnp.transpose(lse_cols[...])[: lse_rows.shape[1]]
+            there = slice(third * width, (third + 1) * width)
+            value = times(normed[pack], project[:, there])
+            if offset_ref is not None:
+                value = value + offset_ref[...].astype(F32)
+            mixed[pack, :, there] = value.astype(LOW)
+
+        def scores_of(pair, slot):
+            query, key, _ = heads_of(pack, pair)
+            for side in range(2):
+                own = (lane < HEAD_DIM) == (side == 0)
+                one = jnp.where(own, query * SCORE_SCALE, 0.0).astype(LOW)
+                score_buf[slot, side] = times_t(key, one) + bias[...]
+
+        def attend(pair, slot):
+            value_across = jnp.transpose(heads_of(pack, pair)[2])
+            outs = []
+            for side in range(2):
+                heads = slice(side * HEAD_DIM, (side + 1) * HEAD_DIM)
+                scores = score_buf[slot, side]
+                key_max = jnp.max(scores, axis=0, keepdims=True)
+                exponent = jnp.exp(scores - key_max)
+                key_sum = jnp.sum(exponent, axis=0, keepdims=True)
+                outs.append(times(value_across[heads], exponent.astype(LOW)) * (1.0 / key_sum))
+                log_sum = key_max + jnp.log(key_sum)
+                log_sums[pack, 2 * pair + side] = jnp.broadcast_to(log_sum, (8, SEQ))
+            attended[pack, :, part(pair, PAIR)] = jnp.transpose(jnp.concatenate(outs, axis=0)).astype(LOW)
+
+        scores_of(0, 0)
+
+        def attend_step(index):
+            for slot in range(2):
+                pair = 2 * index + slot
+                scores_of(jnp.minimum(pair + 1, PAIRS - 1), 1 - slot)
+                attend(pair, slot)
+
+        loop(PAIRS // 2, attend_step)
 
         @pl.when(first)
         def _():
             weights[1].wait()
 
-        def out_step(tile):
-            here = part(tile, TILE)
-            middle[pack, :, here] = x_in[pack, :, here].astype(F32) + (
-                times(attended[pack], out_weight[:, here]) + out_bias[:, here].astype(F32)
-            )
-
-        loop(width // TILE, out_step)
+        middle[pack] = x_in[pack].astype(F32) + (
+            times(attended[pack], out_weight[...]) + out_bias[...].astype(F32)
+        )
         gain2 = second_gain[...].astype(F32)
         shift2 = second_shift[...].astype(F32)
 
@@ -297,26 +301,20 @@
             weights[2].wait()
 
         def up_step(tile):
-            here = part(tile, TILE)
+            here = part(tile, width)
             upper = times(second_normed[pack], up_weight[:, here]) + up_bias[:, here].astype(F32)
             act, act_slope = gelu_both(upper)
             hidden[pack, :, here] = act.astype(LOW)
             slope[pack, :, here] = act_slope.astype(LOW)
 
-        loop(hidden_width // TILE, up_step)
+        loop(hidden_width // width, up_step)
 
         @pl.when(first)
         def _():
             weights[3].wait()
 
-        def down_step(tile):
-            here = part(tile, TILE)
-            value = middle[pack, :, here] + (
-                times(hidden[pack], down_weight[:, here]) + down_bias[:, here].astype(F32)
-            )
-            result[pack, :, here] = value.astype(LOW)
-
-        loop(width // TILE, down_step)
+        value = middle[pack] + (times(hidden[pack], down_weight[...]) + down_bias[...].astype(F32))
+        result[pack] = value.astype(LOW)
 
         @pl.when(section == 0)
         def _():
@@ -345,20 +343,16 @@
         loop(SEQ // ROWS, fold_g)
 
         def hidden_step(tile):
-            here = part(tile, TILE)
+            here = part(tile, WIDE)
             value = times_t(g_in[pack], down_weight[here]).astype(LOW).astype(F32)
             low = (value * slope[pack, :, here].astype(F32)).astype(LOW)
             slope[pack, :, here] = low
             up_sums[:, here] += fold_rows(low.astype(F32))
 
-        loop(hidden_width // TILE, hidden_step)
+        loop(hidden_width // WIDE, hidden_step)
         store(7, pack).start()
 
-        def second_step(tile):
-            here = part(tile, TILE)
-            wide[:, here] = times_t(slope[pack], up_weight[here])
-
-        loop(width // TILE, second_step)
+        wide[...] = times_t(slope[pack], up_weight[...])
         gain2 = second_gain[...].astype(F32)
 
         def second_back(block):
@@ -376,64 +370,44 @@
         loop(SEQ // ROWS, second_back)
         store(6, pack).start()
 
-        def attended_step(tile):
-            here = part(tile, TILE)
-            attended_low[:, here] = times_t(branch[pack], out_weight[here]).astype(LOW)
-
-        loop(width // TILE, attended_step)
+        attended_low[...] = times_t(branch[pack], out_weight[...]).astype(LOW)
 
         def attend_back(pair):
             here = part(pair, PAIR)
-            key_part = pl.ds(pl.multiple_of(width + pair * PAIR, PAIR), PAIR)
-            value_part = pl.ds(pl.multiple_of(2 * width + pair * PAIR, PAIR), PAIR)
-            query = mixed[pack, :, here]
-            key = mixed[pack, :, key_part]
-            value = mixed[pack, :, value_part]
+            query, key, value = heads_of(pack, pair)
             upstream = attended_low[:, here]
-            key_across = jnp.transpose(key)
-            query_across = []
-            key_grad = [0.0, 0.0]
-            value_grad = [0.0, 0.0]
+            key_across, up_across = jnp.transpose(key), jnp.transpose(upstream)
+            one_query = []
             for side in range(2):
                 own = (lane < HEAD_DIM) == (side == 0)
-                one_query = jnp.where(own, query * SCORE_SCALE, 0.0).astype(LOW)
+                one_query.append(jnp.where(own, query * SCORE_SCALE, 0.0).astype(LOW))
                 one_up = jnp.where(own, upstream, 0.0).astype(LOW)
-                log_row = lse_rows[pack, pl.ds(2 * pair + side, 1)]
+                score_buf[0, side] = times_t(key, one_query[side]) + bias[...]
+                score_buf[1, side] = times_t(value, one_up)
+            for side in range(2):
+                soft = jnp.exp(score_buf[0, side] - log_sums[pack, 2 * pair + side, 0:1])
+                inner = jnp.sum(soft * score_buf[1, side], axis=0, keepdims=True)
+                soft_low[side] = soft.astype(LOW)
+                score_buf[0, side] = soft
+                score_low[side] = (score_buf[0, side] * (score_buf[1, side] - inner)).astype(LOW)
+            query_across, value_across, key_grad = [], [], 0.0
+            for side in range(2):
                 heads = slice(side * HEAD_DIM, (side + 1) * HEAD_DIM)
-                inner = 0.0
-                for block in range(SEQ // TILE):
-                    rows = slice(block * TILE, (block + 1) * TILE)
-                    soft = jnp.exp(times_t(key[rows], one_query) + bias[rows] - log_row)
-                    weighted = soft * times_t(value[rows], one_up)
-                    value_grad[block] += times(soft.astype(LOW), one_up)
-                    inner += jnp.sum(fold_rows(weighted), axis=0, keepdims=True)
-                    soft_all[rows] = soft
-                    weighted_all[rows] = weighted
-                across = 0.0
-                for block in range(SEQ // TILE):
-                    rows = slice(block * TILE, (block + 1) * TILE)
-                    score_low = (weighted_all[rows] - soft_all[rows] * inner).astype(LOW)
-                    key_grad[block] += times(score_low, one_query)
-                    across += times(key_across[heads, rows], score_low)
-                query_across.append(across)
+                value_across.append(times_t(up_across[heads], soft_low[side]))
+                key_grad += times(score_low[side], one_query[side])
+                query_across.append(times(key_across[heads], score_low[side]))
             query_grad = (jnp.transpose(jnp.concatenate(query_across, axis=0)) * SCORE_SCALE).astype(LOW)
-            mixed[pack, :, here] = query_grad
+            value_grad = jnp.transpose(jnp.concatenate(value_across, axis=0)).astype(LOW)
             sums[2, :, here] += fold_rows(query_grad.astype(F32))
-            for block in range(SEQ // TILE):
-                rows = slice(block * TILE, (block + 1) * TILE)
-                mixed[pack, rows, key_part] = key_grad[block].astype(LOW)
-                low = value_grad[block].astype(LOW)
-                mixed[pack, rows, value_part] = low
-                sums[3, :, here] += fold_rows(low.astype(F32))
+            sums[3, :, here] += fold_rows(value_grad.astype(F32))
+            for third, grad in enumerate((query_grad, key_grad.astype(LOW), value_grad)):
+                start = pl.multiple_of(third * width + pair * PAIR, PAIR)
+                mixed[pack, :, pl.ds(start, PAIR)] = grad
 
         loop(PAIRS, attend_back)
         store(5, pack).start()
 
-        def first_step(tile):
-            here = part(tile, TILE)
-            wide[:, here] = times_t(mixed[pack], project[here])
-
-        loop(width // TILE, first_step)
+        wide[...] = times_t(mixed[pack], project[...])
         gain = first_gain[...].astype(F32)
 
         def first_back(block):
@@ -530,10 +504,10 @@
         held(width, F32),
         held(width),
         pltpu.VMEM((SEQ, SEQ), F32),
-        pltpu.VMEM((SEQ, 128), F32),
-        pltpu.VMEM((packs, 16, SEQ), F32),
-        pltpu.VMEM((SEQ, SEQ), F32),
-        pltpu.VMEM((SEQ, SEQ), F32),
+        pltpu.VMEM((packs, HEADS, 8, SEQ), F32),
+        pltpu.VMEM((2, 2, SEQ, SEQ), F32),
+        pltpu.VMEM((2, SEQ, SEQ), LOW),
+        pltpu.VMEM((2, SEQ, SEQ), LOW),
         pltpu.VMEM((8, 8, width), F32),
         pltpu.VMEM((8, hidden_width), F32),
         pltpu.SemaphoreType.DMA((4,)),
@@ -696,39 +670,39 @@
         return jnp.minimum(j, first_up) + jnp.where(j >= first_mixed, 1, 0)
 
     def product(j, start, count, tile):
-        return times(lefts[left_of(j), start : start + count], rights[right_of(j), :, part(tile, TILE)])
+        return times(lefts[left_of(j), start : start + count], rights[right_of(j), :, part(tile, width)])
 
     def stage_core(j):
         def step(tile):
-            send_core[j, :, part(tile, TILE)] = product(j, 0, half, tile).astype(LOW)
-
-        loop(width // TILE, step)
+            send_core[j, :, part(tile, width)] = product(j, 0, half, tile).astype(LOW)
+
+        loop(1, step)
         to_core(j).start()
 
     def stage_x(j):
         to_core(j).wait_recv()
 
         def step(tile):
-            here = part(tile, TILE)
+            here = part(tile, width)
             value = product(j, half, quarter, tile) + take_core[j, :quarter, here].astype(F32)
             send_x[j, :, here] = value.astype(LOW)
 
-        loop(width // TILE, step)
+        loop(1, step)
         to_x(j).start()
 
     def stage_z(j):
         to_x(j).wait_recv()
 
         def step(tile):
-            here = part(tile, TILE)
+            here = part(tile, width)
             value = (
                 product(j, half + quarter, quarter, tile)
                 + take_core[j, quarter:, here].astype(F32)
                 + take_x[j, :, here].astype(F32)
             )
-            own[:, :, here] = value.reshape(levels, unit, TILE)
-
-        loop(width // TILE, step)
+            own[:, :, here] = value.reshape(levels, unit, width)
+
+        loop(1, step)
         for hop in range(1, levels):
             send_z[j, hop - 1] = own[(z + hop) % levels].astype(LOW)
             to_z(j, hop).start()

time: 317 us -> 284 us (0.90)
  Pallas kernels: 302 us -> 269 us
    pallas_call x1, Pallas kernels: 197 us -> 166 us  [relay(): pl.pallas_call(relay_kernel, out_shape=outs, in_specs=[anywhere, anywhere...]
where the time goes in v5:
time: 284 us; the launch traced here: 283 us
  Pallas kernels  269 us (95%)
  local copies, waits for them, and re-layouts  12.8 us (5%)
    pallas_call x1, Pallas kernels, relay(): pl.pallas_call(relay_kernel, out_shape=outs, in_specs=[anywhere, anywhere...  166 us
    pallas_call x1, Pallas kernels, reduce_parts(): pl.pallas_call(reduce_kernel, out_shape=(jax.ShapeDtypeStruct((units, uni...  103 us

profile of v5, /device:TPU:0, one launch (start us, length us, event | category | flops | bytes accessed | tf_op | source)
XLA Modules:
  0.0 283.4 jit_solution(5088684410293233504)
XLA Ops:
  0.6 1.3 select_convert_fusion
  1.9 165.5 %relay.1 = (bf16[1024,768]{1,0:T(8,128)(2,1)}, f32[1024,768]{1,0:T(8,128)}, f32[12,768]{1,0:T(8,128)}, bf16[1024,768]{1,0:T(8,128)(2,1)}, bf16[1024,768]{1,0:T(8...) custom-call(bf16[1024,768]{1,0:T(8,128)(2,1)} %x_hbm.1, ...), custom_call_target="tpu_custom_call" | custom-call | tf_op jit(solution)/shard_map/relay/pallas_call | solution.py:519
  167.5 103.2 %reduce.1 = (f32[12,48,768]{2,1,0:T(8,128)}, f32[12,768]{1,0:T(8,128)}) custom-call(f32[12,768]{1,0:T(8,128)} %get-tuple-element.30.vector_ref, bf16[1024,768]{1,0:T(8,128)(2,1)} %get-tuple-element.31.branch_hbm, bf16[1024,768]{1,0:T(8,128)(2,1)} %get-tuple-element.32.output_hbm, bf16[1024,3072]{1,0:T(8,128)(2,1)} %get-tuple-element.33.upper_hbm, ...), custom_call_target="tpu_custom_call" | custom-call | tf_op jit(solution)/shard_map/reduce/pallas_call | solution.py:802
  270.6 2.1 slice_bitcast_fusion
  272.8 0.0 copy-start.1
  272.8 0.4 copy.32
  273.2 1.1 broadcast_in_dim_reshape.3
  274.3 1.8 slice.45
  276.1 0.0 copy-start
  276.1 1.7 slice_bitcast_fusion.1
  277.8 0.0 copy-done.1
  277.8 0.1 constant_dynamic-slice_fusion.1
  277.9 0.5 fusion
  278.5 0.6 constant_dynamic-slice_fusion
  279.1 2.7 copy.36
  281.8 0.0 copy-done
  281.8 1.7 copy.37
  (3 shorter events, 0.0 us)
Async XLA Ops:
  272.8 5.0 %copy-start.1 = (f32[12,768]{1,0:T(8,128)S(1)}, f32[12,768]{1,0:T(8,128)}, u32[]{:S(2)}) copy-start(f32[12,768]{1,0:T(8,128)} %get-tuple-element.39) | copy-start | bytes 110596
  276.1 5.7 %copy-start = (f32[1024,768]{1,0:T(8,128)S(1)}, f32[1024,768]{1,0:T(8,128)}, u32[]{:S(2)}) copy-start(f32[1024,768]{1,0:T(8,128)} %get-tuple-element.29) | copy-start | bytes 9437188

commit v6 on v5

--- a/solution.py
+++ b/solution.py
@@ -71,14 +71,15 @@
 
 def gelu_both(upper):
     cumulative = 0.5 * (1.0 + lax.erf(upper * (0.5**0.5)))
-    density = jnp.exp(-0.5 * (upper * upper)) * 0.3989422804014327
+    density = jnp.exp2((upper * upper) * -0.7213475204444817) * 0.3989422804014327
     return upper * cumulative, cumulative + upper * density
 
 
 def relay_kernel(
     x_hbm,
     cot_hbm,
-    code_ref,
+    segment_ref,
+    valid_ref,
     first_gain,
     first_shift,
     project_hbm,
@@ -117,16 +118,14 @@
     hidden,
     slope,
     result,
-    branch,
-    attended_low,
     wide,
-    input_grad,
     grad_low,
     bias,
-    log_sums,
+    inv_sums,
     score_buf,
-    soft_low,
     score_low,
+    exponents,
+    outputs_across,
     sums,
     up_sums,
     weight_sem,
@@ -137,10 +136,11 @@
 ):
     section = lax.axis_index("section")
     width = x_in.shape[2]
-    hidden_width = hidden.shape[2]
+    hidden_width = hidden.shape[1]
     packs = x_in.shape[0]
     last = lax.axis_size("section") - 1
     partner = {"section": 1 - section}
+    branch, attended_low, input_grad = normed, attended, wide
 
     def rows_of(ref, pack):
         return ref.at[pl.ds(pl.multiple_of(pack * SEQ, SEQ), SEQ)]
@@ -174,7 +174,7 @@
 
     def hop_forward(pack):
         return pltpu.make_async_remote_copy(
-            src_ref=result.at[pack],
+            src_ref=result,
             dst_ref=x_in.at[pack],
             send_sem=send_sem.at[0, pack],
             recv_sem=x_sem.at[pack],
@@ -184,7 +184,7 @@
 
     def hop_backward(pack):
         return pltpu.make_async_remote_copy(
-            src_ref=grad_low.at[pack],
+            src_ref=grad_low,
             dst_ref=g_in.at[pack],
             send_sem=send_sem.at[1, pack],
             recv_sem=g_sem.at[pack],
@@ -207,7 +207,8 @@
 
     def store(index, pack):
         source, target = kept[index]
-        return pltpu.make_async_copy(source.at[pack], rows_of(target, pack), out_sem.at[index, pack])
+        source = source if len(source.shape) == 2 else source.at[pack]
+        return pltpu.make_async_copy(source, rows_of(target, pack), out_sem.at[index, pack])
 
     lane = lax.broadcasted_iota(jnp.int32, (SEQ, PAIR), 1)
 
@@ -229,13 +230,19 @@
         gain = first_gain[...].astype(F32)
         shift = first_shift[...].astype(F32)
 
+        @pl.when(pack > 0)
+        def _():
+            store(1, pack - 1).wait()
+
         def norm_step(block):
             rows = part(block, ROWS)
             white, _ = norm_rows(x_in[pack, rows].astype(F32))
-            normed[pack, rows] = (white * gain + shift).astype(LOW)
+            normed[rows] = (white * gain + shift).astype(LOW)
 
         loop(SEQ // ROWS, norm_step)
-        fill_bias(code_ref[pack], bias)
+        store(1, pack).start()
+        places = lax.broadcasted_iota(jnp.int32, (1, SEQ), 1) + SEQ
+        fill_bias(jnp.where(valid_ref[pack] == 1, segment_ref[pack], places).astype(F32), bias)
 
         @pl.when(first)
         def _():
@@ -243,7 +250,7 @@
 
         for third, offset_ref in enumerate((query_bias, None, value_bias)):
             there = slice(third * width, (third + 1) * width)
-            value = times(normed[pack], project[:, there])
+            value = times(normed[...], project[:, there])
             if offset_ref is not None:
                 value = value + offset_ref[...].astype(F32)
             mixed[pack, :, there] = value.astype(LOW)
@@ -257,17 +264,24 @@
 
         def attend(pair, slot):
             value_across = jnp.transpose(heads_of(pack, pair)[2])
+            ones = jnp.ones((16, SEQ), LOW)
             outs = []
             for side in range(2):
                 heads = slice(side * HEAD_DIM, (side + 1) * HEAD_DIM)
                 scores = score_buf[slot, side]
                 key_max = jnp.max(scores, axis=0, keepdims=True)
-                exponent = jnp.exp(scores - key_max)
-                key_sum = jnp.sum(exponent, axis=0, keepdims=True)
-                outs.append(times(value_across[heads], exponent.astype(LOW)) * (1.0 / key_sum))
-                log_sum = key_max + jnp.log(key_sum)
-                log_sums[pack, 2 * pair + side] = jnp.broadcast_to(log_sum, (8, SEQ))
-            attended[pack, :, part(pair, PAIR)] = jnp.transpose(jnp.concatenate(outs, axis=0)).astype(LOW)
+                exponent = jnp.exp(scores - key_max).astype(LOW)
+                exponents[pack, 2 * pair + side] = exponent
+                sums_too = times(jnp.concatenate([value_across[heads], ones], axis=0), exponent)
+                inverse = 1.0 / sums_too[HEAD_DIM : HEAD_DIM + 1]
+                inv_sums[pack, 2 * pair + side] = jnp.broadcast_to(inverse, (8, SEQ))
+                outs.append(sums_too[:HEAD_DIM] * inverse)
+                outputs_across[pack, 2 * pair + side] = outs[side]
+            attended[:, part(pair, PAIR)] = jnp.transpose(jnp.concatenate(outs, axis=0)).astype(LOW)
+
+        @pl.when(pack > 0)
+        def _():
+            store(2, pack - 1).wait()
 
         scores_of(0, 0)
 
@@ -278,23 +292,30 @@
                 attend(pair, slot)
 
         loop(PAIRS // 2, attend_step)
+        store(2, pack).start()
 
         @pl.when(first)
         def _():
             weights[1].wait()
 
         middle[pack] = x_in[pack].astype(F32) + (
-            times(attended[pack], out_weight[...]) + out_bias[...].astype(F32)
+            times(attended[...], out_weight[...]) + out_bias[...].astype(F32)
         )
         gain2 = second_gain[...].astype(F32)
         shift2 = second_shift[...].astype(F32)
 
+        @pl.when(pack > 0)
+        def _():
+            store(3, pack - 1).wait()
+            store(4, pack - 1).wait()
+
         def second_step(block):
             rows = part(block, ROWS)
             white, _ = norm_rows(middle[pack, rows])
-            second_normed[pack, rows] = (white * gain2 + shift2).astype(LOW)
+            second_normed[rows] = (white * gain2 + shift2).astype(LOW)
 
         loop(SEQ // ROWS, second_step)
+        store(3, pack).start()
 
         @pl.when(first)
         def _():
@@ -302,26 +323,34 @@
 
         def up_step(tile):
             here = part(tile, width)
-            upper = times(second_normed[pack], up_weight[:, here]) + up_bias[:, here].astype(F32)
+            upper = times(second_normed[...], up_weight[:, here]) + up_bias[:, here].astype(F32)
             act, act_slope = gelu_both(upper)
-            hidden[pack, :, here] = act.astype(LOW)
+            hidden[:, here] = act.astype(LOW)
             slope[pack, :, here] = act_slope.astype(LOW)
 
         loop(hidden_width // width, up_step)
+        store(4, pack).start()
 
         @pl.when(first)
         def _():
             weights[3].wait()
 
-        value = middle[pack] + (times(hidden[pack], down_weight[...]) + down_bias[...].astype(F32))
-        result[pack] = value.astype(LOW)
+        @pl.when(pack > 0)
+        def _():
+            store(0, pack - 1).wait()
+
+        @pl.when((pack > 0) & (section == 0))
+        def _():
+            hop_forward(pack - 1).wait_send()
+
+        value = middle[pack] + (times(hidden[...], down_weight[...]) + down_bias[...].astype(F32))
+        result[...] = value.astype(LOW)
 
         @pl.when(section == 0)
         def _():
             hop_forward(pack).start()
 
-        for index in range(5):
-            store(index, pack).start()
+        store(0, pack).start()
 
     def backward(order):
         pack = packs - 1 - order
@@ -335,7 +364,6 @@
             hop_backward(pack).wait_recv()
 
         store(8, pack).start()
-        fill_bias(code_ref[pack], bias)
 
         def fold_g(block):
             sums[7] += fold_rows(g_in[pack, part(block, ROWS)].astype(F32))
@@ -351,6 +379,16 @@
 
         loop(hidden_width // WIDE, hidden_step)
         store(7, pack).start()
+
+        @pl.when(order > 0)
+        def _():
+            store(9, pack + 1).wait()
+            store(6, pack + 1).wait()
+
+        @pl.when(order == 0)
+        def _():
+            store(1, pack).wait()
+            store(2, pack).wait()
 
         wide[...] = times_t(slope[pack], up_weight[...])
         gain2 = second_gain[...].astype(F32)
@@ -364,37 +402,31 @@
             sums[6] += fold_rows(grad)
             middle[pack, rows] = total
             low = total.astype(LOW)
-            branch[pack, rows] = low
+            branch[rows] = low
             sums[4] += fold_rows(low.astype(F32))
 
         loop(SEQ // ROWS, second_back)
         store(6, pack).start()
 
-        attended_low[...] = times_t(branch[pack], out_weight[...]).astype(LOW)
+        attended_low[...] = times_t(branch[...], out_weight[...]).astype(LOW)
 
         def attend_back(pair):
             here = part(pair, PAIR)
             query, key, value = heads_of(pack, pair)
-            upstream = attended_low[:, here]
-            key_across, up_across = jnp.transpose(key), jnp.transpose(upstream)
-            one_query = []
-            for side in range(2):
-                own = (lane < HEAD_DIM) == (side == 0)
-                one_query.append(jnp.where(own, query * SCORE_SCALE, 0.0).astype(LOW))
-                one_up = jnp.where(own, upstream, 0.0).astype(LOW)
-                score_buf[0, side] = times_t(key, one_query[side]) + bias[...]
-                score_buf[1, side] = times_t(value, one_up)
-            for side in range(2):
-                soft = jnp.exp(score_buf[0, side] - log_sums[pack, 2 * pair + side, 0:1])
-                inner = jnp.sum(soft * score_buf[1, side], axis=0, keepdims=True)
-                soft_low[side] = soft.astype(LOW)
-                score_buf[0, side] = soft
-                score_low[side] = (score_buf[0, side] * (score_buf[1, side] - inner)).astype(LOW)
+            key_across, up_across = jnp.transpose(key), jnp.transpose(attended_low[:, here])
+            empty = jnp.zeros((HEAD_DIM, SEQ), LOW)
             query_across, value_across, key_grad = [], [], 0.0
             for side in range(2):
+                head = 2 * pair + side
                 heads = slice(side * HEAD_DIM, (side + 1) * HEAD_DIM)
-                value_across.append(times_t(up_across[heads], soft_low[side]))
-                key_grad += times(score_low[side], one_query[side])
+                own = (lane < HEAD_DIM) == (side == 0)
+                one_query = jnp.where(own, query * SCORE_SCALE, 0.0).astype(LOW)
+                one_up = (up_across[heads].astype(F32) * inv_sums[pack, head, 0:1]).astype(LOW)
+                inner = jnp.sum(one_up.astype(F32) * outputs_across[pack, head], axis=0, keepdims=True)
+                soft_grad = times(value, jnp.concatenate([one_up, empty][:: 1 - 2 * side], axis=0))
+                score_low[side] = (exponents[pack, head].astype(F32) * (soft_grad - inner)).astype(LOW)
+                value_across.append(times_t(one_up, exponents[pack, head]))
+                key_grad += times(score_low[side], one_query)
                 query_across.append(times(key_across[heads], score_low[side]))
             query_grad = (jnp.transpose(jnp.concatenate(query_across, axis=0)) * SCORE_SCALE).astype(LOW)
             value_grad = jnp.transpose(jnp.concatenate(value_across, axis=0)).astype(LOW)
@@ -408,6 +440,10 @@
         store(5, pack).start()
 
         wide[...] = times_t(mixed[pack], project[...])
+        @pl.when((order > 0) & (section == last))
+        def _():
+            hop_backward(pack + 1).wait_send()
+
         gain = first_gain[...].astype(F32)
 
         def first_back(block):
@@ -417,8 +453,8 @@
             total = middle[pack, rows] + norm_back(grad, white, scale, gain)
             sums[0] += fold_rows(grad * white)
             sums[1] += fold_rows(grad)
-            input_grad[pack, rows] = total
-            grad_low[pack, rows] = total.astype(LOW)
+            input_grad[rows] = total
+            grad_low[rows] = total.astype(LOW)
 
         loop(SEQ // ROWS, first_back)
 
@@ -432,25 +468,28 @@
     loop(packs, backward)
 
     count = sums.shape[0]
+    vector_ref[count:] = jnp.zeros((vector_ref.shape[0] - count, width), F32)
     for index in range(count):
         vector_ref[index : index + 1] = jnp.sum(sums[index], axis=0, keepdims=True)
     for index in range(hidden_width // width):
         lanes = slice(index * width, (index + 1) * width)
         vector_ref[count + index : count + index + 1] = jnp.sum(up_sums[:, lanes], axis=0, keepdims=True)
 
+    for index in (0, 3, 4):
+        store(index, packs - 1).wait()
+    for index in (6, 9):
+        store(index, 0).wait()
     for pack in range(packs):
-        for index in range(len(kept)):
+        for index in (5, 7, 8):
             store(index, pack).wait()
 
     @pl.when(section == 0)
     def _():
-        for pack in range(packs):
-            hop_forward(pack).wait_send()
+        hop_forward(packs - 1).wait_send()
 
     @pl.when(section == last)
     def _():
-        for pack in range(packs):
-            hop_backward(pack).wait_send()
+        hop_backward(0).wait_send()
 
 
 def relay(arrays):
@@ -458,8 +497,6 @@
     rows, width = inputs.shape
     hidden_width = arrays[13].shape[2]
     packs = rows // SEQ
-    places = lax.broadcasted_iota(jnp.int32, (rows,), 0) + SEQ
-    code = jnp.where(valid_flags == 1, segments, places).astype(F32).reshape(packs, 1, SEQ)
     anywhere = pl.BlockSpec(memory_space=pl.ANY)
     vmem = pl.BlockSpec(memory_space=pltpu.VMEM)
 
@@ -469,7 +506,7 @@
     outs = (
         low(width),
         jax.ShapeDtypeStruct((rows, width), F32),
-        jax.ShapeDtypeStruct((8 + hidden_width // width, width), F32),
+        jax.ShapeDtypeStruct((16, width), F32),
         low(width),
         low(width),
         low(width),
@@ -490,24 +527,22 @@
         pltpu.VMEM((hidden_width, width), LOW),
         held(width),
         held(width),
-        held(width),
+        pltpu.VMEM((SEQ, width), LOW),
         held(3 * width),
-        held(width),
+        pltpu.VMEM((SEQ, width), LOW),
         held(width, F32),
-        held(width),
+        pltpu.VMEM((SEQ, width), LOW),
+        pltpu.VMEM((SEQ, hidden_width), LOW),
         held(hidden_width),
-        held(hidden_width),
-        held(width),
-        held(width),
         pltpu.VMEM((SEQ, width), LOW),
         pltpu.VMEM((SEQ, width), F32),
-        held(width, F32),
-        held(width),
+        pltpu.VMEM((SEQ, width), LOW),
         pltpu.VMEM((SEQ, SEQ), F32),
         pltpu.VMEM((packs, HEADS, 8, SEQ), F32),
         pltpu.VMEM((2, 2, SEQ, SEQ), F32),
         pltpu.VMEM((2, SEQ, SEQ), LOW),
-        pltpu.VMEM((2, SEQ, SEQ), LOW),
+        pltpu.VMEM((packs, HEADS, SEQ, SEQ), LOW),
+        pltpu.VMEM((packs, HEADS, HEAD_DIM, SEQ), F32),
         pltpu.VMEM((8, 8, width), F32),
         pltpu.VMEM((8, hidden_width), F32),
         pltpu.SemaphoreType.DMA((4,)),
@@ -520,7 +555,7 @@
         relay_kernel,
         out_shape=outs,
         in_specs=[
-            anywhere, anywhere, vmem,
+            anywhere, anywhere, vmem, vmem,
             vmem, vmem, anywhere, vmem, vmem, anywhere, vmem,
             vmem, vmem, anywhere, vmem, anywhere, vmem,
         ],
@@ -528,9 +563,15 @@
         scratch_shapes=scratch,
         name="relay",
         compiler_params=pltpu.CompilerParams(
-            collective_id=0, has_side_effects=True, vmem_limit_bytes=66 * 2**20 - 2**21
+            collective_id=0, has_side_effects=True, vmem_limit_bytes=67043328
         ),
-    )(inputs, cotangent, code, *arrays[4:])
+    )(
+        inputs,
+        cotangent,
+        segments.reshape(packs, 1, SEQ),
+        valid_flags.reshape(packs, 1, SEQ),
+        *arrays[4:],
+    )
 
 
 def reduce_kernel(
@@ -832,13 +873,127 @@
             collective_id=1, has_side_effects=True, vmem_limit_bytes=67043328
         ),
     )(vector, branch, output_low, upper_low, mixed, attended, hidden, second_normed, normed)
+    return whole, total
+
+
+def finish_kernel(
+    whole_ref,
+    total_hbm,
+    result_hbm,
+    input_grad_hbm,
+    result_out,
+    input_grad_out,
+    first_gain_out,
+    first_shift_out,
+    project_out,
+    query_bias_out,
+    value_bias_out,
+    out_weight_out,
+    out_bias_out,
+    second_gain_out,
+    second_shift_out,
+    up_out,
+    up_bias_out,
+    down_out,
+    down_bias_out,
+    total,
+    rows_low,
+    rows_wide,
+    in_sem,
+    out_sem,
+):
+    units, unit, width = total.shape
+    ups = down_out.shape[1] // width
+    blocks = rows_low.shape[0]
+    me = lax.axis_index("dp")
+    shards = lax.axis_size("dp")
     first_up, first_mixed = 1 + ups, 1 + 2 * ups
+    take = pltpu.make_async_copy(total_hbm, total, in_sem.at[2 * blocks])
+    take.start()
+
+    def block_of(ref, block):
+        size = rows_low.shape[1]
+        return ref.at[pl.ds(block * size, size)]
+
+    pairs = []
+    for block in range(blocks):
+        for index, (source, middle, target) in enumerate(
+            ((result_hbm, rows_low, result_out), (input_grad_hbm, rows_wide, input_grad_out))
+        ):
+            slot = 2 * block + index
+            load = pltpu.make_async_copy(block_of(source, block), middle.at[block], in_sem.at[slot])
+            save = pltpu.make_async_copy(middle.at[block], block_of(target, block), out_sem.at[slot])
+            load.start()
+            pairs.append((load, save))
+
+    pieces = [(0, out_weight_out)]
+    pieces += [(1 + block, down_out.at[:, pl.ds(block * width, width)]) for block in range(ups)]
+    pieces += [(first_up + block, up_out.at[pl.ds(block * unit, unit)]) for block in range(ups)]
+    pieces += [(first_mixed + block, project_out.at[pl.ds(block * unit, unit)]) for block in range(3)]
+    take.wait()
+    for index, (source, target) in enumerate(pieces):
+        save = pltpu.make_async_copy(total.at[source], target, out_sem.at[2 * blocks + index])
+        save.start()
+        pieces[index] = save
+    for load, save in pairs:
+        load.wait()
+        save.start()
+    rolled = pltpu.roll(whole_ref[:8], lax.rem(shards - me, shards) * unit, 1)
+    small_outs = (
+        first_gain_out, first_shift_out, query_bias_out, value_bias_out,
+        out_bias_out, second_gain_out, second_shift_out, down_bias_out,
+    )
+    for index, small in enumerate(small_outs):
+        small[...] = rolled[index : index + 1, :unit]
+    span = ups * unit
+    inner = width // span
+    wide_rolled = pltpu.roll(whole_ref[8:16], lax.rem(inner - lax.rem(me, inner), inner) * span, 1)
+    mine = lax.broadcasted_iota(jnp.int32, (8, width), 0) == lax.div(me, inner)
+    up_bias_out[...] = jnp.sum(jnp.where(mine, wide_rolled, 0.0), axis=0, keepdims=True)[:, :span]
+    for _, save in pairs:
+        save.wait()
+    for save in pieces:
+        save.wait()
+
+
+def finish(whole, total, result, input_grad, ups):
+    units, unit, width = total.shape
+    rows = result.shape[0]
+    anywhere = pl.BlockSpec(memory_space=pl.ANY)
+    vmem = pl.BlockSpec(memory_space=pltpu.VMEM)
+
+    def wide(*shape):
+        return jax.ShapeDtypeStruct(shape, F32)
+
+    small, matrix = wide(1, unit), wide(unit, width)
+    blocks = 4
+    outs = pl.pallas_call(
+        finish_kernel,
+        out_shape=(
+            jax.ShapeDtypeStruct(result.shape, LOW), wide(rows, width), small, small,
+            wide(3 * unit, width), small, small, matrix, small, small, small,
+            wide(ups * unit, width), wide(1, ups * unit), wide(unit, ups * width), small,
+        ),
+        in_specs=[vmem] + [anywhere] * 3,
+        out_specs=[
+            anywhere, anywhere, vmem, vmem, anywhere, vmem, vmem, anywhere,
+            vmem, vmem, vmem, anywhere, vmem, anywhere, vmem,
+        ],
+        scratch_shapes=[
+            pltpu.VMEM(total.shape, F32),
+            pltpu.VMEM((blocks, rows // blocks, width), LOW),
+            pltpu.VMEM((blocks, rows // blocks, width), F32),
+            pltpu.SemaphoreType.DMA((2 * blocks + 1,)),
+            pltpu.SemaphoreType.DMA((2 * blocks + units,)),
+        ],
+        name="finish",
+        compiler_params=pltpu.CompilerParams(vmem_limit_bytes=67043328),
+    )(whole, total, result, input_grad)
+    result, input_grad = outs[0][None], outs[1][None]
+    turned = [outs[index].T[None] for index in (4, 7, 11, 13)]
     return (
-        whole,
-        total[first_mixed:].reshape(3 * unit, width).T,
-        total[0].T,
-        total[first_up:first_mixed].reshape(ups * unit, width).T,
-        total[1:first_up].transpose(0, 2, 1).reshape(ups * width, unit),
+        result, input_grad, outs[2], outs[3], turned[0], outs[5], outs[6], turned[1],
+        outs[8], outs[9], outs[10], turned[2], outs[12], turned[3], outs[14],
     )
 
 
@@ -872,9 +1027,10 @@
     lefts = (branch, output_low, upper_low, mixed)
     rights = (attended, hidden, second_normed, normed)
     width = branch.shape[1]
-    aligned = shards % 4 == 0 and width % (16 * shards) == 0
-    combine = reduce_parts if aligned else scatter_parts
-    whole, project_grad, out_grad, up_grad, down_grad = combine(vector, lefts, rights)
+    if shards % 4 == 0 and width % (16 * shards) == 0:
+        whole, total = reduce_parts(vector, lefts, rights)
+        return finish(whole, total, result, input_grad, hidden.shape[1] // width)
+    whole, project_grad, out_grad, up_grad, down_grad = scatter_parts(vector, lefts, rights)
     size = width // shards
     small = lax.dynamic_slice_in_dim(whole[:8], me * size, size, 1)
     up_size = hidden.shape[1] // shards

time: 284 us -> 271 us (0.954)
  local copies, waits for them, and re-layouts: 12.8 us -> 0 us
    pallas_call x0 -> x1, Pallas kernels: none -> 6.47 us  [finish(): pl.pallas_call(finish_kernel, out_shape=(jax.ShapeDtypeStruct(result.shap...]
    pallas_call x1, Pallas kernels: 166 us -> 161 us  [relay(): pl.pallas_call(relay_kernel, out_shape=outs, in_specs=[anywhere, anywhere...]
    unnamed x8 -> x0, local copies, waits for them, and re-layouts: 4.34 us -> none
where the time goes in v6:
time: 271 us
  Pallas kernels  270 us (100%)
    pallas_call x1, Pallas kernels, relay(): pl.pallas_call(relay_kernel, out_shape=outs, in_specs=[anywhere, anywhere...  161 us
    pallas_call x1, Pallas kernels, reduce_parts(): pl.pallas_call(reduce_kernel, out_shape=(jax.ShapeDtypeStruct((units, uni...  102 us
    pallas_call x1, Pallas kernels, finish(): pl.pallas_call(finish_kernel, out_shape=(jax.ShapeDtypeStruct(result.shap...  6.47 us

profile of v6, /device:TPU:0, one launch (start us, length us, event | category | flops | bytes accessed | tf_op | source)
XLA Modules:
  0.0 270.7 jit_solution(3846105905344241183)
XLA Ops:
  0.7 160.9 %relay.1 = (bf16[1024,768]{1,0:T(8,128)(2,1)}, f32[1024,768]{1,0:T(8,128)}, f32[16,768]{1,0:T(8,128)}, bf16[1024,768]{1,0:T(8,128)(2,1)}, bf16[1024,768]{1,0:T(8...) custom-call(bf16[1024,768]{1,0:T(8,128)(2,1)} %x_hbm.1, ...), custom_call_target="tpu_custom_call" | custom-call | tf_op jit(solution)/shard_map/relay/pallas_call | solution.py:554
  161.6 102.5 %reduce.1 = (f32[12,48,768]{2,1,0:T(8,128)}, f32[16,768]{1,0:T(8,128)}) custom-call(f32[16,768]{1,0:T(8,128)} %get-tuple-element.43.vector_ref, bf16[1024,768]{1,0:T(8,128)(2,1)} %get-tuple-element.44.branch_hbm, bf16[1024,768]{1,0:T(8,128)(2,1)} %get-tuple-element.45.output_hbm, bf16[1024,3072]{1,0:T(8,128)(2,1)} %get-tuple-element.46.upper_hbm, ...), custom_call_target="tpu_custom_call" | custom-call | tf_op jit(solution)/shard_map/reduce/pallas_call | solution.py:843
  264.1 6.5 %finish.1 = (bf16[1024,768]{1,0:T(8,128)(2,1)}, f32[1024,768]{1,0:T(8,128)}, f32[1,48]{1,0:T(1,128)}, f32[1,48]{1,0:T(1,128)}, f32[144,768]{1,0:T(8,128)}, /*ind...) custom-call(f32[16,768]{1,0:T(8,128)} %get-tuple-element.52.whole_re, ...), custom_call_target="tpu_custom_call" | custom-call | tf_op jit(solution)/shard_map/finish/pallas_call | solution.py:970

commit v7 on v6

--- a/solution.py
+++ b/solution.py
@@ -12,6 +12,9 @@
 PAIRS = HEADS // 2
 TILE = 256
 WIDE = 1024
+HALF = 256
+CUT = 2
+LAG = 3
 ROWS = 128
 EPSILON = 1e-06
 SCORE_SCALE = 0.125
@@ -145,6 +148,19 @@
     def rows_of(ref, pack):
         return ref.at[pl.ds(pl.multiple_of(pack * SEQ, SEQ), SEQ)]
 
+    def half_of(half):
+        return pl.ds(pl.multiple_of(half * HALF, HALF), HALF)
+
+    def local_rows(source, target, sems, pack, half):
+        there = pl.ds(pl.multiple_of(pack * SEQ + half * HALF, HALF), HALF)
+        return pltpu.make_async_copy(source.at[there], target.at[pack, half_of(half)], sems.at[pack, half])
+
+    def local_x(pack, half):
+        return local_rows(x_hbm, x_in, x_sem, pack, half)
+
+    def local_g(pack, half):
+        return local_rows(cot_hbm, g_in, g_sem, pack, half)
+
     weights = (
         pltpu.make_async_copy(project_hbm.at[0], project, weight_sem.at[0]),
         pltpu.make_async_copy(out_hbm.at[0], out_weight, weight_sem.at[1]),
@@ -155,15 +171,16 @@
     @pl.when(section == 0)
     def _():
         for pack in range(packs):
-            pltpu.make_async_copy(rows_of(x_hbm, pack), x_in.at[pack], x_sem.at[pack]).start()
-
-    for copy in weights:
-        copy.start()
+            for half in range(2):
+                local_x(pack, half).start()
+
+    weights[0].start()
 
     @pl.when(section == last)
     def _():
         for pack in range(packs):
-            pltpu.make_async_copy(rows_of(cot_hbm, pack), g_in.at[pack], g_sem.at[pack]).start()
+            for half in range(2):
+                local_g(pack, half).start()
 
     barrier = pltpu.get_barrier_semaphore()
     pl.semaphore_signal(barrier, inc=1, device_id=partner, device_id_type=MESH)
@@ -172,25 +189,22 @@
     sums[...] = jnp.zeros_like(sums)
     up_sums[...] = jnp.zeros_like(up_sums)
 
-    def hop_forward(pack):
+    def hop(way, source, target, sems, pack, half):
+        rows = half_of(half)
         return pltpu.make_async_remote_copy(
-            src_ref=result,
-            dst_ref=x_in.at[pack],
-            send_sem=send_sem.at[0, pack],
-            recv_sem=x_sem.at[pack],
+            src_ref=source.at[rows],
+            dst_ref=target.at[pack, rows],
+            send_sem=send_sem.at[way, pack, half],
+            recv_sem=sems.at[pack, half],
             device_id=partner,
             device_id_type=MESH,
         )
 
-    def hop_backward(pack):
-        return pltpu.make_async_remote_copy(
-            src_ref=grad_low,
-            dst_ref=g_in.at[pack],
-            send_sem=send_sem.at[1, pack],
-            recv_sem=g_sem.at[pack],
-            device_id=partner,
-            device_id_type=MESH,
-        )
+    def hop_forward(pack, half):
+        return hop(0, result, x_in, x_sem, pack, half)
+
+    def hop_backward(pack, half):
+        return hop(1, grad_low, g_in, g_sem, pack, half)
 
     kept = (
         (result, result_hbm),
@@ -219,14 +233,6 @@
     def forward(pack):
         first = pack == 0
 
-        @pl.when(section == 0)
-        def _():
-            pltpu.make_async_copy(rows_of(x_hbm, pack), x_in.at[pack], x_sem.at[pack]).wait()
-
-        @pl.when(section == last)
-        def _():
-            hop_forward(pack).wait_recv()
-
         gain = first_gain[...].astype(F32)
         shift = first_shift[...].astype(F32)
 
@@ -234,26 +240,40 @@
         def _():
             store(1, pack - 1).wait()
 
-        def norm_step(block):
-            rows = part(block, ROWS)
-            white, _ = norm_rows(x_in[pack, rows].astype(F32))
-            normed[rows] = (white * gain + shift).astype(LOW)
-
-        loop(SEQ // ROWS, norm_step)
-        store(1, pack).start()
         places = lax.broadcasted_iota(jnp.int32, (1, SEQ), 1) + SEQ
         fill_bias(jnp.where(valid_ref[pack] == 1, segment_ref[pack], places).astype(F32), bias)
 
         @pl.when(first)
         def _():
             weights[0].wait()
-
-        for third, offset_ref in enumerate((query_bias, None, value_bias)):
-            there = slice(third * width, (third + 1) * width)
-            value = times(normed[...], project[:, there])
-            if offset_ref is not None:
-                value = value + offset_ref[...].astype(F32)
-            mixed[pack, :, there] = value.astype(LOW)
+            for copy in weights[1:]:
+                copy.start()
+
+        def project_half(half):
+            @pl.when(section == 0)
+            def _():
+                local_x(pack, half).wait()
+
+            @pl.when(section == last)
+            def _():
+                hop_forward(pack, half).wait_recv()
+
+            def norm_step(block):
+                rows = pl.ds(pl.multiple_of(half * HALF + block * ROWS, ROWS), ROWS)
+                white, _ = norm_rows(x_in[pack, rows].astype(F32))
+                normed[rows] = (white * gain + shift).astype(LOW)
+
+            loop(HALF // ROWS, norm_step)
+            rows = half_of(half)
+            for third, offset_ref in enumerate((query_bias, None, value_bias)):
+                there = slice(third * width, (third + 1) * width)
+                value = times(normed[rows], project[:, there])
+                if offset_ref is not None:
+                    value = value + offset_ref[...].astype(F32)
+                mixed[pack, rows, there] = value.astype(LOW)
+
+        loop(2, project_half)
+        store(1, pack).start()
 
         def scores_of(pair, slot):
             query, key, _ = heads_of(pack, pair)
@@ -308,76 +328,73 @@
         def _():
             store(3, pack - 1).wait()
             store(4, pack - 1).wait()
-
-        def second_step(block):
-            rows = part(block, ROWS)
-            white, _ = norm_rows(middle[pack, rows])
-            second_normed[rows] = (white * gain2 + shift2).astype(LOW)
-
-        loop(SEQ // ROWS, second_step)
+            store(0, pack - 1).wait()
+
+        @pl.when(first)
+        def _():
+            weights[2].wait()
+            weights[3].wait()
+
+        def feed_half(half):
+            def second_step(block):
+                rows = pl.ds(pl.multiple_of(half * HALF + block * ROWS, ROWS), ROWS)
+                white, _ = norm_rows(middle[pack, rows])
+                second_normed[rows] = (white * gain2 + shift2).astype(LOW)
+
+            loop(HALF // ROWS, second_step)
+            rows = half_of(half)
+
+            def up_step(tile):
+                here = part(tile, width)
+                upper = times(second_normed[rows], up_weight[:, here]) + up_bias[:, here].astype(F32)
+                act, act_slope = gelu_both(upper)
+                hidden[rows, here] = act.astype(LOW)
+                slope[pack, rows, here] = act_slope.astype(LOW)
+
+            loop(hidden_width // width, up_step)
+
+            @pl.when((pack > 0) & (section == 0))
+            def _():
+                hop_forward(pack - 1, half).wait_send()
+
+            value = middle[pack, rows] + (times(hidden[rows], down_weight[...]) + down_bias[...].astype(F32))
+            result[rows] = value.astype(LOW)
+
+            @pl.when(section == 0)
+            def _():
+                hop_forward(pack, half).start()
+
+        loop(2, feed_half)
         store(3, pack).start()
-
-        @pl.when(first)
-        def _():
-            weights[2].wait()
-
-        def up_step(tile):
-            here = part(tile, width)
-            upper = times(second_normed[...], up_weight[:, here]) + up_bias[:, here].astype(F32)
-            act, act_slope = gelu_both(upper)
-            hidden[:, here] = act.astype(LOW)
-            slope[pack, :, here] = act_slope.astype(LOW)
-
-        loop(hidden_width // width, up_step)
         store(4, pack).start()
-
-        @pl.when(first)
-        def _():
-            weights[3].wait()
-
-        @pl.when(pack > 0)
-        def _():
-            store(0, pack - 1).wait()
-
-        @pl.when((pack > 0) & (section == 0))
-        def _():
-            hop_forward(pack - 1).wait_send()
-
-        value = middle[pack] + (times(hidden[...], down_weight[...]) + down_bias[...].astype(F32))
-        result[...] = value.astype(LOW)
-
-        @pl.when(section == 0)
-        def _():
-            hop_forward(pack).start()
-
         store(0, pack).start()
 
     def backward(order):
         pack = packs - 1 - order
 
-        @pl.when(section == last)
-        def _():
-            pltpu.make_async_copy(rows_of(cot_hbm, pack), g_in.at[pack], g_sem.at[pack]).wait()
-
-        @pl.when(section == 0)
-        def _():
-            hop_backward(pack).wait_recv()
-
+        def hidden_half(half):
+            @pl.when(section == last)
+            def _():
+                local_g(pack, half).wait()
+
+            @pl.when(section == 0)
+            def _():
+                hop_backward(pack, half).wait_recv()
+
+            rows = half_of(half)
+            sums[7] += fold_rows(g_in[pack, rows].astype(F32))
+
+            def hidden_step(tile):
+                here = part(tile, WIDE)
+                value = times_t(g_in[pack, rows], down_weight[here]).astype(LOW).astype(F32)
+                low = (value * slope[pack, rows, here].astype(F32)).astype(LOW)
+                slope[pack, rows, here] = low
+                up_sums[:, here] += fold_rows(low.astype(F32))
+
+            loop(hidden_width // WIDE, hidden_step)
+
+        loop(2, hidden_half)
         store(8, pack).start()
-
-        def fold_g(block):
-            sums[7] += fold_rows(g_in[pack, part(block, ROWS)].astype(F32))
-
-        loop(SEQ // ROWS, fold_g)
-
-        def hidden_step(tile):
-            here = part(tile, WIDE)
-            value = times_t(g_in[pack], down_weight[here]).astype(LOW).astype(F32)
-            low = (value * slope[pack, :, here].astype(F32)).astype(LOW)
-            slope[pack, :, here] = low
-            up_sums[:, here] += fold_rows(low.astype(F32))
-
-        loop(hidden_width // WIDE, hidden_step)
         store(7, pack).start()
 
         @pl.when(order > 0)
@@ -439,29 +456,33 @@
         loop(PAIRS, attend_back)
         store(5, pack).start()
 
-        wide[...] = times_t(mixed[pack], project[...])
-        @pl.when((order > 0) & (section == last))
-        def _():
-            hop_backward(pack + 1).wait_send()
-
         gain = first_gain[...].astype(F32)
 
-        def first_back(block):
-            rows = part(block, ROWS)
-            grad = wide[rows]
-            white, scale = norm_rows(x_in[pack, rows].astype(F32))
-            total = middle[pack, rows] + norm_back(grad, white, scale, gain)
-            sums[0] += fold_rows(grad * white)
-            sums[1] += fold_rows(grad)
-            input_grad[rows] = total
-            grad_low[rows] = total.astype(LOW)
-
-        loop(SEQ // ROWS, first_back)
-
-        @pl.when(section == last)
-        def _():
-            hop_backward(pack).start()
-
+        def first_half(half):
+            rows = half_of(half)
+            wide[rows] = times_t(mixed[pack, rows], project[...])
+
+            @pl.when((order > 0) & (section == last))
+            def _():
+                hop_backward(pack + 1, half).wait_send()
+
+            def first_back(block):
+                rows = pl.ds(pl.multiple_of(half * HALF + block * ROWS, ROWS), ROWS)
+                grad = wide[rows]
+                white, scale = norm_rows(x_in[pack, rows].astype(F32))
+                total = middle[pack, rows] + norm_back(grad, white, scale, gain)
+                sums[0] += fold_rows(grad * white)
+                sums[1] += fold_rows(grad)
+                input_grad[rows] = total
+                grad_low[rows] = total.astype(LOW)
+
+            loop(HALF // ROWS, first_back)
+
+            @pl.when(section == last)
+            def _():
+                hop_backward(pack, half).start()
+
+        loop(2, first_half)
         store(9, pack).start()
 
     loop(packs, forward)
@@ -485,11 +506,13 @@
 
     @pl.when(section == 0)
     def _():
-        hop_forward(packs - 1).wait_send()
+        for half in range(2):
+            hop_forward(packs - 1, half).wait_send()
 
     @pl.when(section == last)
     def _():
-        hop_backward(0).wait_send()
+        for half in range(2):
+            hop_backward(0, half).wait_send()
 
 
 def relay(arrays):
@@ -546,9 +569,9 @@
         pltpu.VMEM((8, 8, width), F32),
         pltpu.VMEM((8, hidden_width), F32),
         pltpu.SemaphoreType.DMA((4,)),
-        pltpu.SemaphoreType.DMA((packs,)),
-        pltpu.SemaphoreType.DMA((packs,)),
-        pltpu.SemaphoreType.DMA((2, packs)),
+        pltpu.SemaphoreType.DMA((packs, 2)),
+        pltpu.SemaphoreType.DMA((packs, 2)),
+        pltpu.SemaphoreType.DMA((2, packs, 2)),
         pltpu.SemaphoreType.DMA((10, packs)),
     ]
     return pl.pallas_call(
@@ -643,14 +666,11 @@
     left_copy(0).start()
     right_copy(0).start()
     left_copy(1).start()
-    for index in range(1, len(sources)):
-        right_copy(index).start()
 
     barrier = pltpu.get_barrier_semaphore()
     peers = [sibling, across] + [level_peer(step) for step in range(1, levels)]
     for peer in peers:
         pl.semaphore_signal(barrier, inc=1, device_id=peer, device_id_type=MESH)
-    pl.semaphore_wait(barrier, len(peers))
 
     def send(source, target, sems, index, peer):
         return pltpu.make_async_remote_copy(
@@ -676,7 +696,6 @@
         return send(vectors.at[min(index, 2)], take_vector.at[index], vector_sems, (index,), peer)
 
     vectors[0] = vector_ref[...]
-    vector_hop(0).start()
 
     def turn(index, group, first_left):
         left_copy(index).wait()
@@ -704,100 +723,102 @@
     half = 2 * levels * unit
     quarter = levels * unit
 
-    def left_of(j):
-        return jnp.maximum(jnp.minimum(j, 1), j + 1 - ups)
-
-    def right_of(j):
-        return jnp.minimum(j, first_up) + jnp.where(j >= first_mixed, 1, 0)
-
-    def product(j, start, count, tile):
-        return times(lefts[left_of(j), start : start + count], rights[right_of(j), :, part(tile, width)])
+    span = width // CUT
+    steps = units * CUT
+
+    def left_of(u):
+        return jnp.maximum(jnp.minimum(u, 1), u + 1 - ups)
+
+    def right_of(u):
+        return jnp.minimum(u, first_up) + jnp.where(u >= first_mixed, 1, 0)
+
+    def product(j, start, count):
+        u = lax.div(j, CUT)
+        return times(lefts[left_of(u), start : start + count], rights[right_of(u), :, part(lax.rem(j, CUT), span)])
 
     def stage_core(j):
-        def step(tile):
-            send_core[j, :, part(tile, width)] = product(j, 0, half, tile).astype(LOW)
-
-        loop(1, step)
+        send_core[j] = product(j, 0, half).astype(LOW)
         to_core(j).start()
 
     def stage_x(j):
         to_core(j).wait_recv()
-
-        def step(tile):
-            here = part(tile, width)
-            value = product(j, half, quarter, tile) + take_core[j, :quarter, here].astype(F32)
-            send_x[j, :, here] = value.astype(LOW)
-
-        loop(1, step)
+        value = product(j, half, quarter) + take_core[j, :quarter].astype(F32)
+        send_x[j] = value.astype(LOW)
         to_x(j).start()
 
     def stage_z(j):
         to_x(j).wait_recv()
-
-        def step(tile):
-            here = part(tile, width)
-            value = (
-                product(j, half + quarter, quarter, tile)
-                + take_core[j, quarter:, here].astype(F32)
-                + take_x[j, :, here].astype(F32)
-            )
-            own[:, :, here] = value.reshape(levels, unit, width)
-
-        loop(1, step)
+        value = product(j, half + quarter, quarter) + take_core[j, quarter:].astype(F32) + take_x[j].astype(F32)
+        own[...] = value.reshape(levels, unit, span)
         for hop in range(1, levels):
             send_z[j, hop - 1] = own[(z + hop) % levels].astype(LOW)
             to_z(j, hop).start()
-        total_ref[j] = own[z]
+        total_ref[lax.div(j, CUT), :, part(lax.rem(j, CUT), span)] = own[z]
 
     def finish(j):
-        value = total_ref[j]
+        u, here = lax.div(j, CUT), part(lax.rem(j, CUT), span)
+        value = total_ref[u, :, here]
         for hop in range(1, levels):
             to_z(j, hop).wait_recv()
             value = value + take_z[j, hop - 1].astype(F32)
-        total_ref[j] = value
+        total_ref[u, :, here] = value
 
     def feed(j):
-        @pl.when(j == 0)
-        def _():
-            turn(0, unit // 16, 0)
-            right_copy(0).wait()
-
         @pl.when(j == 1)
         def _():
             turn(1, unit // 16, 1)
-            for index in range(1, 1 + ups):
+            for index in range(1 + ups, 3 + ups):
+                right_copy(index).start()
+
+        for block in range(ups):
+
+            @pl.when(j == CUT * block + 2)
+            def _(block=block):
+                turn(2 + block, ups * unit // 16, 2)
+
+        for block in range(3):
+
+            @pl.when(j == CUT * (block + ups) + 2)
+            def _(block=block):
+                turn(2 + ups + block, 3 * unit // 16, 2 + ups)
+
+    def need_right(j):
+        for index, when in [(block, block) for block in range(1, 1 + ups)] + [
+            (1 + ups, first_up),
+            (2 + ups, first_mixed),
+        ]:
+
+            @pl.when(j == CUT * when)
+            def _(index=index):
                 right_copy(index).wait()
 
-        @pl.when(j == first_up)
-        def _():
-            for block in range(ups):
-                turn(2 + block, ups * unit // 16, 2)
-            right_copy(1 + ups).wait()
-
-        @pl.when(j == first_mixed)
-        def _():
-            for block in range(3):
-                turn(2 + ups + block, 3 * unit // 16, 2 + ups)
-            right_copy(2 + ups).wait()
+    turn(0, unit // 16, 0)
+    for index in range(1, 1 + ups):
+        right_copy(index).start()
+    right_copy(0).wait()
+    pl.semaphore_wait(barrier, len(peers))
+    vector_hop(0).start()
 
     def advance(j):
         feed(j)
 
-        @pl.when((j >= 1) & (j < units + 1))
+        @pl.when((j >= 1) & (j < steps + 1))
         def _():
             stage_x(j - 1)
 
-        @pl.when(j < units)
+        need_right(j)
+
+        @pl.when(j < steps)
         def _():
             stage_core(j)
 
-        @pl.when((j >= 3) & (j < units + 3))
-        def _():
-            stage_z(j - 3)
-
-        @pl.when(j >= 5)
-        def _():
-            finish(j - 5)
+        @pl.when((j >= LAG) & (j < steps + LAG))
+        def _():
+            stage_z(j - LAG)
+
+        @pl.when(j >= 2 * LAG)
+        def _():
+            finish(j - 2 * LAG)
 
         @pl.when(j == 2)
         def _():
@@ -812,7 +833,7 @@
             for hop in range(1, levels):
                 vector_hop(hop + 1).start()
 
-    loop(units + 5, advance)
+    loop(steps + 2 * LAG, advance)
     whole = vectors[2]
     for hop in range(1, levels):
         vector_hop(hop + 1).wait_recv()
@@ -825,7 +846,7 @@
         for hop in range(1, levels):
             to_z(j, hop).wait_send()
 
-    loop(units, drain)
+    loop(steps, drain)
     for hop in range(levels + 1):
         vector_hop(hop).wait_send()
 
@@ -838,6 +859,7 @@
     ups = hidden.shape[1] // width
     unit, levels = width // shards, shards // 4
     units = 1 + 2 * ups + 3
+    steps, span = units * CUT, width // CUT
     anywhere = pl.BlockSpec(memory_space=pl.ANY)
     vmem = pl.BlockSpec(memory_space=pltpu.VMEM)
     total, whole = pl.pallas_call(
@@ -852,20 +874,20 @@
             pltpu.VMEM((3 + ups, rows, width), LOW),
             pltpu.VMEM((2, rows, width), LOW),
             pltpu.VMEM((5 + ups, width, rows), LOW),
-            pltpu.VMEM((units, 2 * levels * unit, width), LOW),
-            pltpu.VMEM((units, 2 * levels * unit, width), LOW),
-            pltpu.VMEM((units, levels * unit, width), LOW),
-            pltpu.VMEM((units, levels * unit, width), LOW),
-            pltpu.VMEM((units, levels - 1, unit, width), LOW),
-            pltpu.VMEM((units, levels - 1, unit, width), LOW),
-            pltpu.VMEM((levels, unit, width), F32),
+            pltpu.VMEM((steps, 2 * levels * unit, span), LOW),
+            pltpu.VMEM((steps, 2 * levels * unit, span), LOW),
+            pltpu.VMEM((steps, levels * unit, span), LOW),
+            pltpu.VMEM((steps, levels * unit, span), LOW),
+            pltpu.VMEM((steps, levels - 1, unit, span), LOW),
+            pltpu.VMEM((steps, levels - 1, unit, span), LOW),
+            pltpu.VMEM((levels, unit, span), F32),
             pltpu.VMEM((3,) + vector.shape, F32),
             pltpu.VMEM((levels + 1,) + vector.shape, F32),
             pltpu.SemaphoreType.DMA((3 + ups,)),
             pltpu.SemaphoreType.DMA((2,)),
-            pltpu.SemaphoreType.DMA((2, units)),
-            pltpu.SemaphoreType.DMA((2, units)),
-            pltpu.SemaphoreType.DMA((2, units, levels - 1)),
+            pltpu.SemaphoreType.DMA((2, steps)),
+            pltpu.SemaphoreType.DMA((2, steps)),
+            pltpu.SemaphoreType.DMA((2, steps, levels - 1)),
             pltpu.SemaphoreType.DMA((2, levels + 1)),
         ],
         name="reduce",

time: 271 us -> 259 us (0.956)
  Pallas kernels: 270 us -> 258 us
    pallas_call x1, Pallas kernels: 161 us -> 152 us  [relay(): pl.pallas_call(relay_kernel, out_shape=outs, in_specs=[anywhere, anywhere...]
    pallas_call x1, Pallas kernels: 102 us -> 99.6 us  [reduce_parts(): pl.pallas_call(reduce_kernel, out_shape=(jax.ShapeDtypeStruct((units, uni...]
where the time goes in v7:
time: 259 us
  Pallas kernels  258 us (100%)
    pallas_call x1, Pallas kernels, relay(): pl.pallas_call(relay_kernel, out_shape=outs, in_specs=[anywhere, anywhere...  152 us
    pallas_call x1, Pallas kernels, reduce_parts(): pl.pallas_call(reduce_kernel, out_shape=(jax.ShapeDtypeStruct((units, uni...  99.6 us
    pallas_call x1, Pallas kernels, finish(): pl.pallas_call(finish_kernel, out_shape=(jax.ShapeDtypeStruct(result.shap...  6.47 us

profile of v7, /device:TPU:0, one launch (start us, length us, event | category | flops | bytes accessed | tf_op | source)
XLA Modules:
  0.0 258.8 jit_solution(10286090859236481025)
XLA Ops:
  0.7 151.9 %relay.1 = (bf16[1024,768]{1,0:T(8,128)(2,1)}, f32[1024,768]{1,0:T(8,128)}, f32[16,768]{1,0:T(8,128)}, bf16[1024,768]{1,0:T(8,128)(2,1)}, bf16[1024,768]{1,0:T(8...) custom-call(bf16[1024,768]{1,0:T(8,128)(2,1)} %x_hbm.1, ...), custom_call_target="tpu_custom_call" | custom-call | tf_op jit(solution)/shard_map/relay/pallas_call | solution.py:577
  152.5 99.6 %reduce.1 = (f32[12,48,768]{2,1,0:T(8,128)}, f32[16,768]{1,0:T(8,128)}) custom-call(f32[16,768]{1,0:T(8,128)} %get-tuple-element.43.vector_ref, bf16[1024,768]{1,0:T(8,128)(2,1)} %get-tuple-element.44.branch_hbm, bf16[1024,768]{1,0:T(8,128)(2,1)} %get-tuple-element.45.output_hbm, bf16[1024,3072]{1,0:T(8,128)(2,1)} %get-tuple-element.46.upper_hbm, ...), custom_call_target="tpu_custom_call" | custom-call | tf_op jit(solution)/shard_map/reduce/pallas_call | solution.py:865
  252.2 6.5 %finish.1 = (bf16[1024,768]{1,0:T(8,128)(2,1)}, f32[1024,768]{1,0:T(8,128)}, f32[1,48]{1,0:T(1,128)}, f32[1,48]{1,0:T(1,128)}, f32[144,768]{1,0:T(8,128)}, /*ind...) custom-call(f32[16,768]{1,0:T(8,128)} %get-tuple-element.52.whole_re, ...), custom_call_target="tpu_custom_call" | custom-call | tf_op jit(solution)/shard_map/finish/pallas_call | solution.py:992

commit v8 on v7

--- a/solution.py
+++ b/solution.py
@@ -1,3 +1,5 @@
+import functools
+
 import jax
 import jax.numpy as jnp
 from jax import lax
@@ -14,6 +16,8 @@
 WIDE = 1024
 HALF = 256
 CUT = 2
+RING = 6
+LATE = 16
 LAG = 3
 ROWS = 128
 EPSILON = 1e-06
@@ -79,6 +83,7 @@
 
 
 def relay_kernel(
+    defer,
     x_hbm,
     cot_hbm,
     segment_ref,
@@ -107,6 +112,11 @@
     branch_hbm,
     upper_hbm,
     output_hbm,
+    late_exponents,
+    late_outputs,
+    late_inverse,
+    late_upstream,
+    late_middle,
     project,
     out_weight,
     up_weight,
@@ -136,6 +146,7 @@
     g_sem,
     send_sem,
     out_sem,
+    late_sem,
 ):
     section = lax.axis_index("section")
     width = x_in.shape[2]
@@ -229,6 +240,14 @@
     def heads_of(pack, pair):
         start = pl.multiple_of(pair * PAIR, PAIR)
         return [mixed[pack, :, pl.ds(third * width + start, PAIR)] for third in range(3)]
+
+    late = (
+        pltpu.make_async_copy(exponents.at[0], late_exponents, late_sem.at[0]),
+        pltpu.make_async_copy(outputs_across.at[0], late_outputs, late_sem.at[1]),
+        pltpu.make_async_copy(inv_sums.at[0], late_inverse, late_sem.at[2]),
+        pltpu.make_async_copy(attended_low, late_upstream, late_sem.at[3]),
+        pltpu.make_async_copy(middle.at[0], late_middle, late_sem.at[4]),
+    )
 
     def forward(pack):
         first = pack == 0
@@ -453,8 +472,9 @@
                 start = pl.multiple_of(third * width + pair * PAIR, PAIR)
                 mixed[pack, :, pl.ds(start, PAIR)] = grad
 
-        loop(PAIRS, attend_back)
-        store(5, pack).start()
+        def attend_all():
+            loop(PAIRS, attend_back)
+            store(5, pack).start()
 
         gain = first_gain[...].astype(F32)
 
@@ -482,10 +502,35 @@
             def _():
                 hop_backward(pack, half).start()
 
-        loop(2, first_half)
-        store(9, pack).start()
+        def first_all():
+            loop(2, first_half)
+            store(9, pack).start()
+
+        if not defer:
+            attend_all()
+            first_all()
+        else:
+            put_off = (order == packs - 1) & (section == 0)
+
+            @pl.when(put_off)
+            def _():
+                store(5, pack).start()
+                for copy in late[3:]:
+                    copy.start()
+
+            @pl.when(jnp.logical_not(put_off))
+            def _():
+                attend_all()
+                first_all()
 
     loop(packs, forward)
+    if defer:
+
+        @pl.when(section == 0)
+        def _():
+            for copy in late[:3]:
+                copy.start()
+
     loop(packs, backward)
 
     count = sums.shape[0]
@@ -498,8 +543,20 @@
 
     for index in (0, 3, 4):
         store(index, packs - 1).wait()
-    for index in (6, 9):
-        store(index, 0).wait()
+    store(6, 0).wait()
+    if not defer:
+        store(9, 0).wait()
+    else:
+
+        @pl.when(section == last)
+        def _():
+            store(9, 0).wait()
+
+        @pl.when(section == 0)
+        def _():
+            for copy in late:
+                copy.wait()
+
     for pack in range(packs):
         for index in (5, 7, 8):
             store(index, pack).wait()
@@ -515,7 +572,7 @@
             hop_backward(0, half).wait_send()
 
 
-def relay(arrays):
+def relay(arrays, defer):
     inputs, cotangent, segments, valid_flags = arrays[:4]
     rows, width = inputs.shape
     hidden_width = arrays[13].shape[2]
@@ -538,6 +595,11 @@
         low(width),
         low(hidden_width),
         low(width),
+        jax.ShapeDtypeStruct((HEADS, SEQ, SEQ), LOW),
+        jax.ShapeDtypeStruct((HEADS, HEAD_DIM, SEQ), F32),
+        jax.ShapeDtypeStruct((HEADS, 8, SEQ), F32),
+        jax.ShapeDtypeStruct((SEQ, width), LOW),
+        jax.ShapeDtypeStruct((SEQ, width), F32),
     )
 
     def held(columns, kind=LOW):
@@ -573,16 +635,17 @@
         pltpu.SemaphoreType.DMA((packs, 2)),
         pltpu.SemaphoreType.DMA((2, packs, 2)),
         pltpu.SemaphoreType.DMA((10, packs)),
+        pltpu.SemaphoreType.DMA((5,)),
     ]
     return pl.pallas_call(
-        relay_kernel,
+        functools.partial(relay_kernel, defer),
         out_shape=outs,
         in_specs=[
             anywhere, anywhere, vmem, vmem,
             vmem, vmem, anywhere, vmem, vmem, anywhere, vmem,
             vmem, vmem, anywhere, vmem, anywhere, vmem,
         ],
-        out_specs=[anywhere, anywhere, vmem] + [anywhere] * 8,
+        out_specs=[anywhere, anywhere, vmem] + [anywhere] * 13,
         scratch_shapes=scratch,
         name="relay",
         compiler_params=pltpu.CompilerParams(
@@ -607,8 +670,17 @@
     hidden_hbm,
     second_hbm,
     normed_hbm,
+    x_hbm,
+    project_hbm,
+    first_gain,
+    late_exponents,
+    late_outputs,
+    late_inverse,
+    late_upstream,
+    late_middle,
     total_ref,
     whole_ref,
+    late_grad,
     rights,
     loaded,
     lefts,
@@ -627,6 +699,20 @@
     x_sems,
     z_sems,
     vector_sems,
+    mixed,
+    exponents,
+    outputs_across,
+    inverse,
+    upstream,
+    project,
+    score_low,
+    middle,
+    x_in,
+    wide,
+    sums,
+    late_sems,
+    pair_sems,
+    half_sems,
 ):
     units, unit, width = total_ref.shape
     rows = rights.shape[1]
@@ -659,9 +745,13 @@
 
     def left_copy(index):
         source, block = chunks[index]
-        return pltpu.make_async_copy(
-            source.at[:, pl.ds(block * width, width)], loaded.at[index % 2], load_sem.at[index % 2]
-        )
+        columns = pl.ds(block * width, width)
+        if index >= 2 + ups:
+            behind = pl.ds(SEQ, rows - SEQ)
+            return pltpu.make_async_copy(
+                source.at[behind, columns], loaded.at[index % 2, behind], load_sem.at[index % 2]
+            )
+        return pltpu.make_async_copy(source.at[:, columns], loaded.at[index % 2], load_sem.at[index % 2])
 
     left_copy(0).start()
     right_copy(0).start()
@@ -683,10 +773,10 @@
         )
 
     def to_core(j):
-        return send(send_core.at[j], take_core.at[j], core_sems, (j,), sibling)
+        return send(send_core.at[lax.rem(j, RING)], take_core.at[j], core_sems, (j,), sibling)
 
     def to_x(j):
-        return send(send_x.at[j], take_x.at[j], x_sems, (j,), across)
+        return send(send_x.at[lax.rem(j, RING)], take_x.at[j], x_sems, (j,), across)
 
     def to_z(j, step):
         return send(send_z.at[j, step - 1], take_z.at[j, step - 1], z_sems, (j, step - 1), level_peer(step))
@@ -694,8 +784,6 @@
     def vector_hop(index):
         peer = (sibling, across)[index] if index < 2 else level_peer(index - 1)
         return send(vectors.at[min(index, 2)], take_vector.at[index], vector_sems, (index,), peer)
-
-    vectors[0] = vector_ref[...]
 
     def turn(index, group, first_left):
         left_copy(index).wait()
@@ -704,7 +792,14 @@
         pieces = unit // 16
 
         def step(lane_block):
-            turned = jnp.transpose(source[:, part(lane_block, 128)])
+            here = part(lane_block, 128)
+            if index >= 2 + ups:
+                there = pl.ds(pl.multiple_of(block * width + lane_block * 128, 128), 128)
+                turned = jnp.concatenate(
+                    [jnp.transpose(mixed[:, there]), jnp.transpose(source[SEQ:, here])], axis=1
+                )
+            else:
+                turned = jnp.transpose(source[:, here])
             for piece in range(8):
                 place = block * (width // 16) + lane_block * 8 + piece
                 shard, inner = lax.div(place, group), lax.rem(place, group)
@@ -737,13 +832,22 @@
         return times(lefts[left_of(u), start : start + count], rights[right_of(u), :, part(lax.rem(j, CUT), span)])
 
     def stage_core(j):
-        send_core[j] = product(j, 0, half).astype(LOW)
+        @pl.when(j >= RING)
+        def _():
+            to_core(j - RING).wait_send()
+
+        send_core[lax.rem(j, RING)] = product(j, 0, half).astype(LOW)
         to_core(j).start()
 
     def stage_x(j):
         to_core(j).wait_recv()
         value = product(j, half, quarter) + take_core[j, :quarter].astype(F32)
-        send_x[j] = value.astype(LOW)
+
+        @pl.when(j >= RING)
+        def _():
+            to_x(j - RING).wait_send()
+
+        send_x[lax.rem(j, RING)] = value.astype(LOW)
         to_x(j).start()
 
     def stage_z(j):
@@ -778,7 +882,7 @@
 
         for block in range(3):
 
-            @pl.when(j == CUT * (block + ups) + 2)
+            @pl.when(j == CUT * first_mixed - 4 + block)
             def _(block=block):
                 turn(2 + ups + block, 3 * unit // 16, 2 + ups)
 
@@ -797,7 +901,121 @@
         right_copy(index).start()
     right_copy(0).wait()
     pl.semaphore_wait(barrier, len(peers))
-    vector_hop(0).start()
+
+    def pair_copies(pair, slot):
+        heads = pl.ds(pair * 2, 2)
+        return (
+            pltpu.make_async_copy(late_exponents.at[heads], exponents.at[slot], pair_sems.at[0, slot]),
+            pltpu.make_async_copy(late_outputs.at[heads], outputs_across.at[slot], pair_sems.at[1, slot]),
+        )
+
+    def half_copies(half):
+        half_rows = pl.ds(pl.multiple_of(half * HALF, HALF), HALF)
+        return (
+            pltpu.make_async_copy(late_middle.at[half_rows], middle, half_sems.at[0]),
+            pltpu.make_async_copy(x_hbm.at[half_rows], x_in, half_sems.at[1]),
+            pltpu.make_async_copy(wide, late_grad.at[half_rows], half_sems.at[2]),
+        )
+
+    late_loads = (
+        pltpu.make_async_copy(late_inverse, inverse, late_sems.at[1]),
+        pltpu.make_async_copy(late_upstream, upstream, late_sems.at[2]),
+        pltpu.make_async_copy(project_hbm.at[0], project, late_sems.at[3]),
+    )
+    mixed_load = pltpu.make_async_copy(mixed_hbm.at[pl.ds(0, SEQ)], mixed, late_sems.at[0])
+    mixed_load.start()
+    sums[...] = jnp.zeros_like(sums)
+    lane = lax.broadcasted_iota(jnp.int32, (SEQ, PAIR), 1)
+    section = lax.axis_index("section")
+
+    @pl.when(section == 0)
+    def _():
+        for copy in late_loads:
+            copy.start()
+        for copy in pair_copies(0, 0) + half_copies(0)[:2]:
+            copy.start()
+
+    def attend_late(pair):
+        slot = lax.rem(pair, 2)
+        for copy in pair_copies(pair, slot):
+            copy.wait()
+
+        @pl.when(pair < PAIRS - 1)
+        def _():
+            for copy in pair_copies(pair + 1, 1 - slot):
+                copy.start()
+
+        here = part(pair, PAIR)
+        places = [pl.ds(pl.multiple_of(third * width + pair * PAIR, PAIR), PAIR) for third in range(3)]
+        query, key, value = [mixed[:, place] for place in places]
+        key_across, up_across = jnp.transpose(key), jnp.transpose(upstream[:, here])
+        empty = jnp.zeros((HEAD_DIM, SEQ), LOW)
+        query_across, value_across, key_grad = [], [], 0.0
+        for side in range(2):
+            heads = slice(side * HEAD_DIM, (side + 1) * HEAD_DIM)
+            own_lanes = (lane < HEAD_DIM) == (side == 0)
+            one_query = jnp.where(own_lanes, query * SCORE_SCALE, 0.0).astype(LOW)
+            one_up = (up_across[heads].astype(F32) * inverse[2 * pair + side, 0:1]).astype(LOW)
+            inner = jnp.sum(one_up.astype(F32) * outputs_across[slot, side], axis=0, keepdims=True)
+            soft_grad = times(value, jnp.concatenate([one_up, empty][:: 1 - 2 * side], axis=0))
+            score_low[side] = (exponents[slot, side].astype(F32) * (soft_grad - inner)).astype(LOW)
+            value_across.append(times_t(one_up, exponents[slot, side]))
+            key_grad += times(score_low[side], one_query)
+            query_across.append(times(key_across[heads], score_low[side]))
+        query_grad = (jnp.transpose(jnp.concatenate(query_across, axis=0)) * SCORE_SCALE).astype(LOW)
+        value_grad = jnp.transpose(jnp.concatenate(value_across, axis=0)).astype(LOW)
+        sums[2, :, here] += fold_rows(query_grad.astype(F32))
+        sums[3, :, here] += fold_rows(value_grad.astype(F32))
+        for place, grad in zip(places, (query_grad, key_grad.astype(LOW), value_grad)):
+            mixed[:, place] = grad
+
+    def first_late(half):
+        loads = half_copies(half)
+        for copy in loads[:2]:
+            copy.wait()
+
+        @pl.when(half > 0)
+        def _():
+            half_copies(half - 1)[2].wait()
+
+        wide[...] = times_t(mixed[pl.ds(pl.multiple_of(half * HALF, HALF), HALF)], project[...])
+        gain = first_gain[...].astype(F32)
+
+        def back(block):
+            some = part(block, ROWS)
+            grad = wide[some]
+            white, scale = norm_rows(x_in[some].astype(F32))
+            sums[0] += fold_rows(grad * white)
+            sums[1] += fold_rows(grad)
+            wide[some] = middle[some] + norm_back(grad, white, scale, gain)
+
+        loop(HALF // ROWS, back)
+        loads[2].start()
+
+        @pl.when(half == 0)
+        def _():
+            for copy in half_copies(1)[:2]:
+                copy.start()
+
+    def late(j):
+        pair = lax.div(j - 3, 2)
+
+        @pl.when(j == 3)
+        def _():
+            mixed_load.wait()
+
+        @pl.when((section == 0) & (j == 3))
+        def _():
+            for copy in late_loads:
+                copy.wait()
+
+        @pl.when((section == 0) & (j >= 3) & (j < 3 + 2 * PAIRS) & (lax.rem(j, 2) == 1))
+        def _():
+            attend_late(pair)
+
+        @pl.when((section == 0) & (j >= LATE) & (j < LATE + 2))
+        def _():
+            first_late(j - LATE)
 
     def advance(j):
         feed(j)
@@ -820,13 +1038,22 @@
         def _():
             finish(j - 2 * LAG)
 
-        @pl.when(j == 2)
+        late(j)
+
+        @pl.when(j == LATE + 2)
+        def _():
+            vectors[0] = vector_ref[...]
+            for index in range(4):
+                vectors[0, index : index + 1] += jnp.sum(sums[index], axis=0, keepdims=True)
+            vector_hop(0).start()
+
+        @pl.when(j == LATE + 4)
         def _():
             vector_hop(0).wait_recv()
             vectors[1] = vectors[0] + take_vector[0]
             vector_hop(1).start()
 
-        @pl.when(j == 4)
+        @pl.when(j == LATE + 6)
         def _():
             vector_hop(1).wait_recv()
             vectors[2] = vectors[1] + take_vector[1]
@@ -841,8 +1068,11 @@
     whole_ref[...] = whole
 
     def drain(j):
-        to_core(j).wait_send()
-        to_x(j).wait_send()
+        @pl.when(j >= steps - RING)
+        def _():
+            to_core(j).wait_send()
+            to_x(j).wait_send()
+
         for hop in range(1, levels):
             to_z(j, hop).wait_send()
 
@@ -850,8 +1080,12 @@
     for hop in range(levels + 1):
         vector_hop(hop).wait_send()
 
-
-def reduce_parts(vector, lefts, rights):
+    @pl.when(section == 0)
+    def _():
+        half_copies(1)[2].wait()
+
+
+def reduce_parts(vector, lefts, rights, late):
     shards = lax.axis_size("dp")
     branch, output_low, upper_low, mixed = lefts
     attended, hidden, second_normed, normed = rights
@@ -862,21 +1096,22 @@
     steps, span = units * CUT, width // CUT
     anywhere = pl.BlockSpec(memory_space=pl.ANY)
     vmem = pl.BlockSpec(memory_space=pltpu.VMEM)
-    total, whole = pl.pallas_call(
+    return pl.pallas_call(
         reduce_kernel,
         out_shape=(
             jax.ShapeDtypeStruct((units, unit, width), F32),
             jax.ShapeDtypeStruct(vector.shape, F32),
+            jax.ShapeDtypeStruct((SEQ, width), F32),
         ),
-        in_specs=[vmem] + [anywhere] * 8,
-        out_specs=[vmem, vmem],
+        in_specs=[vmem] + [anywhere] * 10 + [vmem] + [anywhere] * 5,
+        out_specs=[vmem, vmem, anywhere],
         scratch_shapes=[
             pltpu.VMEM((3 + ups, rows, width), LOW),
             pltpu.VMEM((2, rows, width), LOW),
             pltpu.VMEM((5 + ups, width, rows), LOW),
+            pltpu.VMEM((RING, 2 * levels * unit, span), LOW),
             pltpu.VMEM((steps, 2 * levels * unit, span), LOW),
-            pltpu.VMEM((steps, 2 * levels * unit, span), LOW),
-            pltpu.VMEM((steps, levels * unit, span), LOW),
+            pltpu.VMEM((RING, levels * unit, span), LOW),
             pltpu.VMEM((steps, levels * unit, span), LOW),
             pltpu.VMEM((steps, levels - 1, unit, span), LOW),
             pltpu.VMEM((steps, levels - 1, unit, span), LOW),
@@ -889,13 +1124,26 @@
             pltpu.SemaphoreType.DMA((2, steps)),
             pltpu.SemaphoreType.DMA((2, steps, levels - 1)),
             pltpu.SemaphoreType.DMA((2, levels + 1)),
+            pltpu.VMEM((SEQ, 3 * width), LOW),
+            pltpu.VMEM((2, 2, SEQ, SEQ), LOW),
+            pltpu.VMEM((2, 2, HEAD_DIM, SEQ), F32),
+            pltpu.VMEM((HEADS, 8, SEQ), F32),
+            pltpu.VMEM((SEQ, width), LOW),
+            pltpu.VMEM((width, 3 * width), LOW),
+            pltpu.VMEM((2, SEQ, SEQ), LOW),
+            pltpu.VMEM((HALF, width), F32),
+            pltpu.VMEM((HALF, width), LOW),
+            pltpu.VMEM((HALF, width), F32),
+            pltpu.VMEM((4, 8, width), F32),
+            pltpu.SemaphoreType.DMA((4,)),
+            pltpu.SemaphoreType.DMA((2, 2)),
+            pltpu.SemaphoreType.DMA((3,)),
         ],
         name="reduce",
         compiler_params=pltpu.CompilerParams(
             collective_id=1, has_side_effects=True, vmem_limit_bytes=67043328
         ),
-    )(vector, branch, output_low, upper_low, mixed, attended, hidden, second_normed, normed)
-    return whole, total
+    )(vector, branch, output_low, upper_low, mixed, attended, hidden, second_normed, normed, *late)
 
 
 def finish_kernel(
@@ -903,6 +1151,7 @@
     total_hbm,
     result_hbm,
     input_grad_hbm,
+    late_grad,
     result_out,
     input_grad_out,
     first_gain_out,
@@ -929,6 +1178,7 @@
     blocks = rows_low.shape[0]
     me = lax.axis_index("dp")
     shards = lax.axis_size("dp")
+    section = lax.axis_index("section")
     first_up, first_mixed = 1 + ups, 1 + 2 * ups
     take = pltpu.make_async_copy(total_hbm, total, in_sem.at[2 * blocks])
     take.start()
@@ -945,8 +1195,13 @@
             slot = 2 * block + index
             load = pltpu.make_async_copy(block_of(source, block), middle.at[block], in_sem.at[slot])
             save = pltpu.make_async_copy(middle.at[block], block_of(target, block), out_sem.at[slot])
-            load.start()
             pairs.append((load, save))
+            if index == 1 and (block + 1) * rows_low.shape[1] <= SEQ:
+                other = pltpu.make_async_copy(block_of(late_grad, block), middle.at[block], in_sem.at[slot])
+                pl.when(section == 0)(other.start)
+                pl.when(section != 0)(load.start)
+            else:
+                load.start()
 
     pieces = [(0, out_weight_out)]
     pieces += [(1 + block, down_out.at[:, pl.ds(block * width, width)]) for block in range(ups)]
@@ -978,7 +1233,7 @@
         save.wait()
 
 
-def finish(whole, total, result, input_grad, ups):
+def finish(whole, total, result, input_grad, late_grad, ups):
     units, unit, width = total.shape
     rows = result.shape[0]
     anywhere = pl.BlockSpec(memory_space=pl.ANY)
@@ -996,7 +1251,7 @@
             wide(3 * unit, width), small, small, matrix, small, small, small,
             wide(ups * unit, width), wide(1, ups * unit), wide(unit, ups * width), small,
         ),
-        in_specs=[vmem] + [anywhere] * 3,
+        in_specs=[vmem] + [anywhere] * 4,
         out_specs=[
             anywhere, anywhere, vmem, vmem, anywhere, vmem, vmem, anywhere,
             vmem, vmem, vmem, anywhere, vmem, anywhere, vmem,
@@ -1010,7 +1265,7 @@
         ],
         name="finish",
         compiler_params=pltpu.CompilerParams(vmem_limit_bytes=67043328),
-    )(whole, total, result, input_grad)
+    )(whole, total, result, input_grad, late_grad)
     result, input_grad = outs[0][None], outs[1][None]
     turned = [outs[index].T[None] for index in (4, 7, 11, 13)]
     return (
@@ -1042,16 +1297,19 @@
 def on_device(*arrays):
     shards = lax.axis_size("dp")
     me = lax.axis_index("dp")
+    width = arrays[0].shape[1]
+    aligned = shards % 4 == 0 and width % (16 * shards) == 0
     (
         result, input_grad, vector,
         normed, attended, second_normed, hidden, mixed, branch, upper_low, output_low,
-    ) = relay(arrays)
+        *late,
+    ) = relay(arrays, aligned)
     lefts = (branch, output_low, upper_low, mixed)
     rights = (attended, hidden, second_normed, normed)
-    width = branch.shape[1]
-    if shards % 4 == 0 and width % (16 * shards) == 0:
-        whole, total = reduce_parts(vector, lefts, rights)
-        return finish(whole, total, result, input_grad, hidden.shape[1] // width)
+    if aligned:
+        late = (arrays[0], arrays[6], arrays[4], *late)
+        total, whole, late_grad = reduce_parts(vector, lefts, rights, late)
+        return finish(whole, total, result, input_grad, late_grad, hidden.shape[1] // width)
     whole, project_grad, out_grad, up_grad, down_grad = scatter_parts(vector, lefts, rights)
     size = width // shards
     small = lax.dynamic_slice_in_dim(whole[:8], me * size, size, 1)

time: 259 us -> 250 us (0.965)
  Pallas kernels: 258 us -> 249 us
    pallas_call x1, Pallas kernels: 152 us -> 141 us  [relay(): pl.pallas_call(functools.partial(relay_kernel, defer), out_shape=outs, in...]
where the time goes in v8:
time: 250 us; the launch traced here: 249 us
  Pallas kernels  249 us (100%)
    pallas_call x1, Pallas kernels, relay(): pl.pallas_call(functools.partial(relay_kernel, defer), out_shape=outs, in...  141 us
    pallas_call x1, Pallas kernels, reduce_parts(): pl.pallas_call(reduce_kernel, out_shape=(jax.ShapeDtypeStruct((units, uni...  101 us
    pallas_call x1, Pallas kernels, finish(): pl.pallas_call(finish_kernel, out_shape=(jax.ShapeDtypeStruct(result.shap...  6.48 us

profile of v8, /device:TPU:0, one launch (start us, length us, event | category | flops | bytes accessed | tf_op | source)
XLA Modules:
  0.0 249.3 jit_solution(4323809485386696226)
XLA Ops:
  0.7 140.9 %relay.1 = (bf16[1024,768]{1,0:T(8,128)(2,1)}, f32[1024,768]{1,0:T(8,128)}, f32[16,768]{1,0:T(8,128)}, bf16[1024,768]{1,0:T(8,128)(2,1)}, bf16[1024,768]{1,0:T(8...) custom-call(bf16[1024,768]{1,0:T(8,128)(2,1)} %x_hbm.3, ...), custom_call_target="tpu_custom_call" | custom-call | tf_op jit(solution)/shard_map/relay/pallas_call | solution.py:640
  141.6 101.1 %reduce.1 = (f32[12,48,768]{2,1,0:T(8,128)}, f32[16,768]{1,0:T(8,128)}, f32[512,768]{1,0:T(8,128)}) custom-call(f32[16,768]{1,0:T(8,128)} %get-tuple-element.49.vector_ref, bf16[1024,768]{1,0:T(8,128)(2,1)} %get-tuple-element.50.branch_hbm, bf16[1024,768]{1,0:T(8,128)(2,1)} %get-tuple-element.51.output_hbm, bf16[1024,3072]{1,0:T(8,128)(2,1)} %get-tuple-element.52.upper_hbm, ...), custom_call_target="tpu_custom_call" | custom-call | tf_op jit(solution)/shard_map/reduce/pallas_call | solution.py:1099
  242.7 6.5 %finish.1 = (bf16[1024,768]{1,0:T(8,128)(2,1)}, f32[1024,768]{1,0:T(8,128)}, f32[1,48]{1,0:T(1,128)}, f32[1,48]{1,0:T(1,128)}, f32[144,768]{1,0:T(8,128)}, /*ind...) custom-call(f32[16,768]{1,0:T(8,128)} %get-tuple-element.63.whole_re, ...), custom_call_target="tpu_custom_call" | custom-call | tf_op jit(solution)/shard_map/finish/pallas_call | solution.py:1247

commit v9 on v8

--- a/solution.py
+++ b/solution.py
@@ -13,8 +13,9 @@
 PAIR = 2 * HEAD_DIM
 PAIRS = HEADS // 2
 TILE = 256
-WIDE = 1024
+WIDE = 3072
 HALF = 256
+UP_WIDE = 1536
 CUT = 2
 RING = 6
 LATE = 16
@@ -364,13 +365,13 @@
             rows = half_of(half)
 
             def up_step(tile):
-                here = part(tile, width)
+                here = part(tile, UP_WIDE)
                 upper = times(second_normed[rows], up_weight[:, here]) + up_bias[:, here].astype(F32)
                 act, act_slope = gelu_both(upper)
                 hidden[rows, here] = act.astype(LOW)
                 slope[pack, rows, here] = act_slope.astype(LOW)
 
-            loop(hidden_width // width, up_step)
+            loop(hidden_width // UP_WIDE, up_step)
 
             @pl.when((pack > 0) & (section == 0))
             def _():

time: 250 us -> 246 us (0.984)
  Pallas kernels: 249 us -> 244 us
    pallas_call x1, Pallas kernels: 141 us -> 137 us  [relay(): pl.pallas_call(functools.partial(relay_kernel, defer), out_shape=outs, in...]
where the time goes in v9:
time: 246 us; the launch traced here: 245 us
  Pallas kernels  244 us (99%)
    pallas_call x1, Pallas kernels, relay(): pl.pallas_call(functools.partial(relay_kernel, defer), out_shape=outs, in...  137 us
    pallas_call x1, Pallas kernels, reduce_parts(): pl.pallas_call(reduce_kernel, out_shape=(jax.ShapeDtypeStruct((units, uni...  101 us
    pallas_call x1, Pallas kernels, finish(): pl.pallas_call(finish_kernel, out_shape=(jax.ShapeDtypeStruct(result.shap...  6.48 us

profile of v9, /device:TPU:0, one launch (start us, length us, event | category | flops | bytes accessed | tf_op | source)
XLA Modules:
  0.0 245.3 jit_solution(10975146093517097760)
XLA Ops:
  0.7 137.1 %relay.1 = (bf16[1024,768]{1,0:T(8,128)(2,1)}, f32[1024,768]{1,0:T(8,128)}, f32[16,768]{1,0:T(8,128)}, bf16[1024,768]{1,0:T(8,128)(2,1)}, bf16[1024,768]{1,0:T(8...) custom-call(bf16[1024,768]{1,0:T(8,128)(2,1)} %x_hbm.3, ...), custom_call_target="tpu_custom_call" | custom-call | tf_op jit(solution)/shard_map/relay/pallas_call | solution.py:641
  137.7 100.9 %reduce.1 = (f32[12,48,768]{2,1,0:T(8,128)}, f32[16,768]{1,0:T(8,128)}, f32[512,768]{1,0:T(8,128)}) custom-call(f32[16,768]{1,0:T(8,128)} %get-tuple-element.49.vector_ref, bf16[1024,768]{1,0:T(8,128)(2,1)} %get-tuple-element.50.branch_hbm, bf16[1024,768]{1,0:T(8,128)(2,1)} %get-tuple-element.51.output_hbm, bf16[1024,3072]{1,0:T(8,128)(2,1)} %get-tuple-element.52.upper_hbm, ...), custom_call_target="tpu_custom_call" | custom-call | tf_op jit(solution)/shard_map/reduce/pallas_call | solution.py:1100
  238.7 6.5 %finish.1 = (bf16[1024,768]{1,0:T(8,128)(2,1)}, f32[1024,768]{1,0:T(8,128)}, f32[1,48]{1,0:T(1,128)}, f32[1,48]{1,0:T(1,128)}, f32[144,768]{1,0:T(8,128)}, /*ind...) custom-call(f32[16,768]{1,0:T(8,128)} %get-tuple-element.63.whole_re, ...), custom_call_target="tpu_custom_call" | custom-call | tf_op jit(solution)/shard_map/finish/pallas_call | solution.py:1248

commit v10 on v9

--- a/solution.py
+++ b/solution.py
@@ -133,7 +133,6 @@
     slope,
     result,
     wide,
-    grad_low,
     bias,
     inv_sums,
     score_buf,
@@ -155,7 +154,7 @@
     packs = x_in.shape[0]
     last = lax.axis_size("section") - 1
     partner = {"section": 1 - section}
-    branch, attended_low, input_grad = normed, attended, wide
+    branch, attended_low, input_grad, grad_low = normed, attended, wide, result
 
     def rows_of(ref, pack):
         return ref.at[pl.ds(pl.multiple_of(pack * SEQ, SEQ), SEQ)]
@@ -279,11 +278,11 @@
                 hop_forward(pack, half).wait_recv()
 
             def norm_step(block):
-                rows = pl.ds(pl.multiple_of(half * HALF + block * ROWS, ROWS), ROWS)
+                rows = pl.ds(pl.multiple_of(half * HALF + block * HALF, HALF), HALF)
                 white, _ = norm_rows(x_in[pack, rows].astype(F32))
                 normed[rows] = (white * gain + shift).astype(LOW)
 
-            loop(HALF // ROWS, norm_step)
+            loop(HALF // HALF, norm_step)
             rows = half_of(half)
             for third, offset_ref in enumerate((query_bias, None, value_bias)):
                 there = slice(third * width, (third + 1) * width)
@@ -357,11 +356,11 @@
 
         def feed_half(half):
             def second_step(block):
-                rows = pl.ds(pl.multiple_of(half * HALF + block * ROWS, ROWS), ROWS)
+                rows = pl.ds(pl.multiple_of(half * HALF + block * HALF, HALF), HALF)
                 white, _ = norm_rows(middle[pack, rows])
                 second_normed[rows] = (white * gain2 + shift2).astype(LOW)
 
-            loop(HALF // ROWS, second_step)
+            loop(HALF // HALF, second_step)
             rows = half_of(half)
 
             def up_step(tile):
@@ -424,14 +423,20 @@
 
         @pl.when(order == 0)
         def _():
+            store(0, pack).wait()
             store(1, pack).wait()
             store(2, pack).wait()
 
+        @pl.when((order == 0) & (section == 0))
+        def _():
+            for half in range(2):
+                hop_forward(pack, half).wait_send()
+
         wide[...] = times_t(slope[pack], up_weight[...])
         gain2 = second_gain[...].astype(F32)
 
         def second_back(block):
-            rows = part(block, ROWS)
+            rows = part(block, HALF)
             grad = wide[rows]
             white, scale = norm_rows(middle[pack, rows])
             total = g_in[pack, rows].astype(F32) + norm_back(grad, white, scale, gain2)
@@ -442,7 +447,7 @@
             branch[rows] = low
             sums[4] += fold_rows(low.astype(F32))
 
-        loop(SEQ // ROWS, second_back)
+        loop(SEQ // HALF, second_back)
         store(6, pack).start()
 
         attended_low[...] = times_t(branch[...], out_weight[...]).astype(LOW)
@@ -488,7 +493,7 @@
                 hop_backward(pack + 1, half).wait_send()
 
             def first_back(block):
-                rows = pl.ds(pl.multiple_of(half * HALF + block * ROWS, ROWS), ROWS)
+                rows = pl.ds(pl.multiple_of(half * HALF + block * HALF, HALF), HALF)
                 grad = wide[rows]
                 white, scale = norm_rows(x_in[pack, rows].astype(F32))
                 total = middle[pack, rows] + norm_back(grad, white, scale, gain)
@@ -497,7 +502,7 @@
                 input_grad[rows] = total
                 grad_low[rows] = total.astype(LOW)
 
-            loop(HALF // ROWS, first_back)
+            loop(HALF // HALF, first_back)
 
             @pl.when(section == last)
             def _():
@@ -542,7 +547,7 @@
         lanes = slice(index * width, (index + 1) * width)
         vector_ref[count + index : count + index + 1] = jnp.sum(up_sums[:, lanes], axis=0, keepdims=True)
 
-    for index in (0, 3, 4):
+    for index in (3, 4):
         store(index, packs - 1).wait()
     store(6, 0).wait()
     if not defer:
@@ -561,11 +566,6 @@
     for pack in range(packs):
         for index in (5, 7, 8):
             store(index, pack).wait()
-
-    @pl.when(section == 0)
-    def _():
-        for half in range(2):
-            hop_forward(packs - 1, half).wait_send()
 
     @pl.when(section == last)
     def _():
@@ -622,7 +622,6 @@
         held(hidden_width),
         pltpu.VMEM((SEQ, width), LOW),
         pltpu.VMEM((SEQ, width), F32),
-        pltpu.VMEM((SEQ, width), LOW),
         pltpu.VMEM((SEQ, SEQ), F32),
         pltpu.VMEM((packs, HEADS, 8, SEQ), F32),
         pltpu.VMEM((2, 2, SEQ, SEQ), F32),

time: 246 us -> 242 us (0.984)
  Pallas kernels: 244 us -> 241 us
    pallas_call x1, Pallas kernels: 137 us -> 134 us  [relay(): pl.pallas_call(functools.partial(relay_kernel, defer), out_shape=outs, in...]
where the time goes in v10:
time: 242 us
  Pallas kernels  241 us (100%)
    pallas_call x1, Pallas kernels, relay(): pl.pallas_call(functools.partial(relay_kernel, defer), out_shape=outs, in...  134 us
    pallas_call x1, Pallas kernels, reduce_parts(): pl.pallas_call(reduce_kernel, out_shape=(jax.ShapeDtypeStruct((units, uni...  101 us
    pallas_call x1, Pallas kernels, finish(): pl.pallas_call(finish_kernel, out_shape=(jax.ShapeDtypeStruct(result.shap...  6.48 us

profile of v10, /device:TPU:0, one launch (start us, length us, event | category | flops | bytes accessed | tf_op | source)
XLA Modules:
  0.0 242.2 jit_solution(14747212671965365422)
XLA Ops:
  0.7 133.7 %relay.1 = (bf16[1024,768]{1,0:T(8,128)(2,1)}, f32[1024,768]{1,0:T(8,128)}, f32[16,768]{1,0:T(8,128)}, bf16[1024,768]{1,0:T(8,128)(2,1)}, bf16[1024,768]{1,0:T(8...) custom-call(bf16[1024,768]{1,0:T(8,128)(2,1)} %x_hbm.3, ...), custom_call_target="tpu_custom_call" | custom-call | tf_op jit(solution)/shard_map/relay/pallas_call | solution.py:640
  134.4 101.2 %reduce.1 = (f32[12,48,768]{2,1,0:T(8,128)}, f32[16,768]{1,0:T(8,128)}, f32[512,768]{1,0:T(8,128)}) custom-call(f32[16,768]{1,0:T(8,128)} %get-tuple-element.49.vector_ref, bf16[1024,768]{1,0:T(8,128)(2,1)} %get-tuple-element.50.branch_hbm, bf16[1024,768]{1,0:T(8,128)(2,1)} %get-tuple-element.51.output_hbm, bf16[1024,3072]{1,0:T(8,128)(2,1)} %get-tuple-element.52.upper_hbm, ...), custom_call_target="tpu_custom_call" | custom-call | tf_op jit(solution)/shard_map/reduce/pallas_call | solution.py:1099
  235.5 6.5 %finish.1 = (bf16[1024,768]{1,0:T(8,128)(2,1)}, f32[1024,768]{1,0:T(8,128)}, f32[1,48]{1,0:T(1,128)}, f32[1,48]{1,0:T(1,128)}, f32[144,768]{1,0:T(8,128)}, /*ind...) custom-call(f32[16,768]{1,0:T(8,128)} %get-tuple-element.63.whole_re, ...), custom_call_target="tpu_custom_call" | custom-call | tf_op jit(solution)/shard_map/finish/pallas_call | solution.py:1247

commit v11 on v10

--- a/solution.py
+++ b/solution.py
@@ -262,12 +262,6 @@
         places = lax.broadcasted_iota(jnp.int32, (1, SEQ), 1) + SEQ
         fill_bias(jnp.where(valid_ref[pack] == 1, segment_ref[pack], places).astype(F32), bias)
 
-        @pl.when(first)
-        def _():
-            weights[0].wait()
-            for copy in weights[1:]:
-                copy.start()
-
         def project_half(half):
             @pl.when(section == 0)
             def _():
@@ -283,6 +277,13 @@
                 normed[rows] = (white * gain + shift).astype(LOW)
 
             loop(HALF // HALF, norm_step)
+
+            @pl.when(first & (half == 0))
+            def _():
+                weights[0].wait()
+                for copy in weights[1:]:
+                    copy.start()
+
             rows = half_of(half)
             for third, offset_ref in enumerate((query_bias, None, value_bias)):
                 there = slice(third * width, (third + 1) * width)

time: 242 us -> 243 us (level)
  no operation moved by 1% of the time
where the time goes in v11:
time: 243 us; the launch traced here: 242 us
  Pallas kernels  242 us (100%)
    pallas_call x1, Pallas kernels, relay(): pl.pallas_call(functools.partial(relay_kernel, defer), out_shape=outs, in...  134 us
    pallas_call x1, Pallas kernels, reduce_parts(): pl.pallas_call(reduce_kernel, out_shape=(jax.ShapeDtypeStruct((units, uni...  101 us
    pallas_call x1, Pallas kernels, finish(): pl.pallas_call(finish_kernel, out_shape=(jax.ShapeDtypeStruct(result.shap...  6.48 us

profile of v11, /device:TPU:0, one launch (start us, length us, event | category | flops | bytes accessed | tf_op | source)
XLA Modules:
  0.0 242.4 jit_solution(9813494604431839970)
XLA Ops:
  0.7 133.7 %relay.1 = (bf16[1024,768]{1,0:T(8,128)(2,1)}, f32[1024,768]{1,0:T(8,128)}, f32[16,768]{1,0:T(8,128)}, bf16[1024,768]{1,0:T(8,128)(2,1)}, bf16[1024,768]{1,0:T(8...) custom-call(bf16[1024,768]{1,0:T(8,128)(2,1)} %x_hbm.3, ...), custom_call_target="tpu_custom_call" | custom-call | tf_op jit(solution)/shard_map/relay/pallas_call | solution.py:641
  134.4 101.4 %reduce.1 = (f32[12,48,768]{2,1,0:T(8,128)}, f32[16,768]{1,0:T(8,128)}, f32[512,768]{1,0:T(8,128)}) custom-call(f32[16,768]{1,0:T(8,128)} %get-tuple-element.49.vector_ref, bf16[1024,768]{1,0:T(8,128)(2,1)} %get-tuple-element.50.branch_hbm, bf16[1024,768]{1,0:T(8,128)(2,1)} %get-tuple-element.51.output_hbm, bf16[1024,3072]{1,0:T(8,128)(2,1)} %get-tuple-element.52.upper_hbm, ...), custom_call_target="tpu_custom_call" | custom-call | tf_op jit(solution)/shard_map/reduce/pallas_call | solution.py:1100
  235.8 6.5 %finish.1 = (bf16[1024,768]{1,0:T(8,128)(2,1)}, f32[1024,768]{1,0:T(8,128)}, f32[1,48]{1,0:T(1,128)}, f32[1,48]{1,0:T(1,128)}, f32[144,768]{1,0:T(8,128)}, /*ind...) custom-call(f32[16,768]{1,0:T(8,128)} %get-tuple-element.63.whole_re, ...), custom_call_target="tpu_custom_call" | custom-call | tf_op jit(solution)/shard_map/finish/pallas_call | solution.py:1248
